TPU v7x, 32 devices: a whole 2x2x4 slice. The times are simulated.
32 devices in a mesh: tile: 16 (over z, y, core), slide: 2 (over x).
Axes of the slice: x: 2, y: 2, z: 4, core: 2. Of those that a mesh axis runs over, the one named last changes fastest.
Arguments:
- feats: bfloat16 [2, 64, 1024, 128], P('slide', 'tile'), may hold values from -6 to 6
- cotangent: bfloat16 [2, 64, 1024, 128], P('slide', 'tile'), may hold values from -6 to 6
- w_reduce: bfloat16 [512, 1024], replicated, may hold values from -0.1875 to 0.1875
- w_group: bfloat16 [512, 144], replicated, may hold values from -0.5 to 0.5
- w_expand: bfloat16 [512, 1024], replicated, may hold values from -0.25 to 0.25
- scale1: float32 [512], replicated, may hold values from 0.25 to 1.75
- shift1: float32 [512], replicated, may hold values from -3 to 3
- scale2: float32 [512], replicated, may hold values from 0.25 to 1.75
- shift2: float32 [512], replicated, may hold values from -3 to 3
- scale3: float32 [1024], replicated, may hold values from 0.25 to 1.75
- shift3: float32 [1024], replicated, may hold values from -3 to 3
- tile_count: int32 [2, 16], P('slide'), may hold values from 1 to 4, as said below
- joined: int32 [2, 31], P('slide'), may hold values 0 or 1
Outputs:
- out: bfloat16 [2, 64, 1024, 128], P('slide', 'tile')
- grad_feats: bfloat16 [2, 64, 1024, 128], P('slide', 'tile')
- grad_reduce: float32 [512, 1024], P('tile')
- grad_group: float32 [512, 144], P('tile')
- grad_expand: float32 [512, 1024], P('tile')
Inputs may be any that keep to these rules, and one draw needn't show every extreme that they name: `tile_count`: each device of a slide holds 1 to 4 tissue tiles, and some device of every slide holds exactly 4; a slide holds 32 tissue tiles in all; the tiles held by devices 0 .. d-1 of a slide number 2d-1, 2d or 2d+1.
All inputs are finite; a program needn't handle non-finite values. No bound on the sum of `joined` on one device may be relied on, other than what follows from the above.
Results may differ from a plain program's by a relative error of at most 0.0064.
Values may be sent and summed in bfloat16 or wider, within the bound.
No kernel may reach another device: no remote copies, remote signals or barrier semaphores. Data moves between devices by JAX's collectives and lax.ppermute only.
A program may use at most 128 MiB of HBM per device.

v0:
```python
import math

import jax
import jax.numpy as jnp
from jax import lax
from jax.sharding import PartitionSpec as P

CIN = 1024
MID = 512
GW = 16
TH = 16
TW = 8
LIVE_DEV = 2


def with_halo(shard, sides, width):
    for axis, dim in sides:
        size, length = (lax.axis_size(axis), shard.shape[dim])
        up = [(i, (i + 1) % size) for i in range(size - 1)]
        down = [(j, i) for i, j in up]
        last = lax.slice_in_dim(shard, length - width, length, axis=dim)
        initial = lax.slice_in_dim(shard, 0, width, axis=dim)
        before = lax.ppermute(last, axis, up)
        after = lax.ppermute(initial, axis, down)
        shard = jnp.concatenate([before, shard, after], axis=dim)
    return shard


def activate(values):
    return values * jax.nn.sigmoid(values)


def slope(values):
    sigmoid_v = jax.nn.sigmoid(values)
    return sigmoid_v + values * sigmoid_v * (1.0 - sigmoid_v)


def edge_pair(field_map, last_slot):
    tile_total, channels = (field_map.shape[0], field_map.shape[1])
    grid_view = field_map.reshape(tile_total, channels, TH, TW)
    left_column = grid_view[0, :, :, 0]
    right_column = lax.dynamic_index_in_dim(grid_view, last_slot, 0, keepdims=False)[:, :, TW - 1]
    return jnp.stack([left_column.T, right_column.T], 0)


def framed(field_map, rim_cols, band_index, last_slot, seam_links):
    tile_total, channels = (field_map.shape[0], field_map.shape[1])
    grid_view = field_map.reshape(tile_total, channels, TH, TW)
    slot_ids = jnp.arange(tile_total, dtype=jnp.int32)
    right_cols = grid_view[:, :, :, TW - 1]
    left_cols = grid_view[:, :, :, 0]
    before_col = jnp.where(
        (slot_ids > 0)[:, None, None], jnp.roll(right_cols, 1, axis=0), rim_cols[0].T[None]
    )
    after_col = jnp.where(
        (slot_ids < last_slot)[:, None, None], jnp.roll(left_cols, -1, axis=0), rim_cols[3].T[None]
    )
    link_total = seam_links.shape[0]
    left_link = jnp.where(
        band_index > 0, jnp.take(seam_links, jnp.clip(band_index - 1, 0, link_total - 1)), 0
    )
    right_link = jnp.where(
        band_index < link_total, jnp.take(seam_links, jnp.clip(band_index, 0, link_total - 1)), 0
    )
    before_col = before_col * left_link.astype(field_map.dtype)[:, None, None]
    after_col = after_col * right_link.astype(field_map.dtype)[:, None, None]
    widened = jnp.concatenate([before_col[..., None], grid_view, after_col[..., None]], axis=3)
    flattened = widened.reshape(tile_total, channels, TH * (TW + 2))
    return jnp.pad(flattened, ((0, 0), (0, 0), (TW + 2, TW + 4)))


def block_width():
    return min(MID, 128)


def dense_taps(kernel):
    width = block_width()
    blocks = MID // width
    per_block = width // GW
    tap_weights = kernel.reshape(blocks, per_block, GW, 9, GW)
    picker = jnp.eye(per_block, dtype=kernel.dtype)
    spread = tap_weights[:, :, :, :, None, :] * picker[None, :, None, None, :, None]
    return spread.reshape(blocks, width, 9, width)


def stacked_windows(framed_map, transposed):
    tile_total = framed_map.shape[0]
    width = block_width()
    blocks = MID // width
    span_len = TH * (TW + 2)
    windows = []
    for offset in range(9):
        row_off, col_off = (offset // 3, offset % 3)
        if transposed:
            begin_at = (2 - row_off) * (TW + 2) + 2 - col_off
        else:
            begin_at = row_off * (TW + 2) + col_off
        windows.append(
            lax.slice_in_dim(framed_map, begin_at, begin_at + span_len, axis=2).reshape(
                tile_total, blocks, width, span_len
            )
        )
    return jnp.stack(windows, 2)


def group_apply(framed_map, kernel, transposed):
    tile_total = framed_map.shape[0]
    dense = dense_taps(kernel)
    windows = stacked_windows(framed_map, transposed)
    if transposed:
        summed = jnp.einsum("boti,nbtop->nbip", dense, windows, preferred_element_type=jnp.float32)
    else:
        summed = jnp.einsum("boti,nbtip->nbop", dense, windows, preferred_element_type=jnp.float32)
    trimmed = summed.reshape(tile_total, MID, TH, TW + 2)[:, :, :, :TW]
    return trimmed.reshape(tile_total, MID, TH * TW)


def group_weight_grad(errors, framed_map):
    tile_total = errors.shape[0]
    width = block_width()
    blocks = MID // width
    per_block = width // GW
    span_len = TH * (TW + 2)
    extended = jnp.pad(errors.reshape(tile_total, MID, TH, TW), ((0, 0), (0, 0), (0, 0), (0, 2)))
    extended = extended.reshape(tile_total, blocks, width, span_len)
    windows = stacked_windows(framed_map, False)
    full_grad = jnp.einsum(
        "nbop,nbtip->boti", extended, windows, preferred_element_type=jnp.float32
    )
    full_grad = full_grad.reshape(blocks, per_block, GW, 9, per_block, GW)
    picker = jnp.eye(per_block, dtype=jnp.float32)
    kept = jnp.einsum("bxotyi,xy->bxoti", full_grad, picker, precision=lax.Precision.HIGHEST)
    return kept.reshape(MID, 9 * GW)


def bottleneck(
    tiles_in,
    cot_in,
    band_index,
    occupied,
    last_slot,
    seam_links,
    w_reduce,
    w_group,
    w_expand,
    scale1,
    shift1,
    scale2,
    shift2,
    scale3,
    shift3,
):
    keep_mask = occupied.astype(jnp.float32)[:, None, None]
    reduced = jnp.einsum("oc,ncp->nop", w_reduce, tiles_in, preferred_element_type=jnp.float32)
    pre_reduce = reduced * scale1[:, None] + shift1[:, None]
    hidden_a = activate(pre_reduce).astype(jnp.bfloat16)
    rims_a = with_halo(edge_pair(hidden_a, last_slot), (("tile", 0),), 1)
    frame_a = framed(hidden_a, rims_a, band_index, last_slot, seam_links)
    pre_group = group_apply(frame_a, w_group, False) * scale2[:, None] + shift2[:, None]
    hidden_b = activate(pre_group).astype(jnp.bfloat16)
    expanded = jnp.einsum("oc,nop->ncp", w_expand, hidden_b, preferred_element_type=jnp.float32)
    residual_sum = expanded * scale3[:, None] + shift3[:, None] + tiles_in.astype(jnp.float32)
    outputs = (activate(residual_sum) * keep_mask).astype(jnp.bfloat16)
    back_grad = cot_in.astype(jnp.float32) * slope(residual_sum) * keep_mask
    error_c = (back_grad * scale3[:, None]).astype(jnp.bfloat16)
    pulled = jnp.einsum("oc,ncp->nop", w_expand, error_c, preferred_element_type=jnp.float32)
    error_b = (pulled * slope(pre_group) * scale2[:, None]).astype(jnp.bfloat16)
    rims_b = with_halo(edge_pair(error_b, last_slot), (("tile", 0),), 1)
    frame_b = framed(error_b, rims_b, band_index, last_slot, seam_links)
    error_a = (
        group_apply(frame_b, w_group, True) * slope(pre_reduce) * scale1[:, None] * keep_mask
    ).astype(jnp.bfloat16)
    grad_in = (
        jnp.einsum("oc,nop->ncp", w_reduce, error_a, preferred_element_type=jnp.float32) + back_grad
    ).astype(jnp.bfloat16)
    group_grad = group_weight_grad(error_b, frame_a)
    return (outputs, grad_in, error_a, hidden_b, error_c, group_grad)


def shards(
    feats,
    cotangent,
    w_reduce,
    w_group,
    w_expand,
    scale1,
    shift1,
    scale2,
    shift2,
    scale3,
    shift3,
    tile_count,
    joined,
):
    position = lax.axis_index("tile")
    tile_devices = lax.axis_size("tile")
    counts = tile_count[0]
    starts = jnp.cumsum(counts) - counts
    held_tiles = lax.dynamic_index_in_dim(counts, position, 0, keepdims=False)
    first_band = lax.dynamic_index_in_dim(starts, position, 0, keepdims=False)
    seam_links = joined[0]
    home_in = feats[0]
    home_cot = cotangent[0]
    slot_total = home_in.shape[0]
    slot_ids = jnp.arange(slot_total, dtype=jnp.int32)
    home_band = first_band + slot_ids
    occupied_home = slot_ids < held_tiles
    outputs, grad_in, error_a, hidden_b, error_c, group_grad = bottleneck(
        home_in,
        home_cot,
        home_band,
        occupied_home,
        held_tiles - 1,
        seam_links,
        w_reduce,
        w_group,
        w_expand,
        scale1,
        shift1,
        scale2,
        shift2,
        scale3,
        shift3,
    )
    scale_all = 1.0 / math.sqrt(lax.axis_size("slide") * LIVE_DEV * tile_devices * TH * TW)
    part_reduce = jnp.einsum("nop,ncp->oc", error_a, home_in, preferred_element_type=jnp.float32)
    part_expand = jnp.einsum("nop,ncp->oc", hidden_b, error_c, preferred_element_type=jnp.float32)
    whole = lax.psum(
        jnp.concatenate([part_reduce, group_grad, part_expand], 1) * scale_all, "slide"
    )
    combined = lax.psum_scatter(whole, "tile", scatter_dimension=0, tiled=True)
    grad_reduce = combined[:, :CIN]
    grad_group = combined[:, CIN : CIN + 9 * GW]
    grad_expand = combined[:, CIN + 9 * GW :]
    return (outputs[None], grad_in[None], grad_reduce, grad_group, grad_expand)


def solution(mesh):
    in_specs = (
        P("slide", "tile", None, None),
        P("slide", "tile", None, None),
        P(),
        P(),
        P(),
        P(),
        P(),
        P(),
        P(),
        P(),
        P(),
        P("slide", None),
        P("slide", None),
    )
    out_specs = (
        P("slide", "tile", None, None),
        P("slide", "tile", None, None),
        P("tile", None),
        P("tile", None),
        P("tile", None),
    )
    return jax.shard_map(shards, mesh=mesh, in_specs=in_specs, out_specs=out_specs, check_vma=False)
```

profile of v0, /device:TPU:0, one launch (start us, length us, event | category | flops | bytes accessed | tf_op | source)
XLA Modules:
  0.0 319.6 jit_solution(13082657350752524841)
XLA Ops:
  7.3 2.4 fusion.14
  12.9 1.3 collective-permute-start.1
  16.8 3.6 %collective-permute-start = (bf16[1,16,512]{2,1,0:T(8,128)(2,1)}, bf16[1,16,512]{2,1,0:T(8,128)(2,1)}, u32[]{:S(2)}, u32[]{:S(2)}) collective-permute-start(bf16[1,16,512]{2,1,0:T(8,128)(2,1)} %bitcast.226), channel_id=1, source_target_pairs={{0,2},{2,4},{4,6},{6,8},{8,10},{10,12},{12,14},{14,16},{16,18},{18... | collective-permute-start | bytes 49160 | tf_op jit(solution)/shard_map/ppermute | solution.py:23
  20.4 1.2 compare_convert_fusion
  24.6 1.2 fusion.48
  27.1 2.3 copy.85
  29.7 1.3 copy.109
  33.1 6.2 %mul.199 = bf16[4,8,16,9,8,16]{5,4,2,1,3,0:T(8,128)(2,1)} broadcast(bf16[4,8,16,9,16]{4,2,1,3,0:T(8,128)(2,1)S(1)} %copy.106), dimensions={0,1,2,3,5} | broadcast | bytes 1327104 | tf_op jit(solution)/shard_map/mul | solution.py:82
  39.4 10.4 %mul.200 = bf16[4,128,9,128]{3,1,2,0:T(8,128)(2,1)S(1)} reshape(bf16[4,8,16,9,8,16]{5,4,2,1,3,0:T(8,128)(2,1)} %mul.199) | data formatting | bytes 2359296 | tf_op jit(solution)/shard_map/mul | solution.py:82
  51.8 1.7 pad_maximum_fusion
  53.5 1.2 reshape.304
  55.2 3.5 %pad_slice_fusion.8 = (bf16[4,512,160]{1,0,2:T(4,128)(2,1)}, bf16[4,512,160]{1,0,2:T(4,128)(2,1)}, bf16[4,512,160]{1,0,2:T(4,128)(2,1)}, bf16[4,512,160]{1,0,2:T...) fusion(bf16[4,512,160]{1,0,2:T(4,128)(2,1)S(1)} %bitcast.232), kind=kLoop, calls=%fused_computation.119 | loop fusion | bytes 5898240 | tf_op jit(solution)/shard_map/slice | solution.py:99
  58.8 1.7 reshape.309
  60.5 2.4 reshape.302
  62.9 2.4 reshape.303
  65.3 2.4 reshape.305
  67.7 2.4 reshape.306
  70.1 12.6 %reshape.307 = bf16[4,4,1,128,160]{3,1,0,4,2:T(4,128)(2,1)} reshape(bf16[4,512,160]{1,0,2:T(4,128)(2,1)} %get-tuple-element.36) | data formatting | bytes 1310720 | tf_op jit(solution)/shard_map/stack;reshape | solution.py:103
  82.8 2.4 reshape.308
  85.2 2.4 reshape.301
  87.6 1.4 copy_dynamic-update-slice_fusion.17
  89.0 1.3 copy_dynamic-update-slice_fusion.16
  90.3 1.3 copy_dynamic-update-slice_fusion.15
  91.6 1.2 copy_dynamic-update-slice_fusion.14
  94.0 2.5 copy-done.3
  96.5 1.7 convolution_bitcast_fusion.3
  99.1 1.8 reshape.258
  100.9 1.3 slice.170
  102.2 4.4 %fusion.4 = (f32[4,1024,128]{1,2,0:T(8,128)S(1)}, bf16[1,4,1024,128]{2,3,1,0:T(8,128)(2,1)}) fusion(bf16[1,4,1024,128]{2,3,1,0:T(8,128)(2,1)} %copy.109, f32[4]{0:T(128)} %compare_convert_fusion, bf16[1,4,1024,128]{2,3,1,0:T(8,128)(2,1)} %copy.85, f32[1024]{0:T(1024)} %param.25, f32[1024]{0:T(1024)} %param.24, bf16[512,1024]{1,0:T(8,128)(2,1)S(1)} %copy-done, ...), kind=kOutput, calls=%fused_computation.8 | convolution fusion | flops 547094528 | bytes 7352336 | tf_op jit(solution)/shard_map/oc,nop->ncp/dot_general | solution.py:161
  108.0 2.4 convolution_bitcast_fusion
  110.4 1.3 collective-permute-start.3
  111.8 4.5 %collective-permute-start.2 = (bf16[1,16,512]{2,1,0:T(8,128)(2,1)S(1)}, bf16[1,16,512]{2,1,0:T(8,128)(2,1)S(1)}, u32[]{:S(2)}, u32[]{:S(2)}) collective-permute-start(bf16[1,16,512]{2,1,0:T(8,128)(2,1)S(1)} %bitcast.235), channel_id=1, source_target_pairs={{0,2},{2,4},{4,6},{6,8},{8,10},{10,12},{12,14},{14,16},{16,18},{18... | collective-permute-start | bytes 49160 | tf_op jit(solution)/shard_map/ppermute | solution.py:23
  118.2 1.2 reshape.315
  119.4 1.4 copy.110
  121.1 5.4 %fusion.6 = f32[4,128,9,128]{3,1,2,0:T(8,128)} fusion(bf16[4,4,9,128,160]{3,4,2,0,1:T(8,128)(2,1)} %copy-done.3, bf16[4,4,128,160,1]{2,1,3,0,4:T(4,128)(2,1)S(1)} %bitcast.230), kind=kOutput, calls=%fused_computation.15 | convolution fusion | flops 754974720 | bytes 8912896 | tf_op jit(solution)/shard_map/nbop,nbtip->boti/dot_general | solution.py:127
  126.6 3.7 %pad_slice_fusion = (bf16[4,512,160]{1,0,2:T(4,128)(2,1)}, bf16[4,512,160]{1,0,2:T(4,128)(2,1)}, bf16[4,512,160]{1,0,2:T(4,128)(2,1)}, bf16[4,512,160]{1,0,2:T(4...) fusion(bf16[4,512,160]{1,0,2:T(4,128)(2,1)S(1)} %bitcast.231), kind=kLoop, calls=%fused_computation.111 | loop fusion | bytes 5898240 | tf_op jit(solution)/shard_map/slice | solution.py:99
  130.3 1.7 reshape.318
  132.0 2.4 reshape.311
  134.4 2.4 reshape.312
  136.8 2.4 reshape.313
  141.4 1.8 reshape.317
  143.2 2.4 reshape.310
  145.6 1.4 copy_dynamic-update-slice_fusion.8
  147.0 1.3 copy_dynamic-update-slice_fusion.7
  148.3 1.3 copy_dynamic-update-slice_fusion.6
  149.6 1.3 copy_dynamic-update-slice_fusion.5
  152.0 1.7 convolution_bitcast_fusion.2
  154.5 1.9 reshape.262
  156.4 1.4 slice.176
  158.8 3.9 %convolution_bitcast_fusion.1 = f32[512,1024]{1,0:T(8,128)} fusion(bf16[1,4,1024,128]{3,2,1,0:T(8,128)(2,1)} %param.15, f32[4,512,16,8]{1,0,3,2:T(4,128)S(1)} %slice.176, f32[4,512,128]{1,2,0:T(8,128)S(1)} %copy-done.18, f32[4]{0:T(128)S(1)} %copy-done.36, f32[512]{0:T(512)S(1)} %copy-done.35), kind=kOutput, calls=%fused_computation.17 | convolution fusion | flops 539754496 | bytes 5244944 | tf_op jit(solution)/shard_map/nop,ncp->oc/dot_general | solution.py:226
  162.8 9.8 %reshape.265 = f32[4,8,16,9,8,16]{5,4,2,1,3,0:T(8,128)} reshape(f32[4,128,9,128]{3,1,2,0:T(8,128)S(1)} %copy-done.4) | data formatting | bytes 4718592 | tf_op jit(solution)/shard_map/reshape | solution.py:130
  172.6 12.9 %fusion = f32[8,1,4,16,9,16]{5,1,4,3,2,0:T(1,128)S(1)} fusion(f32[4,8,16,9,8,16]{5,4,2,1,3,0:T(8,128)} %reshape.265, pred[8,8,1,1,1,1]{1,0,2,3,4,5:T(8,128)(4,1)S(1)} %fusion.45), kind=kOutput, calls=%fused_computation.2 | convolution fusion | flops 7077888 | bytes 2654272 | tf_op jit(solution)/shard_map/bxotyi,xy->bxoti/dot_general | solution.py:132
  185.5 4.2 %copy.150 = f32[8,1,4,16,9,16]{3,0,2,5,4,1:T(8,128)} copy(f32[8,1,4,16,9,16]{5,1,4,3,2,0:T(1,128)S(1)} %fusion) | data formatting | bytes 589824 | tf_op jit(solution)/shard_map/bxotyi,xy->bxoti/dot_general | solution.py:132
  189.7 3.3 %reshape.266 = f32[512,144]{0,1:T(8,128)S(1)} reshape(f32[4,8,16,9,16]{2,1,0,4,3:T(8,128)} %bitcast.229) | data formatting | bytes 589824 | tf_op jit(solution)/shard_map/reshape | solution.py:133
  193.2 5.2 %concatenate.57 = f32[512,2192]{1,0:T(8,128)} concatenate(f32[512,1024]{1,0:T(8,128)} %convolution_bitcast_fusion.1, f32[512,144]{1,0:T(8,128)S(1)} %copy.138, f32[512,1024]{1,0:T(8,128)S(1)} %copy-done.16), dimensions={1} | concatenate | bytes 8978432 | tf_op jit(solution)/shard_map/concatenate | solution.py:229
  198.4 4.9 %broadcast_multiply_fusion = f32[512,2192]{1,0:T(8,128)} fusion(f32[512,2192]{1,0:T(8,128)} %concatenate.57), kind=kLoop, calls=%fused_computation.6 | loop fusion | flops 1122304 | bytes 8978432 | tf_op jit(solution)/shard_map/mul | solution.py:229
  203.4 1.1 copy-done.21
  204.5 1.3 copy.139
  205.8 78.5 %reduce-scatter.2.cloned.1.call-done = f32[32,2192]{1,0:T(8,128)} async-done(((f32[512,2192]{1,0:T(8,128)}), f32[32,2192]{1,0:T(8,128)}) %reduce-scatter.2.cloned.1.call-update) | async-done | bytes 280592 | tf_op jit(solution)/shard_map/reduce_scatter | solution.py:231
  284.4 4.1 %fusion.10 = bf16[1,4,1024,128]{2,3,1,0:T(8,128)(2,1)} fusion(f32[4,1024,128]{1,2,0:T(8,128)} %copy-done.37, bf16[512,1024]{1,0:T(8,128)(2,1)} %param.17, f32[4,512,16,8]{1,0,3,2:T(4,128)S(1)} %copy-done.23, f32[4,512,128]{1,2,0:T(8,128)S(1)} %copy-done.19, f32[4]{0:T(128)S(1)} %copy-done.36, f32[512]{0:T(512)S(1)} %copy-done.35), kind=kOutput, calls=%fused_computation.21 | convolution fusion | flops 540803072 | bytes 6293520 | tf_op jit(solution)/shard_map/oc,nop->ncp/dot_general | solution.py:174
  288.5 2.3 copy.140
  290.8 18.7 %all-reduce.5.cloned.1.call-done = f32[32,2192]{1,0:T(8,128)} async-done(((f32[32,2192]{1,0:T(8,128)}), f32[32,2192]{1,0:T(8,128)}) %all-reduce.5.cloned.1.call-update) | async-done | bytes 280592 | tf_op jit(solution)/shard_map/psum | solution.py:228
  309.5 1.4 slice.178
  310.9 1.7 fusion.58
  (138 shorter events, 24.5 us)
Async XLA Ops:
  7.2 95.0 %copy-start = (bf16[512,1024]{1,0:T(8,128)(2,1)S(1)}, bf16[512,1024]{1,0:T(8,128)(2,1)}, u32[]{:S(2)}) copy-start(bf16[512,1024]{1,0:T(8,128)(2,1)} %param.19) | copy-start | bytes 3145732
  7.2 7.0 %copy-start.31 = (s32[1,16]{1,0:T(1,128)S(1)}, s32[1,16]{1,0:T(1,128)}, u32[]{:S(2)}) copy-start(s32[1,16]{1,0:T(1,128)} %param.26) | copy-start | bytes 196
  7.2 16.8 %copy-start.2 = (s32[1,31]{1,0:T(1,128)S(1)}, s32[1,31]{1,0:T(1,128)}, u32[]{:S(2)}) copy-start(s32[1,31]{1,0:T(1,128)} %param.27) | copy-start | bytes 376
  7.2 22.5 %copy-start.20 = (bf16[1,4,1024,128]{3,2,1,0:T(8,128)(2,1)S(1)}, bf16[1,4,1024,128]{3,2,1,0:T(8,128)(2,1)}, u32[]{:S(2)}) copy-start(bf16[1,4,1024,128]{3,2,1,0:T(8,128)(2,1)} %param.16) | copy-start | bytes 3145732
  7.2 277.2 %reduce-scatter.2.cloned.1.call-start = ((), (), s32[]{:S(2)}) async-start(), calls=%async_computation.1 | async-start | bytes 5013504 | tf_op jit(solution)/shard_map/reduce_scatter | solution.py:231
  9.7 1.0 copy-start.17
  10.7 20.3 %copy-start.27 = (bf16[512,144]{0,1:T(8,128)(2,1)S(1)}, bf16[512,144]{0,1:T(8,128)(2,1)}, u32[]{:S(2)}) copy-start(bf16[512,144]{0,1:T(8,128)(2,1)} %param.18) | copy-start | bytes 442372
  11.0 18.7 %copy-start.5 = (bf16[4,512,16,8]{1,3,2,0:T(8,128)(2,1)}, bf16[4,512,16,8]{1,3,2,0:T(8,128)(2,1)S(1)}, u32[]{:S(2)}) copy-start(bf16[4,512,16,8]{1,3,2,0:T(8,128)(2,1)S(1)} %fusion.39) | copy-start | bytes 1572868
  11.7 0.6 copy-start.25
  12.9 36.8 %collective-permute-start.1 = (bf16[1,16,512]{2,1,0:T(8,128)(2,1)}, bf16[1,16,512]{2,1,0:T(8,128)(2,1)}, u32[]{:S(2)}, u32[]{:S(2)}) collective-permute-start(bf16[1,16,512]{2,1,0:T(8,128)(2,1)} %bitcast.225), channel_id=1, source_target_pairs={{2,0},{4,2},{6,4},{8,6},{10,8},{12,10},{14,12},{16,14},{18,16},{20... | collective-permute-start | bytes 49160 | tf_op jit(solution)/shard_map/ppermute | solution.py:24
  16.8 34.0 %collective-permute-start = (bf16[1,16,512]{2,1,0:T(8,128)(2,1)}, bf16[1,16,512]{2,1,0:T(8,128)(2,1)}, u32[]{:S(2)}, u32[]{:S(2)}) collective-permute-start(bf16[1,16,512]{2,1,0:T(8,128)(2,1)} %bitcast.226), channel_id=1, source_target_pairs={{0,2},{2,4},{4,6},{6,8},{8,10},{10,12},{12,14},{14,16},{16,18},{18... | collective-permute-start | bytes 49160 | tf_op jit(solution)/shard_map/ppermute | solution.py:23
  29.7 64.3 %copy-start.6 = (bf16[128,128]{1,0:T(8,128)(2,1)}, bf16[128,128]{1,0:T(8,128)(2,1)S(1)}, u32[]{:S(2)}) copy-start(bf16[128,128]{1,0:T(8,128)(2,1)S(1)} %mul.202) | copy-start | bytes 98308
  39.4 10.4 %copy-start.24 = (bf16[3,512,16,1]{1,3,2,0:T(2,128)(2,1)S(1)}, bf16[3,512,16,1]{1,3,2,0:T(2,128)(2,1)}, u32[]{:S(2)}) copy-start(bf16[3,512,16,1]{1,3,2,0:T(2,128)(2,1)} %get-tuple-element.48) | copy-start | bytes 147460
  39.4 10.4 %copy-start.26 = (bf16[1,512,16,1]{1,3,2,0:T(2,128)(2,1)S(1)}, bf16[1,512,16,1]{1,3,2,0:T(2,128)(2,1)}, u32[]{:S(2)}) copy-start(bf16[1,512,16,1]{1,3,2,0:T(2,128)(2,1)} %copy-done.25) | copy-start | bytes 49156
  39.4 10.4 %copy-start.29 = (bf16[4]{0:T(256)(128)(2,1)S(1)}, bf16[4]{0:T(256)(128)(2,1)}, u32[]{:S(2)}) copy-start(bf16[4]{0:T(256)(128)(2,1)} %fusion.48) | copy-start | bytes 28
  39.4 11.4 %copy-start.28 = (bf16[1,512,16,1]{1,3,2,0:T(2,128)(2,1)S(1)}, bf16[1,512,16,1]{1,3,2,0:T(2,128)(2,1)}, u32[]{:S(2)}) copy-start(bf16[1,512,16,1]{1,3,2,0:T(2,128)(2,1)} %get-tuple-element.45) | copy-start | bytes 49156
  87.6 5.3 %copy-start.13 = (bf16[4,4,1,128,160]{3,1,0,4,2:T(4,128)(2,1)S(1)}, bf16[4,4,1,128,160]{3,1,0,4,2:T(4,128)(2,1)}, u32[]{:S(2)}) copy-start(bf16[4,4,1,128,160]{3,1,0,4,2:T(4,128)(2,1)} %reshape.305) | copy-start | bytes 1966084
  87.6 5.5 %copy-start.12 = (bf16[4,4,1,128,160]{3,1,0,4,2:T(4,128)(2,1)S(1)}, bf16[4,4,1,128,160]{3,1,0,4,2:T(4,128)(2,1)}, u32[]{:S(2)}) copy-start(bf16[4,4,1,128,160]{3,1,0,4,2:T(4,128)(2,1)} %reshape.306) | copy-start | bytes 1966084
  87.6 5.7 %copy-start.10 = (bf16[4,4,1,128,160]{3,1,0,4,2:T(4,128)(2,1)S(1)}, bf16[4,4,1,128,160]{3,1,0,4,2:T(4,128)(2,1)}, u32[]{:S(2)}) copy-start(bf16[4,4,1,128,160]{3,1,0,4,2:T(4,128)(2,1)} %reshape.307) | copy-start | bytes 1966084
  87.6 6.0 %copy-start.9 = (bf16[4,4,1,128,160]{3,1,0,4,2:T(4,128)(2,1)S(1)}, bf16[4,4,1,128,160]{3,1,0,4,2:T(4,128)(2,1)}, u32[]{:S(2)}) copy-start(bf16[4,4,1,128,160]{3,1,0,4,2:T(4,128)(2,1)} %reshape.308) | copy-start | bytes 1966084
  94.0 2.5 copy-start.3
  102.2 4.5 %copy-start.32 = (f32[1024]{0:T(1024)S(1)}, f32[1024]{0:T(1024)}, u32[]{:S(2)}) copy-start(f32[1024]{0:T(1024)} %param.24) | copy-start | bytes 12292
  102.2 4.5 %copy-start.33 = (f32[512]{0:T(512)S(1)}, f32[512]{0:T(512)}, u32[]{:S(2)}) copy-start(f32[512]{0:T(512)} %param.23) | copy-start | bytes 6148
  102.2 4.4 %copy-start.34 = (f32[512]{0:T(512)S(1)}, f32[512]{0:T(512)}, u32[]{:S(2)}) copy-start(f32[512]{0:T(512)} %param.22) | copy-start | bytes 6148
  106.6 1.4 copy-start.37
  107.8 8.5 %copy-start.30 = (bf16[4]{0:T(256)(128)(2,1)S(1)}, bf16[4]{0:T(256)(128)(2,1)}, u32[]{:S(2)}) copy-start(bf16[4]{0:T(256)(128)(2,1)} %fusion.48) | copy-start | bytes 28
  110.4 5.9 %collective-permute-start.3 = (bf16[1,16,512]{2,1,0:T(8,128)(2,1)S(1)}, bf16[1,16,512]{2,1,0:T(8,128)(2,1)S(1)}, u32[]{:S(2)}, u32[]{:S(2)}) collective-permute-start(bf16[1,16,512]{2,1,0:T(8,128)(2,1)S(1)} %bitcast.236), channel_id=1, source_target_pairs={{2,0},{4,2},{6,4},{8,6},{10,8},{12,10},{14,12},{16,14},{18,16},{20... | collective-permute-start | bytes 49160 | tf_op jit(solution)/shard_map/ppermute | solution.py:24
  111.8 5.4 %collective-permute-start.2 = (bf16[1,16,512]{2,1,0:T(8,128)(2,1)S(1)}, bf16[1,16,512]{2,1,0:T(8,128)(2,1)S(1)}, u32[]{:S(2)}, u32[]{:S(2)}) collective-permute-start(bf16[1,16,512]{2,1,0:T(8,128)(2,1)S(1)} %bitcast.235), channel_id=1, source_target_pairs={{0,2},{2,4},{4,6},{6,8},{8,10},{10,12},{12,14},{14,16},{16,18},{18... | collective-permute-start | bytes 49160 | tf_op jit(solution)/shard_map/ppermute | solution.py:23
  121.1 5.5 %copy-start.15 = (bf16[4,512,16,10]{1,0,3,2:T(4,128)(2,1)S(1)}, bf16[4,512,16,10]{1,0,3,2:T(4,128)(2,1)}, u32[]{:S(2)}) copy-start(bf16[4,512,16,10]{1,0,3,2:T(4,128)(2,1)} %copy.110) | copy-start | bytes 1966084
  141.4 9.7 %copy-start.8 = (bf16[4,4,1,128,160]{3,1,4,0,2:T(4,128)(2,1)S(1)}, bf16[4,4,1,128,160]{3,1,4,0,2:T(4,128)(2,1)}, u32[]{:S(2)}) copy-start(bf16[4,4,1,128,160]{3,1,4,0,2:T(4,128)(2,1)} %reshape.315) | copy-start | bytes 1966084
  145.6 5.3 %copy-start.14 = (bf16[4,4,1,128,160]{3,1,0,4,2:T(4,128)(2,1)S(1)}, bf16[4,4,1,128,160]{3,1,0,4,2:T(4,128)(2,1)}, u32[]{:S(2)}) copy-start(bf16[4,4,1,128,160]{3,1,0,4,2:T(4,128)(2,1)} %reshape.314) | copy-start | bytes 1966084
  145.6 5.7 %copy-start.11 = (bf16[4,4,1,128,160]{3,1,0,4,2:T(4,128)(2,1)S(1)}, bf16[4,4,1,128,160]{3,1,0,4,2:T(4,128)(2,1)}, u32[]{:S(2)}) copy-start(bf16[4,4,1,128,160]{3,1,0,4,2:T(4,128)(2,1)} %reshape.316) | copy-start | bytes 1966084
  148.3 3.7 %copy-start.7 = (bf16[128,128]{1,0:T(8,128)(2,1)S(1)}, bf16[128,128]{1,0:T(8,128)(2,1)}, u32[]{:S(2)}) copy-start(bf16[128,128]{1,0:T(8,128)(2,1)} %copy-done.6) | copy-start | bytes 98308
  153.6 5.2 %copy-start.18 = (f32[4,512,128]{1,2,0:T(8,128)S(1)}, f32[4,512,128]{1,2,0:T(8,128)}, u32[]{:S(2)}) copy-start(f32[4,512,128]{1,2,0:T(8,128)} %copy-done.17) | copy-start | bytes 3145732
  153.7 5.2 %copy-start.35 = (f32[512]{0:T(512)S(1)}, f32[512]{0:T(512)}, u32[]{:S(2)}) copy-start(f32[512]{0:T(512)} %param.20) | copy-start | bytes 6148
  153.7 5.2 %copy-start.36 = (f32[4]{0:T(128)S(1)}, f32[4]{0:T(128)}, u32[]{:S(2)}) copy-start(f32[4]{0:T(128)} %compare_convert_fusion) | copy-start | bytes 52
  156.4 6.4 %copy-start.4 = (f32[4,128,9,128]{3,1,2,0:T(8,128)S(1)}, f32[4,128,9,128]{3,1,2,0:T(8,128)}, u32[]{:S(2)}) copy-start(f32[4,128,9,128]{3,1,2,0:T(8,128)} %fusion.6) | copy-start | bytes 7077892
  157.9 1.0 copy-start.22
  189.7 3.5 %copy-start.16 = (f32[512,1024]{1,0:T(8,128)S(1)}, f32[512,1024]{1,0:T(8,128)}, u32[]{:S(2)}) copy-start(f32[512,1024]{1,0:T(8,128)} %convolution_bitcast_fusion) | copy-start | bytes 6291460
  203.3 1.2 copy-start.21
  203.3 81.1 %copy-start.19 = (f32[4,512,128]{1,2,0:T(8,128)S(1)}, f32[4,512,128]{1,2,0:T(8,128)}, u32[]{:S(2)}) copy-start(f32[4,512,128]{1,2,0:T(8,128)} %copy-done.17) | copy-start | bytes 3145732
  203.3 81.1 %copy-start.23 = (f32[4,512,16,8]{1,0,3,2:T(4,128)S(1)}, f32[4,512,16,8]{1,0,3,2:T(4,128)}, u32[]{:S(2)}) copy-start(f32[4,512,16,8]{1,0,3,2:T(4,128)} %copy-done.22) | copy-start | bytes 3145732
  203.3 106.1 %all-reduce.5.cloned.1.call-start = ((), (), s32[]{:S(2)}) async-start(), calls=%async_computation.2 | async-start | bytes 589824 | tf_op jit(solution)/shard_map/psum | solution.py:228
  284.4 28.2 %copy-start.1 = (bf16[512,1024]{1,0:T(8,128)(2,1)S(1)}, bf16[512,1024]{1,0:T(8,128)(2,1)}, u32[]{:S(2)}) copy-start(bf16[512,1024]{1,0:T(8,128)(2,1)} %param.19) | copy-start | bytes 3145732
Sparse Core Ops, SparseCore 0:
  203.5 80.8 reduce-scatter.1
  286.8 22.6 all-reduce.4
where the time goes:
time: 325 us; the launch traced here: 320 us
  local copies, waits for them, and re-layouts  141 us (43%)
  waiting for transfers between devices  97.8 us (30%)
  matrix products  40.1 us (12%)
  between operations  16.3 us (5%)
  other arithmetic  14 us (4%)
  starting transfers between devices  10.8 us (3%)
    reduce_scatter x1, waiting for transfers between devices, shards(): combined = lax.psum_scatter(whole, 'tile', scatter_dimension=0, tiled=True)  78.5 us
    another operation x20, local copies, waits for them, and re-layouts, stacked_windows(): return jnp.stack(windows, 2)  46.9 us
    unnamed x100, local copies, waits for them, and re-layouts  26.9 us
    mul x6, local copies, waits for them, and re-layouts, dense_taps(): tap_weights[:, :, :, :, None, :] * picker[None, :, None, None, :, None]  19 us
    psum x1, waiting for transfers between devices, shards(): lax.psum(jnp.concatenate([part_reduce, group_grad, part_expand], 1) * sca...  18.7 us
    dot_general x1, matrix products, group_weight_grad(): jnp.einsum('bxotyi,xy->bxoti', full_grad, picker, precision=lax.Precision...  12.9 us
    reshape x1, local copies, waits for them, and re-layouts, group_weight_grad(): full_grad = full_grad.reshape(blocks, per_block, GW, 9, per_block, GW)  9.81 us
    ppermute x2, starting transfers between devices, with_halo(): before = lax.ppermute(last, axis, up)  8.16 us
  transfers between devices with their start and end apart: 6, of which 3 were waited for; matrix products, arithmetic and copies ran while one was open for 12% of the time, Pallas kernels for 0%

commit v1 on v0

v1 whole, which is shorter than its diff:
```python
import functools
import math

import jax
import jax.numpy as jnp
from jax import lax
from jax.experimental import pallas as pl
from jax.experimental.pallas import tpu as pltpu
from jax.sharding import PartitionSpec as P

CIN = 1024
MID = 512
GW = 16
TH = 16
TW = 8
PIX = 128
SLOTS = 4
HALF = 256
TAPS = 9
KDIM = TAPS * HALF
PAY = 48
LIVE_DEV = 2
BF = jnp.bfloat16
F32 = jnp.float32
VMEM_LIMIT = 56 * 1024 * 1024

HELD, L_LINK, R_LINK, L_IDX, R_IDX, META = 0, 1, 6, 11, 16, 24


def nt_dot(a, b):
    return lax.dot_general(a, b, (((1,), (1,)), ((), ())), preferred_element_type=F32)


def tn_dot(a, b):
    return lax.dot_general(a, b, (((0,), (0,)), ((), ())), preferred_element_type=F32)


def nn_dot(a, b):
    return lax.dot_general(a, b, (((1,), (0,)), ((), ())), preferred_element_type=F32)


def sigmoid(v):
    return 0.5 * jnp.tanh(0.5 * v) + 0.5


def column(row_ref):
    row = row_ref[...]
    return jnp.transpose(jnp.broadcast_to(row, (PIX, row.shape[1])))


def wide(col, lanes):
    return jnp.concatenate([col] * (lanes // PIX), axis=1)


def edge_select(rows, lane_of):
    row = lax.broadcasted_iota(jnp.int32, (rows, PIX), 0)
    lane = lax.broadcasted_iota(jnp.int32, (rows, PIX), 1)
    return (lane == lane_of(row)).astype(F32).astype(BF)


def x_lane(first):
    return lambda row: (row % TH) * TW + row // TH + first


def g_lane(col):
    return lambda row: row * TW + col


def edge_kernel(count_ref, joined_ref, x_any, g_any, core_ref, other_ref, meta_ref, xbuf, gbuf, sems):
    me = lax.axis_index("tile")
    devices = count_ref.shape[1]
    links = joined_ref.shape[1]
    start = jnp.int32(0)
    held = jnp.int32(0)
    for e in range(devices):
        start = start + jnp.where(e < me, count_ref[0, e], 0)
        held = held + jnp.where(e == me, count_ref[0, e], 0)
    last = held - 1
    copies = []
    for k, (src, dst, slot) in enumerate(
        ((x_any, xbuf, 0), (g_any, gbuf, 0), (x_any, xbuf, last), (g_any, gbuf, last))
    ):
        copy = pltpu.make_async_copy(src.at[slot], dst.at[k // 2], sems.at[k])
        copy.start()
        copies.append(copy)

    def link(at):
        inside = jnp.logical_and(at >= 0, at < links)
        return jnp.where(inside, joined_ref[0, jnp.clip(at, 0, links - 1)], 0)

    meta_ref[HELD] = held
    first_left = link(start - 1)
    last_right = link(start + last)
    for i in range(SLOTS):
        live = i < held
        meta_ref[L_LINK + i] = jnp.where(live, link(start + i - 1), 0)
        meta_ref[R_LINK + i] = jnp.where(live, link(start + i), 0)
        meta_ref[L_IDX + i] = jnp.int32(SLOTS if i == 0 else i - 1)
        meta_ref[R_IDX + i] = jnp.where(i >= last, SLOTS, i + 1).astype(jnp.int32)
    meta_ref[L_LINK + SLOTS] = last_right
    meta_ref[R_LINK + SLOTS] = first_left
    meta_ref[L_IDX + SLOTS] = last
    meta_ref[R_IDX + SLOTS] = jnp.int32(0)

    for copy in copies:
        copy.wait()
    even = me % 2 == 0

    def payload(side, x_first, g_col):
        return (
            nt_dot(edge_select(2 * TH, x_lane(x_first)), xbuf[side]).astype(BF),
            nt_dot(edge_select(TH, g_lane(g_col)), gbuf[side]).astype(BF),
        )

    left_x, left_g = payload(0, 0, 0)
    right_x, right_g = payload(1, TW - 2, TW - 1)

    @pl.when(even)
    def _():
        core_ref[: 2 * TH] = right_x
        core_ref[2 * TH :] = right_g
        other_ref[: 2 * TH] = left_x
        other_ref[2 * TH :] = left_g

    @pl.when(jnp.logical_not(even))
    def _():
        core_ref[: 2 * TH] = left_x
        core_ref[2 * TH :] = left_g
        other_ref[: 2 * TH] = right_x
        other_ref[2 * TH :] = right_g


def prep_kernel(
    meta_ref, x_ref, wr_ref, we_ref, wg_ref, s1_ref, b1_ref,
    hid_ref, slope_ref, dense_ref, denset_ref, wet_ref,
):
    scale = column(s1_ref)
    shift = column(b1_ref)
    held = meta_ref[HELD]
    for half in range(SLOTS // 2):
        tiles = jnp.concatenate([x_ref[2 * half], x_ref[2 * half + 1]], axis=1)
        reduced = nn_dot(wr_ref[...], tiles)
        for k in range(2):
            i = 2 * half + k
            pre = reduced[:, k * PIX : (k + 1) * PIX] * scale + shift
            sig = sigmoid(pre)
            act = pre * sig
            hid_ref[i] = act.astype(BF)
            live = jnp.where(i < held, 1.0, 0.0).astype(F32)
            slope_ref[i] = (sig + act * (1.0 - sig)) * (scale * live)
    tap_row = lax.broadcasted_iota(jnp.int32, (TAPS * GW, KDIM), 0)
    lane = lax.broadcasted_iota(jnp.int32, (TAPS * GW, KDIM), 1)
    pick = (tap_row == (lane // HALF) * GW + lane % GW).astype(F32).astype(BF)
    spread = nn_dot(wg_ref[...], pick)
    row = lax.broadcasted_iota(jnp.int32, (MID, KDIM), 0)
    col = lax.broadcasted_iota(jnp.int32, (MID, KDIM), 1)
    keep = (row % HALF) // GW == (col % HALF) // GW
    dense_ref[...] = jnp.where(keep, spread, 0.0).astype(BF).reshape(2, HALF, KDIM)
    row_t = lax.broadcasted_iota(jnp.int32, (HALF, MID), 0)
    col_t = lax.broadcasted_iota(jnp.int32, (HALF, MID), 1)
    keep_t = row_t // GW == (col_t % HALF) // GW
    prow = lax.broadcasted_iota(jnp.int32, (HALF, TAPS * GW), 0)
    pcol = lax.broadcasted_iota(jnp.int32, (HALF, TAPS * GW), 1)
    for k in range(TAPS):
        pick_t = (pcol == k * GW + prow % GW).astype(F32).astype(BF)
        spread_t = jnp.where(keep_t, nt_dot(pick_t, wg_ref[...]), 0.0).astype(BF)
        for b in range(2):
            denset_ref[b, :, k * HALF : (k + 1) * HALF] = spread_t[:, b * HALF : (b + 1) * HALF]
    wet_ref[...] = jnp.transpose(we_ref[...])


def build_windows(field_ref, win_ref, meta_ref, tiles, transposed):
    lane = lax.broadcasted_iota(jnp.int32, (HALF, PIX), 1)
    col = lane % TW
    first_col = col == 0
    last_col = col == TW - 1
    has_above = lane >= TW
    has_below = lane < PIX - TW
    for i in range(tiles):
        left_at = meta_ref[L_IDX + i]
        right_at = meta_ref[R_IDX + i]
        left_link = meta_ref[L_LINK + i].astype(F32)
        right_link = meta_ref[R_LINK + i].astype(F32)
        lanes = pl.ds(i * PIX, PIX)
        for b in range(2):
            rows = pl.ds(b * HALF, HALF)
            own = field_ref[i, rows, :].astype(F32)
            left = field_ref[left_at, rows, :].astype(F32) * left_link
            right = field_ref[right_at, rows, :].astype(F32) * right_link
            west = jnp.where(first_col, pltpu.roll(left, PIX - TW + 1, 1), pltpu.roll(own, 1, 1))
            east = jnp.where(last_col, pltpu.roll(right, TW - 1, 1), pltpu.roll(own, PIX - 1, 1))
            for v, base in enumerate((west, own, east)):
                above = jnp.where(has_above, pltpu.roll(base, TW, 1), 0.0)
                below = jnp.where(has_below, pltpu.roll(base, PIX - TW, 1), 0.0)
                for u, shifted in enumerate((above, base, below)):
                    tap = 3 * u + v
                    if transposed:
                        tap = TAPS - 1 - tap
                    win_ref[b, pl.ds(tap * HALF, HALF), lanes] = shifted.astype(BF)


def forward_kernel(
    devices, meta_ref, core_ref, other_ref, hid_in, wr_ref, s1_ref, b1_ref, dense_ref,
    s2_ref, b2_ref, wet_ref, we_ref, s3_ref, b3_ref, x_ref, g_ref,
    out_ref, back_ref, errb_ref, send_ref, keep_ref,
    hid_ref, win_ref, hidb_ref, slopeb_ref, errc_ref,
):
    me = lax.axis_index("tile")
    held = meta_ref[HELD]
    odd = me % 2
    scale1 = column(s1_ref)
    shift1 = column(b1_ref)
    core_first = jnp.where(odd == 0, 0, TW - 2)
    other_first = jnp.where(odd == 0, TW - 2, 0)
    core_g = jnp.where(odd == 0, 0, TW - 1)
    other_g = jnp.where(odd == 0, TW - 1, 0)
    edge_x = (
        tn_dot(core_ref[: 2 * TH, :], edge_select(2 * TH, x_lane(core_first)))
        + tn_dot(other_ref[: 2 * TH, :], edge_select(2 * TH, x_lane(other_first)))
    ).astype(BF)
    edge_g = (
        tn_dot(core_ref[2 * TH :, :], edge_select(TH, g_lane(core_g)))
        + tn_dot(other_ref[2 * TH :, :], edge_select(TH, g_lane(other_g)))
    )
    for i in range(SLOTS):
        hid_ref[i] = hid_in[i]
    pre = nn_dot(wr_ref[...], edge_x) * scale1 + shift1
    hid_ref[SLOTS] = (pre * sigmoid(pre)).astype(BF)

    build_windows(hid_ref, win_ref, meta_ref, SLOTS + 1, False)

    scale2 = column(s2_ref)
    shift2 = column(b2_ref)
    for b in range(2):
        conv = nn_dot(dense_ref[b], win_ref[b])
        rows = slice(b * HALF, (b + 1) * HALF)
        for i in range(SLOTS + 1):
            v = conv[:, i * PIX : (i + 1) * PIX] * scale2[rows] + shift2[rows]
            sig = sigmoid(v)
            act = v * sig
            hidb_ref[rows, i * PIX : (i + 1) * PIX] = act.astype(BF)
            slopeb_ref[rows, i * PIX : (i + 1) * PIX] = (sig + act * (1.0 - sig)) * scale2[rows]

    scale3 = column(s3_ref)
    shift3 = column(b3_ref)
    for first, count in ((0, 2), (2, 2), (4, 1)):
        grown = nn_dot(wet_ref[...], hidb_ref[:, first * PIX : (first + count) * PIX])
        for k in range(count):
            i = first + k
            if i < SLOTS:
                tile = x_ref[i].astype(F32)
                cot = g_ref[i].astype(F32)
            else:
                tile = edge_x.astype(F32)
                cot = edge_g
            total = grown[:, k * PIX : (k + 1) * PIX] * scale3 + shift3 + tile
            sig = sigmoid(total)
            act = total * sig
            back = cot * (sig + act * (1.0 - sig))
            if i < SLOTS:
                live = jnp.where(i < held, 1.0, 0.0).astype(F32)
                back = back * live
                out_ref[i] = (act * live).astype(BF)
                back_ref[i] = back
            errc_ref[:, i * PIX : (i + 1) * PIX] = (back * scale3).astype(BF)

    order_rows(devices, me, hidb_ref, errc_ref, SLOTS * PIX, send_ref, keep_ref)

    for first, count in ((0, 2), (2, 2), (4, 1)):
        lanes = slice(first * PIX, (first + count) * PIX)
        pulled = nn_dot(we_ref[...], errc_ref[:, lanes])
        errb = (pulled * slopeb_ref[:, lanes]).astype(BF)
        for k in range(count):
            errb_ref[first + k] = errb[:, k * PIX : (k + 1) * PIX]


def order_rows(devices, me, left_ref, right_ref, lanes, send_ref, keep_ref):
    per = MID // devices
    for ref, flip in ((send_ref, 1), (keep_ref, 0)):
        picked = []
        for pair in range(devices // 2):
            dy, rest = pair // (devices // 4), pair % (devices // 4)
            target = (rest * 4) + (((me // 2) % 2) ^ dy) * 2 + ((me % 2) ^ flip)
            at = pl.multiple_of(target * per, per)
            picked.append(left_ref[pl.ds(at, per), :lanes])
        rows = jnp.concatenate(picked, axis=0)
        ref[...] = nt_dot(rows, right_ref[:, :lanes]).astype(BF)


def backward_kernel(
    devices, meta_ref, errb_ref, hid_ref, slope_ref, denset_ref, x_ref,
    erra_ref, send_ref, keep_ref, win_ref, flat_ref, groups_ref,
):
    me = lax.axis_index("tile")
    build_windows(errb_ref, win_ref, meta_ref, SLOTS, True)
    for b in range(2):
        conv = nn_dot(denset_ref[b], win_ref[b])
        rows = slice(b * HALF, (b + 1) * HALF)
        for i in range(SLOTS):
            err = (conv[:, i * PIX : (i + 1) * PIX] * slope_ref[i, rows, :]).astype(BF)
            flat_ref[rows, i * PIX : (i + 1) * PIX] = err
            erra_ref[i, rows, :] = err
    row = lax.broadcasted_iota(jnp.int32, (HALF, HALF), 0)
    col = lax.broadcasted_iota(jnp.int32, (HALF, HALF), 1)
    same = row // GW == col // GW
    for b in range(2):
        rows = slice(b * HALF, (b + 1) * HALF)
        hid = jnp.concatenate([hid_ref[i, rows, :] for i in range(SLOTS)], axis=1)
        folded = jnp.zeros((HALF, HALF), F32)
        for k in range(TAPS):
            full = nt_dot(win_ref[b, k * HALF : (k + 1) * HALF, :], hid)
            kept = jnp.where(same, full, 0.0).astype(BF)
            place = (col == k * GW + row % GW).astype(F32).astype(BF)
            folded = folded + nn_dot(kept, place)
        groups_ref[rows, :] = folded.astype(BF)
    tiles = jnp.concatenate([x_ref[i] for i in range(SLOTS)], axis=1)
    per = MID // devices
    for ref, flip in ((send_ref, 1), (keep_ref, 0)):
        picked, group_rows = [], []
        for pair in range(devices // 2):
            target = pair * 2 + ((me % 2) ^ flip)
            at = pl.multiple_of(target * per, per)
            picked.append(flat_ref[pl.ds(at, per), :])
            ref[pl.ds(pair * per, per), CIN:] = groups_ref[pl.ds(at, per), :]
        rows = jnp.concatenate(picked, axis=0)
        ref[:, :CIN] = nt_dot(rows, tiles).astype(BF)


def grad_kernel(wr_ref, erra_ref, back_ref, grad_ref):
    for half in range(SLOTS // 2):
        err = jnp.concatenate([erra_ref[2 * half], erra_ref[2 * half + 1]], axis=1)
        pulled = tn_dot(wr_ref[...], err)
        for k in range(2):
            i = 2 * half + k
            grad_ref[i] = (pulled[:, k * PIX : (k + 1) * PIX] + back_ref[i]).astype(BF)


def call(body, name, out_shape, in_smem, in_any, n_in, scratch=(), out_smem=()):
    vmem = pl.BlockSpec(memory_space=pltpu.VMEM)
    smem = pl.BlockSpec(memory_space=pltpu.SMEM)
    anys = pl.BlockSpec(memory_space=pl.ANY)
    return pl.pallas_call(
        body,
        name=name,
        out_shape=out_shape,
        in_specs=[smem if i in in_smem else anys if i in in_any else vmem for i in range(n_in)],
        out_specs=[smem if i in out_smem else vmem for i in range(len(out_shape))],
        scratch_shapes=list(scratch),
        compiler_params=pltpu.CompilerParams(vmem_limit_bytes=VMEM_LIMIT),
    )


def shape(dims, dtype):
    return jax.ShapeDtypeStruct(dims, dtype)


def swap(value, axis, mask):
    size = lax.axis_size(axis)
    return lax.ppermute(value, axis, [(i, i ^ mask) for i in range(size)])


def add_pair(a, b):
    return (a.astype(F32) + b.astype(F32)).astype(BF)


def shards(
    feats, cotangent, w_reduce, w_group, w_expand, scale1, shift1, scale2, shift2,
    scale3, shift3, tile_count, joined,
):
    devices = lax.axis_size("tile")
    slides = lax.axis_size("slide")
    per = MID // devices
    x, g = feats[0], cotangent[0]
    s1, b1, s2, b2 = (v.reshape(1, MID) for v in (scale1, shift1, scale2, shift2))
    s3, b3 = (v.reshape(1, CIN) for v in (scale3, shift3))

    to_core, to_other, meta = call(
        edge_kernel, "edges",
        [shape((PAY, CIN), BF), shape((PAY, CIN), BF), shape((META,), jnp.int32)],
        (0, 1), (2, 3), 4,
        [pltpu.VMEM((2, CIN, PIX), BF), pltpu.VMEM((2, CIN, PIX), BF), pltpu.SemaphoreType.DMA((4,))],
        (2,),
    )(tile_count, joined, x, g)
    from_core = swap(to_core, "tile", 1)
    hops = [(i, i + 1) for i in range(1, devices - 1, 2)]
    from_other = lax.ppermute(to_other, "tile", hops + [(b, a) for a, b in hops])

    hid, slope_a, dense, denset, wet = call(
        prep_kernel, "prep",
        [shape((SLOTS, MID, PIX), BF), shape((SLOTS, MID, PIX), F32), shape((2, HALF, KDIM), BF),
         shape((2, HALF, KDIM), BF), shape((CIN, MID), BF)],
        (0,), (), 7,
    )(meta, x, w_reduce, w_expand, w_group, s1, b1)

    out, back, errb, e_send, e_keep = call(
        functools.partial(forward_kernel, devices), "forward",
        [shape((SLOTS, CIN, PIX), BF), shape((SLOTS, CIN, PIX), F32), shape((SLOTS + 1, MID, PIX), BF),
         shape((HALF, CIN), BF), shape((HALF, CIN), BF)],
        (0,), (), 16,
        [pltpu.VMEM((SLOTS + 1, MID, PIX), BF), pltpu.VMEM((2, KDIM, (SLOTS + 1) * PIX), BF),
         pltpu.VMEM((MID, (SLOTS + 1) * PIX), BF), pltpu.VMEM((MID, (SLOTS + 1) * PIX), F32),
         pltpu.VMEM((CIN, (SLOTS + 1) * PIX), BF)],
    )(meta, from_core, from_other, hid, w_reduce, s1, b1, dense, s2, b2, wet, w_expand, s3, b3, x, g)

    e_core = swap(e_send, "tile", 1)
    erra, r_send, r_keep = call(
        functools.partial(backward_kernel, devices), "backward",
        [shape((SLOTS, MID, PIX), BF), shape((HALF, CIN + HALF), BF), shape((HALF, CIN + HALF), BF)],
        (0,), (), 6,
        [pltpu.VMEM((2, KDIM, SLOTS * PIX), BF), pltpu.VMEM((MID, SLOTS * PIX), BF), pltpu.VMEM((MID, HALF), BF)],
    )(meta, errb, hid, slope_a, denset, x)

    (grad_in,) = call(
        grad_kernel, "grads", [shape((SLOTS, CIN, PIX), BF)], (), (), 3,
    )(w_reduce, erra, back)

    quarter = HALF // 2
    e_half = add_pair(e_keep, e_core)
    e_y = swap(e_half[quarter:], "tile", 2)
    e_quarter = add_pair(e_half[:quarter], e_y)
    r_core = swap(r_send, "tile", 1)
    r_half = add_pair(r_keep, r_core)
    groups4 = [[low + 4 * k for k in range(devices // 4)] for low in range(4)]
    groups2 = [[low + 2 * k for k in range(devices // 2)] for low in range(2)]
    e_all = lax.all_to_all(e_quarter, "tile", 0, 0, axis_index_groups=groups4, tiled=True)
    r_all = lax.all_to_all(r_half, "tile", 0, 0, axis_index_groups=groups2, tiled=True)
    e_sum = jnp.sum(e_all.reshape(devices // 4, per, CIN).astype(F32), 0)
    r_sum = jnp.sum(r_all.reshape(devices // 2, per, CIN + HALF).astype(F32), 0)
    total = jnp.concatenate([e_sum, r_sum], axis=1).astype(BF)
    mask = 1
    while mask < slides:
        total = total.astype(F32) + swap(total.astype(BF), "slide", mask).astype(F32)
        mask *= 2
    norm = 1.0 / math.sqrt(slides * LIVE_DEV * devices * PIX)
    total = total.astype(F32) * norm
    grad_expand = total[:, :CIN]
    grad_reduce = total[:, CIN : 2 * CIN]
    grad_group = total[:, 2 * CIN : 2 * CIN + TAPS * GW]
    return (out[None], grad_in[None], grad_reduce, grad_group, grad_expand)


def solution(mesh):
    tiles = P("slide", "tile", None, None)
    in_specs = (tiles, tiles) + (P(),) * 9 + (P("slide", None), P("slide", None))
    out_specs = (tiles, tiles, P("tile", None), P("tile", None), P("tile", None))
    return jax.shard_map(shards, mesh=mesh, in_specs=in_specs, out_specs=out_specs, check_vma=False)
```

time: 325 us -> 89 us (0.27); the launches traced: 320 us -> 88.7 us
  local copies, waits for them, and re-layouts: 141 us -> 2.86 us
  waiting for transfers between devices: 97.8 us -> 30.6 us
  matrix products: 40.1 us -> 0 us
  Pallas kernels: 0 us -> 35.7 us
  between operations: 16.3 us -> 0.75 us
  other arithmetic: 14 us -> 2.14 us
  starting transfers between devices: 10.8 us -> 16.7 us
    reduce_scatter x1 -> x0, waiting for transfers between devices: 78.5 us -> none  [shards(): combined = lax.psum_scatter(whole, 'tile', scatter_dimension=0, tiled=True)]
    another operation x21 -> x0, local copies, waits for them, and re-layouts: 47 us -> none  [the longest x20 46.9 us: stacked_windows(): return jnp.stack(windows, 2)]
    dot_general x10 -> x0, matrix products: 40.1 us -> none  [the longest x1 12.9 us: group_weight_grad(): jnp.einsum('bxotyi,xy->bxoti', full_grad, picker, precision=lax.Precision...]
    pallas_call x0 -> x5, Pallas kernels: none -> 35.7 us  [the longest x1 11.9 us: shards(): call(functools.partial(forward_kernel, devices), 'forward', [shape((SLOTS...]
    unnamed x100 -> x11, local copies, waits for them, and re-layouts: 26.9 us -> 1.5 us
    all_to_all x0 -> x2, waiting for transfers between devices: none -> 23.4 us  [the longest x1 15.9 us: shards(): lax.all_to_all(r_half, 'tile', 0, 0, axis_index_groups=groups2, tiled=True)]
    mul x6 -> x0, local copies, waits for them, and re-layouts: 19 us -> none  [dense_taps(): tap_weights[:, :, :, :, None, :] * picker[None, :, None, None, :, None]]
    psum x1 -> x0, waiting for transfers between devices: 18.7 us -> none  [shards(): lax.psum(jnp.concatenate([part_reduce, group_grad, part_expand], 1) * sca...]
  transfers between devices with their start and end apart: 6 -> 8, of which waited for: 3 -> 3; matrix products, arithmetic and copies ran while one was open for 12% -> 3% of each run, Pallas kernels for 0% -> 23%
where the time goes in v1:
time: 89 us; the launch traced here: 88.7 us
  Pallas kernels  35.7 us (40%)
  waiting for transfers between devices  30.6 us (34%)
  starting transfers between devices  16.7 us (19%)
  local copies, waits for them, and re-layouts  2.86 us (3%)
  other arithmetic  2.14 us (2%)
    all_to_all x1, waiting for transfers between devices, shards(): lax.all_to_all(r_half, 'tile', 0, 0, axis_index_groups=groups2, tiled=True)  15.9 us
    pallas_call x1, Pallas kernels, shards(): call(functools.partial(forward_kernel, devices), 'forward', [shape((SLOTS...  11.9 us
    pallas_call x1, Pallas kernels, shards(): call(functools.partial(backward_kernel, devices), 'backward', [shape((SLO...  10.6 us
    ppermute x5, starting transfers between devices, swap(): return lax.ppermute(value, axis, [(i, i ^ mask) for i in range(size)])  7.51 us
    all_to_all x1, waiting for transfers between devices, shards(): lax.all_to_all(e_quarter, 'tile', 0, 0, axis_index_groups=groups4, tiled=...  7.49 us
    ppermute x5, waiting for transfers between devices, swap(): return lax.ppermute(value, axis, [(i, i ^ mask) for i in range(size)])  7.19 us
    pallas_call x1, Pallas kernels, shards(): call(prep_kernel, 'prep', [shape((SLOTS, MID, PIX), BF), shape((SLOTS, MI...  6.22 us
    all_to_all x1, starting transfers between devices, shards(): lax.all_to_all(e_quarter, 'tile', 0, 0, axis_index_groups=groups4, tiled=...  4.98 us
  transfers between devices with their start and end apart: 8, of which 3 were waited for; matrix products, arithmetic and copies ran while one was open for 3% of the time, Pallas kernels for 23%

profile of v1, /device:TPU:0, one launch (start us, length us, event | category | flops | bytes accessed | tf_op | source)
XLA Modules:
  0.0 88.7 jit_solution(17557508665555696451)
XLA Ops:
  0.6 0.0 copy-start.2
  0.6 3.2 %edges.1 = (bf16[48,1024]{1,0:T(8,128)(2,1)}, bf16[48,1024]{1,0:T(8,128)(2,1)}, s32[24]{0:T(128)}) custom-call(s32[1,16]{1,0:T(1,128)} %count_ref.1, s32[1,31]{1,0:T(1,128)} %joined_ref.1, bf16[4,1024,128]{2,1,0:T(8,128)(2,1)} %bitcast.12, bf16[4,1024,128]{2,1,0:T(8,128)(2,1)} %bitcast.16), custom_call_target="tpu_custom_call" | custom-call | tf_op jit(solution)/shard_map/edges/pallas_call | solution.py:377
  3.8 0.5 collective-permute-start
  4.3 0.7 collective-permute-start.1
  5.0 0.0 copy-done.2
  5.0 0.8 copy.18.wg_ref
  5.9 6.2 %prep.1 = (bf16[4,512,128]{2,1,0:T(8,128)(2,1)}, f32[4,512,128]{2,1,0:T(8,128)}, bf16[2,256,2304]{2,1,0:T(8,128)(2,1)}, bf16[2,256,2304]{2,1,0:T(8,128)(2,1)}, bf16[1024,512]{1,0:T(8,128)(2,1)}) custom-call(s32[24]{0:T(128)} %get-tuple-element.21.meta_ref, bf16[4,1024,128]{2,1,0:T(8,128)(2,1)} %bitcast.13, bf16[512,1024]{1,0:T(8,128)(2,1)} %wr_ref.5, ...), custom_call_target="tpu_custom_call" | custom-call | tf_op jit(solution)/shard_map/prep/pallas_call | solution.py:388
  12.1 0.0 collective-permute-done.core_ref
  12.1 0.0 copy-start.3
  12.1 0.0 collective-permute-done.1.other_ref
  12.1 0.0 copy-start.4
  12.1 0.6 copy-done.3
  12.7 0.0 copy-done.4
  12.7 11.9 %forward.1 = (bf16[4,1024,128]{2,1,0:T(8,128)(2,1)}, f32[4,1024,128]{2,1,0:T(8,128)}, bf16[5,512,128]{2,1,0:T(8,128)(2,1)}, bf16[256,1024]{1,0:T(8,128)(2,1)}, bf16[256,1024]{1,0:T(8,128)(2,1)}) custom-call(s32[24]{0:T(128)} %get-tuple-element.21.meta_ref, bf16[48,1024]{1,0:T(8,128)(2,1)} %copy-done.3, bf16[48,1024]{1,0:T(8,128)(2,1)} %copy-done.4, ...), custom_call_target="tpu_custom_call" | custom-call | tf_op jit(solution)/shard_map/forward/pallas_call | solution.py:395
  24.7 3.9 %collective-permute-start.2 = (bf16[256,1024]{1,0:T(8,128)(2,1)}, bf16[256,1024]{1,0:T(8,128)(2,1)S(1)}, u32[]{:S(2)}, u32[]{:S(2)}) collective-permute-start(bf16[256,1024]{1,0:T(8,128)(2,1)} %get-tuple-element.34), channel_id=1, source_target_pairs={{0,2},{2,0},{4,6},{6,4},{8,10},{10,8},{12,14},{14,12},{16,18},{18,... | collective-permute-start | bytes 1572872 | tf_op jit(solution)/shard_map/ppermute | solution.py:359
  28.6 0.0 copy-start.1
  28.6 10.6 %backward.1 = (bf16[4,512,128]{2,1,0:T(8,128)(2,1)}, bf16[256,1280]{1,0:T(8,128)(2,1)}, bf16[256,1280]{1,0:T(8,128)(2,1)}) custom-call(s32[24]{0:T(128)} %get-tuple-element.21.meta_ref, bf16[5,512,128]{2,1,0:T(8,128)(2,1)} %get-tuple-element.28.errb_ref, bf16[4,512,128]{2,1,0:T(8,128)(2,1)} %get-tuple-element.24.hid_in.hid_ref, ...), custom_call_target="tpu_custom_call" | custom-call | tf_op jit(solution)/shard_map/backward/pallas_call | solution.py:406
  39.1 0.0 copy-start
  39.1 0.0 collective-permute-start.4
  39.2 0.0 collective-permute-done.2
  39.2 0.0 copy-done.1
  39.2 0.2 add_convert_fusion.1
  39.4 1.6 %collective-permute-start.3 = (bf16[128,1024]{1,0:T(8,128)(2,1)S(1)}, bf16[128,1024]{1,0:T(8,128)(2,1)S(1)}, u32[]{:S(2)}, u32[]{:S(2)}) collective-permute-start(bf16[128,1024]{1,0:T(8,128)(2,1)S(1)} %slice.21), channel_id=1, source_target_pairs={{0,4},{2,6},{4,0},{6,2},{8,12},{10,14},{12,8},{14,10},{16,20},{18,... | collective-permute-start | bytes 786440 | tf_op jit(solution)/shard_map/ppermute | solution.py:359
  41.0 7.2 %collective-permute-done.3 = bf16[128,1024]{1,0:T(8,128)(2,1)S(1)} collective-permute-done((bf16[128,1024]{1,0:T(8,128)(2,1)S(1)}, bf16[128,1024]{1,0:T(8,128)(2,1)S(1)}, u32[]{:S(2)}, u32[]{:S(2)}) %collective-permute-start.3) | collective-permute-done | bytes 262176 | tf_op jit(solution)/shard_map/ppermute | solution.py:359
  48.2 0.8 add_convert_fusion.2
  48.9 5.0 %all-to-all-start = ((bf16[4,32,1024]{2,1,0:T(8,128)(2,1)}), bf16[4,32,1024]{2,1,0:T(8,128)(2,1)S(1)}, u32[]{:S(2)}, u32[]{:S(2)}) async-start(bf16[4,32,1024]{2,1,0:T(8,128)(2,1)} %bitcast.10), calls=%async_computation | async-start | bytes 524288 | tf_op jit(solution)/shard_map/all_to_all | solution.py:425
  53.9 0.0 collective-permute-done.4
  53.9 0.0 copy-done
  53.9 1.0 %add_convert_fusion = bf16[256,1280]{1,0:T(8,128)(2,1)} fusion(bf16[256,1280]{1,0:T(8,128)(2,1)S(1)} %collective-permute-done.4, bf16[256,1280]{1,0:T(8,128)(2,1)S(1)} %copy-done), kind=kLoop, calls=%fused_computation | loop fusion | flops 1310720 | bytes 1966080 | tf_op jit(solution)/shard_map/convert_element_type | solution.py:363
  54.9 7.5 %all-to-all-done = bf16[4,32,1024]{2,1,0:T(8,128)(2,1)S(1)} async-done(((bf16[4,32,1024]{2,1,0:T(8,128)(2,1)}), bf16[4,32,1024]{2,1,0:T(8,128)(2,1)S(1)}, u32[]{:S(2)}, u32[]{:S(2)}) %all-to-all-start) | async-done | bytes 262176 | tf_op jit(solution)/shard_map/all_to_all | solution.py:425
  62.4 3.5 %all-to-all-start.1 = ((bf16[8,32,1280]{2,1,0:T(8,128)(2,1)}), bf16[8,32,1280]{2,1,0:T(8,128)(2,1)S(1)}, u32[]{:S(2)}, u32[]{:S(2)}) async-start(bf16[8,32,1280]{2,1,0:T(8,128)(2,1)} %bitcast.11), calls=%async_computation.1 | async-start | bytes 1310720 | tf_op jit(solution)/shard_map/all_to_all | solution.py:426
  66.0 15.9 %all-to-all-done.1 = bf16[8,32,1280]{2,1,0:T(8,128)(2,1)S(1)} async-done(((bf16[8,32,1280]{2,1,0:T(8,128)(2,1)}), bf16[8,32,1280]{2,1,0:T(8,128)(2,1)S(1)}, u32[]{:S(2)}, u32[]{:S(2)}) %all-to-all-start.1) | async-done | bytes 655392 | tf_op jit(solution)/shard_map/all_to_all | solution.py:426
  81.9 0.1 reduce.1
  82.0 1.5 %collective-permute-start.5 = (bf16[32,2304]{1,0:T(8,128)(2,1)S(1)}, bf16[32,2304]{1,0:T(8,128)(2,1)S(1)}, u32[]{:S(2)}, u32[]{:S(2)}) collective-permute-start(bf16[32,2304]{1,0:T(8,128)(2,1)S(1)} %pad_maximum_fusion), channel_id=1, source_target_pairs={{0,1},{1,0},{2,3},{3,2},{4,5},{5,4},{6,7},{7,6},{8,9},{9,8},{10,11... | collective-permute-start | bytes 442376 | tf_op jit(solution)/shard_map/ppermute | solution.py:359
  83.5 3.8 %grads.1 = bf16[4,1024,128]{2,1,0:T(8,128)(2,1)} custom-call(bf16[512,1024]{1,0:T(8,128)(2,1)} %wr_ref.5, bf16[4,512,128]{2,1,0:T(8,128)(2,1)} %get-tuple-element.31.erra_ref, f32[4,1024,128]{2,1,0:T(8,128)} %get-tuple-element.32.back_ref), custom_call_target="tpu_custom_call" | custom-call | tf_op jit(solution)/shard_map/grads/pallas_call | solution.py:413
  87.3 0.0 collective-permute-done.5
  87.3 0.6 slice.23
  88.0 0.7 fusion
  (4 shorter events, 0.1 us)
Async XLA Ops:
  0.6 4.4 %copy-start.2 = (bf16[512,144]{0,1:T(8,128)(2,1)S(1)}, bf16[512,144]{0,1:T(8,128)(2,1)}, u32[]{:S(2)}) copy-start(bf16[512,144]{0,1:T(8,128)(2,1)} %param.16) | copy-start | bytes 442372
  3.8 8.3 %collective-permute-start = (bf16[48,1024]{1,0:T(8,128)(2,1)}, bf16[48,1024]{1,0:T(8,128)(2,1)S(1)}, u32[]{:S(2)}, u32[]{:S(2)}) collective-permute-start(bf16[48,1024]{1,0:T(8,128)(2,1)} %get-tuple-element.22), channel_id=1, source_target_pairs={{0,2},{2,0},{4,6},{6,4},{8,10},{10,8},{12,14},{14,12},{16,18},{18,... | collective-permute-start | bytes 294920 | tf_op jit(solution)/shard_map/ppermute | solution.py:359
  4.3 7.7 %collective-permute-start.1 = (bf16[48,1024]{1,0:T(8,128)(2,1)}, bf16[48,1024]{1,0:T(8,128)(2,1)S(1)}, u32[]{:S(2)}, u32[]{:S(2)}) collective-permute-start(bf16[48,1024]{1,0:T(8,128)(2,1)} %get-tuple-element.23), channel_id=1, source_target_pairs={{2,4},{6,8},{10,12},{14,16},{18,20},{22,24},{26,28},{4,2},{8,6},{1... | collective-permute-start | bytes 294920 | tf_op jit(solution)/shard_map/ppermute | solution.py:386
  12.1 0.6 copy-start.3
  12.1 0.7 copy-start.4
  24.7 14.5 %collective-permute-start.2 = (bf16[256,1024]{1,0:T(8,128)(2,1)}, bf16[256,1024]{1,0:T(8,128)(2,1)S(1)}, u32[]{:S(2)}, u32[]{:S(2)}) collective-permute-start(bf16[256,1024]{1,0:T(8,128)(2,1)} %get-tuple-element.34), channel_id=1, source_target_pairs={{0,2},{2,0},{4,6},{6,4},{8,10},{10,8},{12,14},{14,12},{16,18},{18,... | collective-permute-start | bytes 1572872 | tf_op jit(solution)/shard_map/ppermute | solution.py:359
  28.6 10.6 %copy-start.1 = (bf16[256,1024]{1,0:T(8,128)(2,1)S(1)}, bf16[256,1024]{1,0:T(8,128)(2,1)}, u32[]{:S(2)}) copy-start(bf16[256,1024]{1,0:T(8,128)(2,1)} %get-tuple-element.33) | copy-start | bytes 1572868
  39.1 14.8 %copy-start = (bf16[256,1280]{1,0:T(8,128)(2,1)S(1)}, bf16[256,1280]{1,0:T(8,128)(2,1)}, u32[]{:S(2)}) copy-start(bf16[256,1280]{1,0:T(8,128)(2,1)} %get-tuple-element.35) | copy-start | bytes 1966084
  39.1 14.8 %collective-permute-start.4 = (bf16[256,1280]{1,0:T(8,128)(2,1)}, bf16[256,1280]{1,0:T(8,128)(2,1)S(1)}, u32[]{:S(2)}, u32[]{:S(2)}) collective-permute-start(bf16[256,1280]{1,0:T(8,128)(2,1)} %get-tuple-element.36), channel_id=1, source_target_pairs={{0,2},{2,0},{4,6},{6,4},{8,10},{10,8},{12,14},{14,12},{16,18},{18,... | collective-permute-start | bytes 1966088 | tf_op jit(solution)/shard_map/ppermute | solution.py:359
  39.4 8.8 %collective-permute-start.3 = (bf16[128,1024]{1,0:T(8,128)(2,1)S(1)}, bf16[128,1024]{1,0:T(8,128)(2,1)S(1)}, u32[]{:S(2)}, u32[]{:S(2)}) collective-permute-start(bf16[128,1024]{1,0:T(8,128)(2,1)S(1)} %slice.21), channel_id=1, source_target_pairs={{0,4},{2,6},{4,0},{6,2},{8,12},{10,14},{12,8},{14,10},{16,20},{18,... | collective-permute-start | bytes 786440 | tf_op jit(solution)/shard_map/ppermute | solution.py:359
  48.9 13.5 %all-to-all-start = ((bf16[4,32,1024]{2,1,0:T(8,128)(2,1)}), bf16[4,32,1024]{2,1,0:T(8,128)(2,1)S(1)}, u32[]{:S(2)}, u32[]{:S(2)}) async-start(bf16[4,32,1024]{2,1,0:T(8,128)(2,1)} %bitcast.10), calls=%async_computation | async-start | bytes 524288 | tf_op jit(solution)/shard_map/all_to_all | solution.py:425
  62.4 19.5 %all-to-all-start.1 = ((bf16[8,32,1280]{2,1,0:T(8,128)(2,1)}), bf16[8,32,1280]{2,1,0:T(8,128)(2,1)S(1)}, u32[]{:S(2)}, u32[]{:S(2)}) async-start(bf16[8,32,1280]{2,1,0:T(8,128)(2,1)} %bitcast.11), calls=%async_computation.1 | async-start | bytes 1310720 | tf_op jit(solution)/shard_map/all_to_all | solution.py:426
  82.0 5.3 %collective-permute-start.5 = (bf16[32,2304]{1,0:T(8,128)(2,1)S(1)}, bf16[32,2304]{1,0:T(8,128)(2,1)S(1)}, u32[]{:S(2)}, u32[]{:S(2)}) collective-permute-start(bf16[32,2304]{1,0:T(8,128)(2,1)S(1)} %pad_maximum_fusion), channel_id=1, source_target_pairs={{0,1},{1,0},{2,3},{3,2},{4,5},{5,4},{6,7},{7,6},{8,9},{9,8},{10,11... | collective-permute-start | bytes 442376 | tf_op jit(solution)/shard_map/ppermute | solution.py:359

commit v2 on v1

--- a/solution.py
+++ b/solution.py
@@ -22,7 +22,6 @@
 LIVE_DEV = 2
 BF = jnp.bfloat16
 F32 = jnp.float32
-VMEM_LIMIT = 56 * 1024 * 1024
 
 HELD, L_LINK, R_LINK, L_IDX, R_IDX, META = 0, 1, 6, 11, 16, 24
 
@@ -66,8 +65,23 @@
     return lambda row: row * TW + col
 
 
-def edge_kernel(count_ref, joined_ref, x_any, g_any, core_ref, other_ref, meta_ref, xbuf, gbuf, sems):
+def edge_kernel(
+    count_hbm, joined_hbm, x_any, g_any, core_ref, other_ref, meta_ref,
+    count_ref, joined_ref, xbuf, gbuf, sems,
+):
     me = lax.axis_index("tile")
+    tables = [
+        pltpu.make_async_copy(count_hbm, count_ref, sems.at[4]),
+        pltpu.make_async_copy(joined_hbm, joined_ref, sems.at[5]),
+    ]
+    firsts = [
+        pltpu.make_async_copy(x_any.at[0], xbuf.at[0], sems.at[0]),
+        pltpu.make_async_copy(g_any.at[0], gbuf.at[0], sems.at[1]),
+    ]
+    for copy in tables + firsts:
+        copy.start()
+    for copy in tables:
+        copy.wait()
     devices = count_ref.shape[1]
     links = joined_ref.shape[1]
     start = jnp.int32(0)
@@ -76,13 +90,12 @@
         start = start + jnp.where(e < me, count_ref[0, e], 0)
         held = held + jnp.where(e == me, count_ref[0, e], 0)
     last = held - 1
-    copies = []
-    for k, (src, dst, slot) in enumerate(
-        ((x_any, xbuf, 0), (g_any, gbuf, 0), (x_any, xbuf, last), (g_any, gbuf, last))
-    ):
-        copy = pltpu.make_async_copy(src.at[slot], dst.at[k // 2], sems.at[k])
+    lasts = [
+        pltpu.make_async_copy(x_any.at[last], xbuf.at[1], sems.at[2]),
+        pltpu.make_async_copy(g_any.at[last], gbuf.at[1], sems.at[3]),
+    ]
+    for copy in lasts:
         copy.start()
-        copies.append(copy)
 
     def link(at):
         inside = jnp.logical_and(at >= 0, at < links)
@@ -102,7 +115,7 @@
     meta_ref[L_IDX + SLOTS] = last
     meta_ref[R_IDX + SLOTS] = jnp.int32(0)
 
-    for copy in copies:
+    for copy in firsts + lasts:
         copy.wait()
     even = me % 2 == 0
 
@@ -151,7 +164,7 @@
     tap_row = lax.broadcasted_iota(jnp.int32, (TAPS * GW, KDIM), 0)
     lane = lax.broadcasted_iota(jnp.int32, (TAPS * GW, KDIM), 1)
     pick = (tap_row == (lane // HALF) * GW + lane % GW).astype(F32).astype(BF)
-    spread = nn_dot(wg_ref[...], pick)
+    spread = tn_dot(wg_ref[...], pick)
     row = lax.broadcasted_iota(jnp.int32, (MID, KDIM), 0)
     col = lax.broadcasted_iota(jnp.int32, (MID, KDIM), 1)
     keep = (row % HALF) // GW == (col % HALF) // GW
@@ -163,7 +176,7 @@
     pcol = lax.broadcasted_iota(jnp.int32, (HALF, TAPS * GW), 1)
     for k in range(TAPS):
         pick_t = (pcol == k * GW + prow % GW).astype(F32).astype(BF)
-        spread_t = jnp.where(keep_t, nt_dot(pick_t, wg_ref[...]), 0.0).astype(BF)
+        spread_t = jnp.where(keep_t, nn_dot(pick_t, wg_ref[...]), 0.0).astype(BF)
         for b in range(2):
             denset_ref[b, :, k * HALF : (k + 1) * HALF] = spread_t[:, b * HALF : (b + 1) * HALF]
     wet_ref[...] = jnp.transpose(we_ref[...])
@@ -176,7 +189,7 @@
     last_col = col == TW - 1
     has_above = lane >= TW
     has_below = lane < PIX - TW
-    for i in range(tiles):
+    for i in tiles:
         left_at = meta_ref[L_IDX + i]
         right_at = meta_ref[R_IDX + i]
         left_link = meta_ref[L_LINK + i].astype(F32)
@@ -199,17 +212,24 @@
                     win_ref[b, pl.ds(tap * HALF, HALF), lanes] = shifted.astype(BF)
 
 
+CHUNKS = ((0, 2), (2, 2), (4, 1))
+
+
 def forward_kernel(
     devices, meta_ref, core_ref, other_ref, hid_in, wr_ref, s1_ref, b1_ref, dense_ref,
-    s2_ref, b2_ref, wet_ref, we_ref, s3_ref, b3_ref, x_ref, g_ref,
-    out_ref, back_ref, errb_ref, send_ref, keep_ref,
-    hid_ref, win_ref, hidb_ref, slopeb_ref, errc_ref,
+    s2_ref, b2_ref, wet_ref, s3_ref, b3_ref, x_ref, g_ref,
+    out_ref, back_ref, errc_ref, slopeb_ref, send_ref, keep_ref,
+    hid_ref, win_ref, hidb_ref,
 ):
     me = lax.axis_index("tile")
     held = meta_ref[HELD]
     odd = me % 2
     scale1 = column(s1_ref)
     shift1 = column(b1_ref)
+    scale2 = column(s2_ref)
+    shift2 = column(b2_ref)
+    scale3 = column(s3_ref)
+    shift3 = column(b3_ref)
     core_first = jnp.where(odd == 0, 0, TW - 2)
     other_first = jnp.where(odd == 0, TW - 2, 0)
     core_g = jnp.where(odd == 0, 0, TW - 1)
@@ -227,24 +247,20 @@
     pre = nn_dot(wr_ref[...], edge_x) * scale1 + shift1
     hid_ref[SLOTS] = (pre * sigmoid(pre)).astype(BF)
 
-    build_windows(hid_ref, win_ref, meta_ref, SLOTS + 1, False)
-
-    scale2 = column(s2_ref)
-    shift2 = column(b2_ref)
-    for b in range(2):
-        conv = nn_dot(dense_ref[b], win_ref[b])
-        rows = slice(b * HALF, (b + 1) * HALF)
-        for i in range(SLOTS + 1):
-            v = conv[:, i * PIX : (i + 1) * PIX] * scale2[rows] + shift2[rows]
-            sig = sigmoid(v)
-            act = v * sig
-            hidb_ref[rows, i * PIX : (i + 1) * PIX] = act.astype(BF)
-            slopeb_ref[rows, i * PIX : (i + 1) * PIX] = (sig + act * (1.0 - sig)) * scale2[rows]
-
-    scale3 = column(s3_ref)
-    shift3 = column(b3_ref)
-    for first, count in ((0, 2), (2, 2), (4, 1)):
-        grown = nn_dot(wet_ref[...], hidb_ref[:, first * PIX : (first + count) * PIX])
+    for first, count in CHUNKS:
+        build_windows(hid_ref, win_ref, meta_ref, range(first, first + count), False)
+        lanes = slice(first * PIX, (first + count) * PIX)
+        for b in range(2):
+            conv = nn_dot(dense_ref[b], win_ref[b, :, lanes])
+            rows = slice(b * HALF, (b + 1) * HALF)
+            for k in range(count):
+                at = slice((first + k) * PIX, (first + k + 1) * PIX)
+                v = conv[:, k * PIX : (k + 1) * PIX] * scale2[rows] + shift2[rows]
+                sig = sigmoid(v)
+                act = v * sig
+                hidb_ref[rows, at] = act.astype(BF)
+                slopeb_ref[rows, at] = (sig + act * (1.0 - sig)) * scale2[rows]
+        grown = nn_dot(wet_ref[...], hidb_ref[:, lanes])
         for k in range(count):
             i = first + k
             if i < SLOTS:
@@ -264,9 +280,27 @@
                 back_ref[i] = back
             errc_ref[:, i * PIX : (i + 1) * PIX] = (back * scale3).astype(BF)
 
-    order_rows(devices, me, hidb_ref, errc_ref, SLOTS * PIX, send_ref, keep_ref)
-
-    for first, count in ((0, 2), (2, 2), (4, 1)):
+    own = SLOTS * PIX
+    for ref, flip in ((send_ref, 1), (keep_ref, 0)):
+        rows = jnp.concatenate([hidb_ref[at, :own] for at in row_blocks(devices, me, flip)], axis=0)
+        ref[...] = nt_dot(rows, errc_ref[:, :own]).astype(BF)
+
+
+def row_blocks(devices, me, flip):
+    per = MID // devices
+    bits = (devices // 2).bit_length() - 1
+    blocks = []
+    for j in range(devices // 2):
+        distance = flip
+        for bit in range(bits):
+            distance |= ((j >> (bits - 1 - bit)) & 1) << (bit + 1)
+        at = pl.multiple_of((me ^ distance) * per, per)
+        blocks.append(pl.ds(at, per))
+    return blocks
+
+
+def pull_kernel(we_ref, errc_ref, slopeb_ref, errb_ref):
+    for first, count in CHUNKS:
         lanes = slice(first * PIX, (first + count) * PIX)
         pulled = nn_dot(we_ref[...], errc_ref[:, lanes])
         errb = (pulled * slopeb_ref[:, lanes]).astype(BF)
@@ -274,32 +308,23 @@
             errb_ref[first + k] = errb[:, k * PIX : (k + 1) * PIX]
 
 
-def order_rows(devices, me, left_ref, right_ref, lanes, send_ref, keep_ref):
-    per = MID // devices
-    for ref, flip in ((send_ref, 1), (keep_ref, 0)):
-        picked = []
-        for pair in range(devices // 2):
-            dy, rest = pair // (devices // 4), pair % (devices // 4)
-            target = (rest * 4) + (((me // 2) % 2) ^ dy) * 2 + ((me % 2) ^ flip)
-            at = pl.multiple_of(target * per, per)
-            picked.append(left_ref[pl.ds(at, per), :lanes])
-        rows = jnp.concatenate(picked, axis=0)
-        ref[...] = nt_dot(rows, right_ref[:, :lanes]).astype(BF)
-
-
 def backward_kernel(
     devices, meta_ref, errb_ref, hid_ref, slope_ref, denset_ref, x_ref,
     erra_ref, send_ref, keep_ref, win_ref, flat_ref, groups_ref,
 ):
     me = lax.axis_index("tile")
-    build_windows(errb_ref, win_ref, meta_ref, SLOTS, True)
-    for b in range(2):
-        conv = nn_dot(denset_ref[b], win_ref[b])
-        rows = slice(b * HALF, (b + 1) * HALF)
-        for i in range(SLOTS):
-            err = (conv[:, i * PIX : (i + 1) * PIX] * slope_ref[i, rows, :]).astype(BF)
-            flat_ref[rows, i * PIX : (i + 1) * PIX] = err
-            erra_ref[i, rows, :] = err
+    side = lax.axis_index("slide") % 2
+    for first, count in CHUNKS[:2]:
+        build_windows(errb_ref, win_ref, meta_ref, range(first, first + count), True)
+        lanes = slice(first * PIX, (first + count) * PIX)
+        for b in range(2):
+            conv = nn_dot(denset_ref[b], win_ref[b, :, lanes])
+            rows = slice(b * HALF, (b + 1) * HALF)
+            for k in range(count):
+                i = first + k
+                err = (conv[:, k * PIX : (k + 1) * PIX] * slope_ref[i, rows, :]).astype(BF)
+                flat_ref[rows, i * PIX : (i + 1) * PIX] = err
+                erra_ref[i, rows, :] = err
     row = lax.broadcasted_iota(jnp.int32, (HALF, HALF), 0)
     col = lax.broadcasted_iota(jnp.int32, (HALF, HALF), 1)
     same = row // GW == col // GW
@@ -313,17 +338,19 @@
             place = (col == k * GW + row % GW).astype(F32).astype(BF)
             folded = folded + nn_dot(kept, place)
         groups_ref[rows, :] = folded.astype(BF)
-    tiles = jnp.concatenate([x_ref[i] for i in range(SLOTS)], axis=1)
-    per = MID // devices
+    width = CIN // 2
+    tiles = [
+        jnp.concatenate([x_ref[i, pl.ds(pl.multiple_of((side ^ dx) * width, width), width), :] for i in range(SLOTS)], axis=1)
+        for dx in range(2)
+    ]
     for ref, flip in ((send_ref, 1), (keep_ref, 0)):
-        picked, group_rows = [], []
-        for pair in range(devices // 2):
-            target = pair * 2 + ((me % 2) ^ flip)
-            at = pl.multiple_of(target * per, per)
-            picked.append(flat_ref[pl.ds(at, per), :])
-            ref[pl.ds(pair * per, per), CIN:] = groups_ref[pl.ds(at, per), :]
-        rows = jnp.concatenate(picked, axis=0)
-        ref[:, :CIN] = nt_dot(rows, tiles).astype(BF)
+        blocks = row_blocks(devices, me, flip)
+        rows = jnp.concatenate([flat_ref[at, :] for at in blocks], axis=0)
+        group_rows = jnp.concatenate([groups_ref[at, :] for at in blocks], axis=0)
+        low, high = group_rows[:, :PIX], group_rows[:, PIX:]
+        for dx in range(2):
+            ref[dx, :, :width] = nt_dot(rows, tiles[dx]).astype(BF)
+            ref[dx, :, width:] = jnp.where(side == dx, low, high)
 
 
 def grad_kernel(wr_ref, erra_ref, back_ref, grad_ref):
@@ -335,10 +362,28 @@
             grad_ref[i] = (pulled[:, k * PIX : (k + 1) * PIX] + back_ref[i]).astype(BF)
 
 
+def finish_kernel(norm, e_ref, r_ref, got_ref, reduce_ref, group_ref, expand_ref):
+    width = CIN // 2
+    own = r_ref[...].astype(F32) * norm
+    other = got_ref[:, CIN:].astype(F32) * norm
+    expand_ref[...] = (e_ref[...].astype(F32) + got_ref[:, :CIN].astype(F32)) * norm
+    even = lax.axis_index("slide") % 2 == 0
+    low = jnp.where(even, own, other)
+    high = jnp.where(even, other, own)
+    reduce_ref[:, :width] = low[:, :width]
+    reduce_ref[:, width:] = high[:, :width]
+    group_ref[:, :PIX] = low[:, width:]
+    group_ref[:, PIX:] = high[:, width : width + TAPS * GW - PIX]
+
+
+LIMITS = {"edges": 3, "prep": 13, "forward": 26, "pull": 6, "backward": 16, "grads": 6, "finish": 2}
+WORK = {"edges": 2, "prep": 3, "forward": 7, "pull": 1.5, "backward": 8, "grads": 2, "finish": 1}
+
+
 def call(body, name, out_shape, in_smem, in_any, n_in, scratch=(), out_smem=()):
     vmem = pl.BlockSpec(memory_space=pltpu.VMEM)
     smem = pl.BlockSpec(memory_space=pltpu.SMEM)
-    anys = pl.BlockSpec(memory_space=pl.ANY)
+    anys = pl.BlockSpec(memory_space=pltpu.HBM)
     return pl.pallas_call(
         body,
         name=name,
@@ -346,7 +391,8 @@
         in_specs=[smem if i in in_smem else anys if i in in_any else vmem for i in range(n_in)],
         out_specs=[smem if i in out_smem else vmem for i in range(len(out_shape))],
         scratch_shapes=list(scratch),
-        compiler_params=pltpu.CompilerParams(vmem_limit_bytes=VMEM_LIMIT),
+        compiler_params=pltpu.CompilerParams(vmem_limit_bytes=LIMITS[name] * 1024 * 1024),
+        cost_estimate=pl.CostEstimate(flops=int(WORK[name] * 1.1e9), bytes_accessed=1 << 20, transcendentals=0),
     )
 
 
@@ -359,8 +405,29 @@
     return lax.ppermute(value, axis, [(i, i ^ mask) for i in range(size)])
 
 
+def cross(value, devices, slides, tile_mask, slide_mask):
+    pairs = [
+        (t * slides + k, (t ^ tile_mask) * slides + (k ^ slide_mask))
+        for t in range(devices)
+        for k in range(slides)
+    ]
+    return lax.ppermute(value, ("tile", "slide"), pairs)
+
+
+def add_all(first, *others):
+    total = first.astype(F32)
+    for other in others:
+        total = total + other.astype(F32)
+    return total.astype(BF)
+
+
 def add_pair(a, b):
-    return (a.astype(F32) + b.astype(F32)).astype(BF)
+    return add_all(a, b)
+
+
+def halve(part, mask):
+    rows = part.shape[0] // 2
+    return add_pair(part[:rows], swap(part[rows:], "tile", mask))
 
 
 def shards(
@@ -377,35 +444,40 @@
     to_core, to_other, meta = call(
         edge_kernel, "edges",
         [shape((PAY, CIN), BF), shape((PAY, CIN), BF), shape((META,), jnp.int32)],
-        (0, 1), (2, 3), 4,
-        [pltpu.VMEM((2, CIN, PIX), BF), pltpu.VMEM((2, CIN, PIX), BF), pltpu.SemaphoreType.DMA((4,))],
+        (), (0, 1, 2, 3), 4,
+        [pltpu.SMEM(tile_count.shape, jnp.int32), pltpu.SMEM(joined.shape, jnp.int32),
+         pltpu.VMEM((2, CIN, PIX), BF), pltpu.VMEM((2, CIN, PIX), BF), pltpu.SemaphoreType.DMA((6,))],
         (2,),
     )(tile_count, joined, x, g)
-    from_core = swap(to_core, "tile", 1)
     hops = [(i, i + 1) for i in range(1, devices - 1, 2)]
     from_other = lax.ppermute(to_other, "tile", hops + [(b, a) for a, b in hops])
+    from_core = swap(to_core, "tile", 1)
 
     hid, slope_a, dense, denset, wet = call(
         prep_kernel, "prep",
         [shape((SLOTS, MID, PIX), BF), shape((SLOTS, MID, PIX), F32), shape((2, HALF, KDIM), BF),
          shape((2, HALF, KDIM), BF), shape((CIN, MID), BF)],
         (0,), (), 7,
-    )(meta, x, w_reduce, w_expand, w_group, s1, b1)
-
-    out, back, errb, e_send, e_keep = call(
+    )(meta, x, w_reduce, w_expand, w_group.T, s1, b1)
+
+    lanes = (SLOTS + 1) * PIX
+    out, back, errc, slope_b, e_send, e_keep = call(
         functools.partial(forward_kernel, devices), "forward",
-        [shape((SLOTS, CIN, PIX), BF), shape((SLOTS, CIN, PIX), F32), shape((SLOTS + 1, MID, PIX), BF),
-         shape((HALF, CIN), BF), shape((HALF, CIN), BF)],
-        (0,), (), 16,
-        [pltpu.VMEM((SLOTS + 1, MID, PIX), BF), pltpu.VMEM((2, KDIM, (SLOTS + 1) * PIX), BF),
-         pltpu.VMEM((MID, (SLOTS + 1) * PIX), BF), pltpu.VMEM((MID, (SLOTS + 1) * PIX), F32),
-         pltpu.VMEM((CIN, (SLOTS + 1) * PIX), BF)],
-    )(meta, from_core, from_other, hid, w_reduce, s1, b1, dense, s2, b2, wet, w_expand, s3, b3, x, g)
+        [shape((SLOTS, CIN, PIX), BF), shape((SLOTS, CIN, PIX), F32), shape((CIN, lanes), BF),
+         shape((MID, lanes), F32), shape((HALF, CIN), BF), shape((HALF, CIN), BF)],
+        (0,), (), 15,
+        [pltpu.VMEM((SLOTS + 1, MID, PIX), BF), pltpu.VMEM((2, KDIM, lanes), BF), pltpu.VMEM((MID, lanes), BF)],
+    )(meta, from_core, from_other, hid, w_reduce, s1, b1, dense, s2, b2, wet, s3, b3, x, g)
 
     e_core = swap(e_send, "tile", 1)
+    (errb,) = call(pull_kernel, "pull", [shape((SLOTS + 1, MID, PIX), BF)], (), (), 3)(w_expand, errc, slope_b)
+    e_part = add_pair(e_keep, e_core)
+    errb, e_part = lax.optimization_barrier((errb, e_part))
+    e_part = halve(e_part, 2)
+
     erra, r_send, r_keep = call(
         functools.partial(backward_kernel, devices), "backward",
-        [shape((SLOTS, MID, PIX), BF), shape((HALF, CIN + HALF), BF), shape((HALF, CIN + HALF), BF)],
+        [shape((SLOTS, MID, PIX), BF), shape((2, HALF, CIN // 2 + PIX), BF), shape((2, HALF, CIN // 2 + PIX), BF)],
         (0,), (), 6,
         [pltpu.VMEM((2, KDIM, SLOTS * PIX), BF), pltpu.VMEM((MID, SLOTS * PIX), BF), pltpu.VMEM((MID, HALF), BF)],
     )(meta, errb, hid, slope_a, denset, x)
@@ -414,28 +486,31 @@
         grad_kernel, "grads", [shape((SLOTS, CIN, PIX), BF)], (), (), 3,
     )(w_reduce, erra, back)
 
+    r_core = swap(r_send, "tile", 1)
+    r_part = add_pair(r_keep, r_core)
     quarter = HALF // 2
-    e_half = add_pair(e_keep, e_core)
-    e_y = swap(e_half[quarter:], "tile", 2)
-    e_quarter = add_pair(e_half[:quarter], e_y)
-    r_core = swap(r_send, "tile", 1)
-    r_half = add_pair(r_keep, r_core)
-    groups4 = [[low + 4 * k for k in range(devices // 4)] for low in range(4)]
-    groups2 = [[low + 2 * k for k in range(devices // 2)] for low in range(2)]
-    e_all = lax.all_to_all(e_quarter, "tile", 0, 0, axis_index_groups=groups4, tiled=True)
-    r_all = lax.all_to_all(r_half, "tile", 0, 0, axis_index_groups=groups2, tiled=True)
-    e_sum = jnp.sum(e_all.reshape(devices // 4, per, CIN).astype(F32), 0)
-    r_sum = jnp.sum(r_all.reshape(devices // 2, per, CIN + HALF).astype(F32), 0)
-    total = jnp.concatenate([e_sum, r_sum], axis=1).astype(BF)
-    mask = 1
+    r_part = add_all(
+        r_part[0, :quarter],
+        cross(r_part[0, quarter:], devices, slides, 2, 0),
+        cross(r_part[1, :quarter], devices, slides, 0, 1),
+        cross(r_part[1, quarter:], devices, slides, 2, 1),
+    )
+    mask = 4
+    while mask < devices:
+        e_part = halve(e_part, mask)
+        r_part = halve(r_part, mask)
+        mask *= 2
+    mask = 2
     while mask < slides:
-        total = total.astype(F32) + swap(total.astype(BF), "slide", mask).astype(F32)
+        e_part = add_pair(e_part, swap(e_part, "slide", mask))
+        r_part = add_pair(r_part, swap(r_part, "slide", mask))
         mask *= 2
+    got = swap(jnp.concatenate([e_part, r_part], axis=1), "slide", 1)
     norm = 1.0 / math.sqrt(slides * LIVE_DEV * devices * PIX)
-    total = total.astype(F32) * norm
-    grad_expand = total[:, :CIN]
-    grad_reduce = total[:, CIN : 2 * CIN]
-    grad_group = total[:, 2 * CIN : 2 * CIN + TAPS * GW]
+    grad_reduce, grad_group, grad_expand = call(
+        functools.partial(finish_kernel, norm), "finish",
+        [shape((per, CIN), F32), shape((per, TAPS * GW), F32), shape((per, CIN), F32)], (), (), 3,
+    )(e_part, r_part, got)
     return (out[None], grad_in[None], grad_reduce, grad_group, grad_expand)
 
 

time: 89 us -> 65 us (0.73)
  waiting for transfers between devices: 30.6 us -> 12.6 us
  Pallas kernels: 35.7 us -> 24 us
  starting transfers between devices: 16.7 us -> 22.7 us
  other arithmetic: 2.14 us -> 0.6 us
  local copies, waits for them, and re-layouts: 2.86 us -> 3.9 us
    all_to_all x2 -> x0, waiting for transfers between devices: 23.4 us -> none  [the longest x1 15.9 us: shards(): lax.all_to_all(r_half, 'tile', 0, 0, axis_index_groups=groups2, tiled=True)]
    ppermute x5 -> x9, starting transfers between devices: 7.51 us -> 18.5 us  [swap(): return lax.ppermute(value, axis, [(i, i ^ mask) for i in range(size)])]
    all_to_all x2 -> x0, starting transfers between devices: 8.52 us -> none  [the longest x1 4.98 us: shards(): lax.all_to_all(e_quarter, 'tile', 0, 0, axis_index_groups=groups4, tiled=...]
    ppermute x5 -> x9, waiting for transfers between devices: 7.19 us -> 12 us  [swap(): return lax.ppermute(value, axis, [(i, i ^ mask) for i in range(size)])]
    pallas_call x1, Pallas kernels: 11.9 us -> 8.28 us  [shards(): call(functools.partial(forward_kernel, devices), 'forward', [shape((SLOTS...]
    ppermute x0 -> x3, starting transfers between devices: none -> 3.55 us  [cross(): return lax.ppermute(value, ('tile', 'slide'), pairs)]
    pallas_call x1, Pallas kernels: 6.22 us -> 2.89 us  [shards(): call(prep_kernel, 'prep', [shape((SLOTS, MID, PIX), BF), shape((SLOTS, MI...]
    pallas_call x1, Pallas kernels: 10.6 us -> 7.62 us  [shards(): call(functools.partial(backward_kernel, devices), 'backward', [shape((SLO...]
  transfers between devices with their start and end apart: 8 -> 13, of which waited for: 3 -> 7; matrix products, arithmetic and copies ran while one was open for 3% -> 1% of each run, Pallas kernels for 23% -> 9%
where the time goes in v2:
time: 65 us; the launch traced here: 64.7 us
  Pallas kernels  24 us (37%)
  starting transfers between devices  22.7 us (35%)
  waiting for transfers between devices  12.6 us (19%)
  local copies, waits for them, and re-layouts  3.9 us (6%)
  between operations  0.95 us (1%)
    ppermute x9, starting transfers between devices, swap(): return lax.ppermute(value, axis, [(i, i ^ mask) for i in range(size)])  18.5 us
    ppermute x9, waiting for transfers between devices, swap(): return lax.ppermute(value, axis, [(i, i ^ mask) for i in range(size)])  12 us
    pallas_call x1, Pallas kernels, shards(): call(functools.partial(forward_kernel, devices), 'forward', [shape((SLOTS...  8.28 us
    pallas_call x1, Pallas kernels, shards(): call(functools.partial(backward_kernel, devices), 'backward', [shape((SLO...  7.62 us
    unnamed x30, local copies, waits for them, and re-layouts  3.81 us
    ppermute x3, starting transfers between devices, cross(): return lax.ppermute(value, ('tile', 'slide'), pairs)  3.55 us
    pallas_call x1, Pallas kernels, shards(): call(prep_kernel, 'prep', [shape((SLOTS, MID, PIX), BF), shape((SLOTS, MI...  2.89 us
    pallas_call x1, Pallas kernels, shards(): call(edge_kernel, 'edges', [shape((PAY, CIN), BF), shape((PAY, CIN), BF),...  1.74 us
  transfers between devices with their start and end apart: 13, of which 7 were waited for; matrix products, arithmetic and copies ran while one was open for 1% of the time, Pallas kernels for 9%

profile of v2, /device:TPU:0, one launch (start us, length us, event | category | flops | bytes accessed | tf_op | source)
XLA Modules:
  0.0 64.7 jit_solution(9741279670772020256)
XLA Ops:
  0.6 0.0 copy-start
  0.6 1.2 %copy-done = bf16[1,4,1024,128]{3,2,1,0:T(8,128)(2,1)S(1)} copy-done((bf16[1,4,1024,128]{3,2,1,0:T(8,128)(2,1)S(1)}, bf16[1,4,1024,128]{3,2,1,0:T(8,128)(2,1)}, u32[]{:S(2)}) %copy-start) | copy-done | bytes 1048600
  1.9 0.0 copy-start.3
  1.9 1.2 %copy-done.3 = bf16[1,4,1024,128]{3,2,1,0:T(8,128)(2,1)S(1)} copy-done((bf16[1,4,1024,128]{3,2,1,0:T(8,128)(2,1)S(1)}, bf16[1,4,1024,128]{3,2,1,0:T(8,128)(2,1)}, u32[]{:S(2)}) %copy-start.3) | copy-done | bytes 1048600
  3.1 0.0 copy-start.13
  3.1 0.7 %copy-done.13 = s32[1,16]{1,0:T(1,128)S(1)} copy-done((s32[1,16]{1,0:T(1,128)S(1)}, s32[1,16]{1,0:T(1,128)}, u32[]{:S(2)}) %copy-start.13) | copy-done | bytes 88
  3.7 0.0 copy-start.14
  3.7 0.7 %copy-done.14 = s32[1,31]{1,0:T(1,128)S(1)} copy-done((s32[1,31]{1,0:T(1,128)S(1)}, s32[1,31]{1,0:T(1,128)}, u32[]{:S(2)}) %copy-start.14) | copy-done | bytes 148
  4.4 0.0 copy-start.2
  4.4 0.0 copy-start.9
  4.4 0.0 copy-start.10
  4.4 1.7 %edges.1 = (bf16[48,1024]{1,0:T(8,128)(2,1)S(1)}, bf16[48,1024]{1,0:T(8,128)(2,1)S(1)}, s32[24]{0:T(128)S(1)}) custom-call(s32[1,16]{1,0:T(1,128)S(1)} %copy-done.13, s32[1,31]{1,0:T(1,128)S(1)} %copy-done.14, bf16[4,1024,128]{2,1,0:T(8,128)(2,1)S(1)} %bitcast.24, bf16[4,1024,128]{2,1,0:T(8,128)(2,1)S(1)} %bitcast.22), custom_call_target="tpu_custom_call" | custom-call | flops 2200000000 | bytes 1048576 | tf_op jit(solution)/shard_map/edges/pallas_call | solution.py:444
  6.2 0.5 collective-permute-start
  6.7 0.7 %collective-permute-start.1 = (bf16[48,1024]{1,0:T(8,128)(2,1)S(1)}, bf16[48,1024]{1,0:T(8,128)(2,1)S(1)}, u32[]{:S(2)}, u32[]{:S(2)}) collective-permute-start(bf16[48,1024]{1,0:T(8,128)(2,1)S(1)} %get-tuple-element.29), channel_id=1, source_target_pairs={{2,4},{6,8},{10,12},{14,16},{18,20},{22,24},{26,28},{4,2},{8,6},{1... | collective-permute-start | bytes 294920 | tf_op jit(solution)/shard_map/ppermute | solution.py:453
  7.4 0.0 copy-done.2
  7.4 0.0 copy-done.4
  7.4 0.0 copy-done.5
  7.4 0.0 copy-done.6
  7.4 0.0 copy-done.9
  7.4 0.0 copy-done.10
  7.4 0.0 copy-start.1
  7.4 0.0 copy-start.7
  7.5 0.0 copy-start.8
  7.5 0.0 copy-start.11
  7.5 0.0 copy-start.12
  7.5 2.9 %prep.1 = (bf16[4,512,128]{2,1,0:T(8,128)(2,1)S(1)}, f32[4,512,128]{2,1,0:T(8,128)S(1)}, bf16[2,256,2304]{2,1,0:T(8,128)(2,1)S(1)}, bf16[2,256,2304]{2,1,0:T(8,128)(2,1)S(1)}, bf16[1024,512]{1,0:T(8,128)(2,1)S(1)}) custom-call(s32[24]{0:T(128)S(1)} %get-tuple-element.27.meta_ref, bf16[4,1024,128]{2,1,0:T(8,128)(2,1)S(1)} %bitcast.25, ...), custom_call_target="tpu_custom_call" | custom-call | flops 3300000000 | bytes 1048576 | tf_op jit(solution)/shard_map/prep/pallas_call | solution.py:456
  10.4 0.0 collective-permute-done.core_ref
  10.4 0.0 collective-permute-done.1.other_ref
  10.4 0.0 copy-done.1
  10.4 0.0 copy-done.7
  10.4 0.0 copy-done.8
  10.4 0.0 copy-done.11
  10.4 0.0 copy-done.12
  10.5 8.3 %forward.1 = (bf16[4,1024,128]{2,1,0:T(8,128)(2,1)}, f32[4,1024,128]{2,1,0:T(8,128)S(1)}, bf16[1024,640]{1,0:T(8,128)(2,1)S(1)}, f32[512,640]{1,0:T(8,128)S(1)},...) custom-call(s32[24]{0:T(128)S(1)} %get-tuple-element.27.meta_ref, ...), custom_call_target="tpu_custom_call" | custom-call | flops 7699999744 | bytes 1048576 | tf_op jit(solution)/shard_map/forward/pallas_call | solution.py:464
  18.7 3.9 %collective-permute-start.2 = (bf16[256,1024]{1,0:T(8,128)(2,1)S(1)}, bf16[256,1024]{1,0:T(8,128)(2,1)S(1)}, u32[]{:S(2)}, u32[]{:S(2)}) collective-permute-start(bf16[256,1024]{1,0:T(8,128)(2,1)S(1)} %get-tuple-element.37), channel_id=1, source_target_pairs={{0,2},{2,0},{4,6},{6,4},{8,10},{10,8},{12,14},{14,12},{16,18},{18,... | collective-permute-start | bytes 1572872 | tf_op jit(solution)/shard_map/ppermute | solution.py:405
  22.6 1.0 %pull.1.errb_ref = bf16[5,512,128]{2,1,0:T(8,128)(2,1)S(1)} custom-call(bf16[512,1024]{1,0:T(8,128)(2,1)S(1)} %copy-done.2, bf16[1024,640]{1,0:T(8,128)(2,1)S(1)} %get-tuple-element.34.errc_ref, f32[512,640]{1,0:T(8,128)S(1)} %get-tuple-element.35.slopeb_ref), custom_call_target="tpu_custom_call" | custom-call | flops 1650000000 | bytes 1048576 | tf_op jit(solution)/shard_map/pull/pallas_call | solution.py:473
  23.6 0.6 collective-permute-done.2
  24.1 0.2 add_convert_fusion.1
  24.3 7.6 %backward.1 = (bf16[4,512,128]{2,1,0:T(8,128)(2,1)S(1)}, bf16[2,256,640]{2,1,0:T(8,128)(2,1)S(1)}, bf16[2,256,640]{2,1,0:T(8,128)(2,1)S(1)}) custom-call(s32[24]{0:T(128)S(1)} %get-tuple-element.27.meta_ref, bf16[5,512,128]{2,1,0:T(8,128)(2,1)S(1)} %pull.1.errb_ref, bf16[4,512,128]{2,1,0:T(8,128)(2,1)S(1)} %get-tuple-element.30.hid_in.hid_ref, ...), custom_call_target="tpu_custom_call" | custom-call | flops 8800000000 | bytes 1048576 | tf_op jit(solution)/shard_map/backward/pallas_call | solution.py:478
  32.0 0.4 collective-permute-start.6
  32.4 2.3 %collective-permute-start.3 = (bf16[128,1024]{1,0:T(8,128)(2,1)S(1)}, bf16[128,1024]{1,0:T(8,128)(2,1)S(1)}, u32[]{:S(2)}, u32[]{:S(2)}) collective-permute-start(bf16[128,1024]{1,0:T(8,128)(2,1)S(1)} %slice.43), channel_id=1, source_target_pairs={{0,4},{2,6},{4,0},{6,2},{8,12},{10,14},{12,8},{14,10},{16,20},{18,... | collective-permute-start | bytes 786440 | tf_op jit(solution)/shard_map/ppermute | solution.py:405
  34.7 0.0 collective-permute-done.6
  34.7 0.2 add_convert_fusion
  35.0 1.7 %collective-permute-start.7 = (bf16[128,640]{1,0:T(8,128)(2,1)S(1)}, bf16[128,640]{1,0:T(8,128)(2,1)S(1)}, u32[]{:S(2)}, u32[]{:S(2)}) collective-permute-start(bf16[128,640]{1,0:T(8,128)(2,1)S(1)} %get-tuple-element.49), channel_id=1, source_target_pairs={{0,4},{1,5},{2,6},{3,7},{4,0},{5,1},{6,2},{7,3},{8,12},{9,13},{10,... | collective-permute-start | bytes 491528 | tf_op jit(solution)/shard_map/ppermute | solution.py:414
  36.7 1.3 %collective-permute-start.9 = (bf16[128,640]{1,0:T(8,128)(2,1)S(1)}, bf16[128,640]{1,0:T(8,128)(2,1)S(1)}, u32[]{:S(2)}, u32[]{:S(2)}) collective-permute-start(bf16[128,640]{1,0:T(8,128)(2,1)S(1)} %get-tuple-element.50), channel_id=1, source_target_pairs={{0,5},{1,4},{2,7},{3,6},{4,1},{5,0},{6,3},{7,2},{8,13},{9,12},{10,... | collective-permute-start | bytes 491528 | tf_op jit(solution)/shard_map/ppermute | solution.py:414
  38.0 0.5 collective-permute-start.8
  38.5 6.8 %collective-permute-done.3 = bf16[128,1024]{1,0:T(8,128)(2,1)S(1)} collective-permute-done((bf16[128,1024]{1,0:T(8,128)(2,1)S(1)}, bf16[128,1024]{1,0:T(8,128)(2,1)S(1)}, u32[]{:S(2)}, u32[]{:S(2)}) %collective-permute-start.3) | collective-permute-done | bytes 262176 | tf_op jit(solution)/shard_map/ppermute | solution.py:405
  45.3 0.1 add_convert_fusion.2
  45.4 2.3 %collective-permute-start.4 = (bf16[64,1024]{1,0:T(8,128)(2,1)S(1)}, bf16[64,1024]{1,0:T(8,128)(2,1)S(1)}, u32[]{:S(2)}, u32[]{:S(2)}) collective-permute-start(bf16[64,1024]{1,0:T(8,128)(2,1)S(1)} %slice.57), channel_id=1, source_target_pairs={{0,8},{2,10},{4,12},{6,14},{8,0},{10,2},{12,4},{14,6},{16,24},{18,... | collective-permute-start | bytes 393224 | tf_op jit(solution)/shard_map/ppermute | solution.py:405
  47.8 0.6 collective-permute-done.7
  48.4 0.0 collective-permute-done.9
  48.4 0.0 collective-permute-done.8
  48.4 0.1 fusion.2
  48.5 2.0 %collective-permute-start.10 = (bf16[64,640]{1,0:T(8,128)(2,1)S(1)}, bf16[64,640]{1,0:T(8,128)(2,1)S(1)}, u32[]{:S(2)}, u32[]{:S(2)}) collective-permute-start(bf16[64,640]{1,0:T(8,128)(2,1)S(1)} %slice.65), channel_id=1, source_target_pairs={{0,8},{2,10},{4,12},{6,14},{8,0},{10,2},{12,4},{14,6},{16,24},{18,... | collective-permute-start | bytes 245768 | tf_op jit(solution)/shard_map/ppermute | solution.py:405
  50.5 0.2 collective-permute-done.4
  50.8 3.4 %collective-permute-start.5 = (bf16[32,1024]{1,0:T(8,128)(2,1)S(1)}, bf16[32,1024]{1,0:T(8,128)(2,1)S(1)}, u32[]{:S(2)}, u32[]{:S(2)}) collective-permute-start(bf16[32,1024]{1,0:T(8,128)(2,1)S(1)} %slice.59), channel_id=1, source_target_pairs={{0,16},{2,18},{4,20},{6,22},{8,24},{10,26},{12,28},{14,30},{16,0},... | collective-permute-start | bytes 196616 | tf_op jit(solution)/shard_map/ppermute | solution.py:405
  54.2 0.0 collective-permute-done.10
  54.2 2.1 %collective-permute-start.11 = (bf16[32,640]{1,0:T(8,128)(2,1)S(1)}, bf16[32,640]{1,0:T(8,128)(2,1)S(1)}, u32[]{:S(2)}, u32[]{:S(2)}) collective-permute-start(bf16[32,640]{1,0:T(8,128)(2,1)S(1)} %slice.67), channel_id=1, source_target_pairs={{0,16},{2,18},{4,20},{6,22},{8,24},{10,26},{12,28},{14,30},{16,0},... | collective-permute-start | bytes 122888 | tf_op jit(solution)/shard_map/ppermute | solution.py:405
  56.3 1.5 %collective-permute-done.5 = bf16[32,1024]{1,0:T(8,128)(2,1)S(1)} collective-permute-done((bf16[32,1024]{1,0:T(8,128)(2,1)S(1)}, bf16[32,1024]{1,0:T(8,128)(2,1)S(1)}, u32[]{:S(2)}, u32[]{:S(2)}) %collective-permute-start.5) | collective-permute-done | bytes 65568 | tf_op jit(solution)/shard_map/ppermute | solution.py:405
  57.8 1.4 %collective-permute-done.11 = bf16[32,640]{1,0:T(8,128)(2,1)S(1)} collective-permute-done((bf16[32,640]{1,0:T(8,128)(2,1)S(1)}, bf16[32,640]{1,0:T(8,128)(2,1)S(1)}, u32[]{:S(2)}, u32[]{:S(2)}) %collective-permute-start.11) | collective-permute-done | bytes 40992 | tf_op jit(solution)/shard_map/ppermute | solution.py:405
  59.2 1.6 %collective-permute-start.12 = (bf16[32,1664]{1,0:T(8,128)(2,1)S(1)}, bf16[32,1664]{1,0:T(8,128)(2,1)S(1)}, u32[]{:S(2)}, u32[]{:S(2)}) collective-permute-start(bf16[32,1664]{1,0:T(8,128)(2,1)S(1)} %pad_maximum_fusion), channel_id=1, source_target_pairs={{0,1},{1,0},{2,3},{3,2},{4,5},{5,4},{6,7},{7,6},{8,9},{9,8},{10,11... | collective-permute-start | bytes 319496 | tf_op jit(solution)/shard_map/ppermute | solution.py:405
  60.8 1.7 %grads.1 = bf16[4,1024,128]{2,1,0:T(8,128)(2,1)} custom-call(bf16[512,1024]{1,0:T(8,128)(2,1)S(1)} %copy-done.5, bf16[4,512,128]{2,1,0:T(8,128)(2,1)S(1)} %get-tuple-element.41.erra_ref, f32[4,1024,128]{2,1,0:T(8,128)S(1)} %get-tuple-element.42.back_ref), custom_call_target="tpu_custom_call" | custom-call | flops 2200000000 | bytes 1048576 | tf_op jit(solution)/shard_map/grads/pallas_call | solution.py:485
  62.5 1.5 %collective-permute-done.12.got_ref = bf16[32,1664]{1,0:T(8,128)(2,1)S(1)} collective-permute-done((bf16[32,1664]{1,0:T(8,128)(2,1)S(1)}, bf16[32,1664]{1,0:T(8,128)(2,1)S(1)}, u32[]{:S(2)}, u32[]{:S(2)}) %collective-permute-start.12) | collective-permute-done | bytes 106528 | tf_op jit(solution)/shard_map/ppermute | solution.py:405
  64.0 0.7 %finish.1 = (f32[32,1024]{1,0:T(8,128)}, f32[32,144]{1,0:T(8,128)}, f32[32,1024]{1,0:T(8,128)}) custom-call(bf16[32,1024]{1,0:T(8,128)(2,1)S(1)} %add_convert_fusion.5.e_ref, bf16[32,640]{1,0:T(8,128)(2,1)S(1)} %add_convert_fusion.6.r_ref, bf16[32,1664]{1,0:T(8,128)(2,1)S(1)} %collective-permute-done.12.got_ref), custom_call_target="tpu_custom_call" | custom-call | flops 1100000000 | bytes 1048576 | tf_op jit(solution)/shard_map/finish/pallas_call | solution.py:510
  (14 shorter events, 0.2 us)
Async XLA Ops:
  0.6 1.2 %copy-start = (bf16[1,4,1024,128]{3,2,1,0:T(8,128)(2,1)S(1)}, bf16[1,4,1024,128]{3,2,1,0:T(8,128)(2,1)}, u32[]{:S(2)}) copy-start(bf16[1,4,1024,128]{3,2,1,0:T(8,128)(2,1)} %param.14) | copy-start | bytes 3145732
  1.9 1.2 %copy-start.3 = (bf16[1,4,1024,128]{3,2,1,0:T(8,128)(2,1)S(1)}, bf16[1,4,1024,128]{3,2,1,0:T(8,128)(2,1)}, u32[]{:S(2)}) copy-start(bf16[1,4,1024,128]{3,2,1,0:T(8,128)(2,1)} %param.13) | copy-start | bytes 3145732
  3.1 0.7 %copy-start.13 = (s32[1,16]{1,0:T(1,128)S(1)}, s32[1,16]{1,0:T(1,128)}, u32[]{:S(2)}) copy-start(s32[1,16]{1,0:T(1,128)} %count_hbm.1) | copy-start | bytes 196
  3.7 0.7 %copy-start.14 = (s32[1,31]{1,0:T(1,128)S(1)}, s32[1,31]{1,0:T(1,128)}, u32[]{:S(2)}) copy-start(s32[1,31]{1,0:T(1,128)} %joined_hbm.1) | copy-start | bytes 376
  4.4 3.0 %copy-start.2 = (bf16[512,1024]{1,0:T(8,128)(2,1)S(1)}, bf16[512,1024]{1,0:T(8,128)(2,1)}, u32[]{:S(2)}) copy-start(bf16[512,1024]{1,0:T(8,128)(2,1)} %we_ref.3) | copy-start | bytes 3145732
  4.4 3.0 %copy-start.4 = (bf16[1,4,1024,128]{3,2,1,0:T(8,128)(2,1)S(1)}, bf16[1,4,1024,128]{3,2,1,0:T(8,128)(2,1)}, u32[]{:S(2)}) copy-start(bf16[1,4,1024,128]{3,2,1,0:T(8,128)(2,1)} %param.13) | copy-start | bytes 3145732
  4.4 3.0 %copy-start.5 = (bf16[512,1024]{1,0:T(8,128)(2,1)S(1)}, bf16[512,1024]{1,0:T(8,128)(2,1)}, u32[]{:S(2)}) copy-start(bf16[512,1024]{1,0:T(8,128)(2,1)} %wr_ref.5) | copy-start | bytes 3145732
  4.4 3.0 %copy-start.6 = (bf16[512,144]{0,1:T(8,128)(2,1)S(1)}, bf16[512,144]{0,1:T(8,128)(2,1)}, u32[]{:S(2)}) copy-start(bf16[512,144]{0,1:T(8,128)(2,1)} %param.16) | copy-start | bytes 442372
  4.4 3.0 %copy-start.9 = (f32[512]{0:T(512)S(1)}, f32[512]{0:T(512)}, u32[]{:S(2)}) copy-start(f32[512]{0:T(512)} %param.18) | copy-start | bytes 6148
  4.4 3.0 %copy-start.10 = (f32[512]{0:T(512)S(1)}, f32[512]{0:T(512)}, u32[]{:S(2)}) copy-start(f32[512]{0:T(512)} %param.19) | copy-start | bytes 6148
  6.2 4.2 %collective-permute-start = (bf16[48,1024]{1,0:T(8,128)(2,1)S(1)}, bf16[48,1024]{1,0:T(8,128)(2,1)S(1)}, u32[]{:S(2)}, u32[]{:S(2)}) collective-permute-start(bf16[48,1024]{1,0:T(8,128)(2,1)S(1)} %get-tuple-element.28), channel_id=1, source_target_pairs={{0,2},{2,0},{4,6},{6,4},{8,10},{10,8},{12,14},{14,12},{16,18},{18,... | collective-permute-start | bytes 294920 | tf_op jit(solution)/shard_map/ppermute | solution.py:405
  6.7 3.7 %collective-permute-start.1 = (bf16[48,1024]{1,0:T(8,128)(2,1)S(1)}, bf16[48,1024]{1,0:T(8,128)(2,1)S(1)}, u32[]{:S(2)}, u32[]{:S(2)}) collective-permute-start(bf16[48,1024]{1,0:T(8,128)(2,1)S(1)} %get-tuple-element.29), channel_id=1, source_target_pairs={{2,4},{6,8},{10,12},{14,16},{18,20},{22,24},{26,28},{4,2},{8,6},{1... | collective-permute-start | bytes 294920 | tf_op jit(solution)/shard_map/ppermute | solution.py:453
  7.4 3.0 %copy-start.1 = (bf16[1,4,1024,128]{3,2,1,0:T(8,128)(2,1)S(1)}, bf16[1,4,1024,128]{3,2,1,0:T(8,128)(2,1)}, u32[]{:S(2)}) copy-start(bf16[1,4,1024,128]{3,2,1,0:T(8,128)(2,1)} %param.14) | copy-start | bytes 3145732
  7.4 3.0 %copy-start.7 = (f32[1024]{0:T(1024)S(1)}, f32[1024]{0:T(1024)}, u32[]{:S(2)}) copy-start(f32[1024]{0:T(1024)} %param.22) | copy-start | bytes 12292
  7.5 3.0 %copy-start.8 = (f32[1024]{0:T(1024)S(1)}, f32[1024]{0:T(1024)}, u32[]{:S(2)}) copy-start(f32[1024]{0:T(1024)} %param.23) | copy-start | bytes 12292
  7.5 3.0 %copy-start.11 = (f32[512]{0:T(512)S(1)}, f32[512]{0:T(512)}, u32[]{:S(2)}) copy-start(f32[512]{0:T(512)} %param.20) | copy-start | bytes 6148
  7.5 3.0 %copy-start.12 = (f32[512]{0:T(512)S(1)}, f32[512]{0:T(512)}, u32[]{:S(2)}) copy-start(f32[512]{0:T(512)} %param.21) | copy-start | bytes 6148
  18.7 5.4 %collective-permute-start.2 = (bf16[256,1024]{1,0:T(8,128)(2,1)S(1)}, bf16[256,1024]{1,0:T(8,128)(2,1)S(1)}, u32[]{:S(2)}, u32[]{:S(2)}) collective-permute-start(bf16[256,1024]{1,0:T(8,128)(2,1)S(1)} %get-tuple-element.37), channel_id=1, source_target_pairs={{0,2},{2,0},{4,6},{6,4},{8,10},{10,8},{12,14},{14,12},{16,18},{18,... | collective-permute-start | bytes 1572872 | tf_op jit(solution)/shard_map/ppermute | solution.py:405
  32.0 2.8 %collective-permute-start.6 = (bf16[2,256,640]{2,1,0:T(8,128)(2,1)S(1)}, bf16[2,256,640]{2,1,0:T(8,128)(2,1)S(1)}, u32[]{:S(2)}, u32[]{:S(2)}) collective-permute-start(bf16[2,256,640]{2,1,0:T(8,128)(2,1)S(1)} %get-tuple-element.45), channel_id=1, source_target_pairs={{0,2},{2,0},{4,6},{6,4},{8,10},{10,8},{12,14},{14,12},{16,18},{18,... | collective-permute-start | bytes 1966088 | tf_op jit(solution)/shard_map/ppermute | solution.py:405
  32.4 12.9 %collective-permute-start.3 = (bf16[128,1024]{1,0:T(8,128)(2,1)S(1)}, bf16[128,1024]{1,0:T(8,128)(2,1)S(1)}, u32[]{:S(2)}, u32[]{:S(2)}) collective-permute-start(bf16[128,1024]{1,0:T(8,128)(2,1)S(1)} %slice.43), channel_id=1, source_target_pairs={{0,4},{2,6},{4,0},{6,2},{8,12},{10,14},{12,8},{14,10},{16,20},{18,... | collective-permute-start | bytes 786440 | tf_op jit(solution)/shard_map/ppermute | solution.py:405
  35.0 13.4 %collective-permute-start.7 = (bf16[128,640]{1,0:T(8,128)(2,1)S(1)}, bf16[128,640]{1,0:T(8,128)(2,1)S(1)}, u32[]{:S(2)}, u32[]{:S(2)}) collective-permute-start(bf16[128,640]{1,0:T(8,128)(2,1)S(1)} %get-tuple-element.49), channel_id=1, source_target_pairs={{0,4},{1,5},{2,6},{3,7},{4,0},{5,1},{6,2},{7,3},{8,12},{9,13},{10,... | collective-permute-start | bytes 491528 | tf_op jit(solution)/shard_map/ppermute | solution.py:414
  36.7 11.7 %collective-permute-start.9 = (bf16[128,640]{1,0:T(8,128)(2,1)S(1)}, bf16[128,640]{1,0:T(8,128)(2,1)S(1)}, u32[]{:S(2)}, u32[]{:S(2)}) collective-permute-start(bf16[128,640]{1,0:T(8,128)(2,1)S(1)} %get-tuple-element.50), channel_id=1, source_target_pairs={{0,5},{1,4},{2,7},{3,6},{4,1},{5,0},{6,3},{7,2},{8,13},{9,12},{10,... | collective-permute-start | bytes 491528 | tf_op jit(solution)/shard_map/ppermute | solution.py:414
  38.0 10.4 %collective-permute-start.8 = (bf16[128,640]{1,0:T(8,128)(2,1)S(1)}, bf16[128,640]{1,0:T(8,128)(2,1)S(1)}, u32[]{:S(2)}, u32[]{:S(2)}) collective-permute-start(bf16[128,640]{1,0:T(8,128)(2,1)S(1)} %get-tuple-element.51), channel_id=1, source_target_pairs={{0,1},{1,0},{2,3},{3,2},{4,5},{5,4},{6,7},{7,6},{8,9},{9,8},{10,11... | collective-permute-start | bytes 491528 | tf_op jit(solution)/shard_map/ppermute | solution.py:414
  45.4 5.3 %collective-permute-start.4 = (bf16[64,1024]{1,0:T(8,128)(2,1)S(1)}, bf16[64,1024]{1,0:T(8,128)(2,1)S(1)}, u32[]{:S(2)}, u32[]{:S(2)}) collective-permute-start(bf16[64,1024]{1,0:T(8,128)(2,1)S(1)} %slice.57), channel_id=1, source_target_pairs={{0,8},{2,10},{4,12},{6,14},{8,0},{10,2},{12,4},{14,6},{16,24},{18,... | collective-permute-start | bytes 393224 | tf_op jit(solution)/shard_map/ppermute | solution.py:405
  48.5 5.7 %collective-permute-start.10 = (bf16[64,640]{1,0:T(8,128)(2,1)S(1)}, bf16[64,640]{1,0:T(8,128)(2,1)S(1)}, u32[]{:S(2)}, u32[]{:S(2)}) collective-permute-start(bf16[64,640]{1,0:T(8,128)(2,1)S(1)} %slice.65), channel_id=1, source_target_pairs={{0,8},{2,10},{4,12},{6,14},{8,0},{10,2},{12,4},{14,6},{16,24},{18,... | collective-permute-start | bytes 245768 | tf_op jit(solution)/shard_map/ppermute | solution.py:405
  50.8 7.1 %collective-permute-start.5 = (bf16[32,1024]{1,0:T(8,128)(2,1)S(1)}, bf16[32,1024]{1,0:T(8,128)(2,1)S(1)}, u32[]{:S(2)}, u32[]{:S(2)}) collective-permute-start(bf16[32,1024]{1,0:T(8,128)(2,1)S(1)} %slice.59), channel_id=1, source_target_pairs={{0,16},{2,18},{4,20},{6,22},{8,24},{10,26},{12,28},{14,30},{16,0},... | collective-permute-start | bytes 196616 | tf_op jit(solution)/shard_map/ppermute | solution.py:405
  54.2 5.0 %collective-permute-start.11 = (bf16[32,640]{1,0:T(8,128)(2,1)S(1)}, bf16[32,640]{1,0:T(8,128)(2,1)S(1)}, u32[]{:S(2)}, u32[]{:S(2)}) collective-permute-start(bf16[32,640]{1,0:T(8,128)(2,1)S(1)} %slice.67), channel_id=1, source_target_pairs={{0,16},{2,18},{4,20},{6,22},{8,24},{10,26},{12,28},{14,30},{16,0},... | collective-permute-start | bytes 122888 | tf_op jit(solution)/shard_map/ppermute | solution.py:405
  59.2 4.8 %collective-permute-start.12 = (bf16[32,1664]{1,0:T(8,128)(2,1)S(1)}, bf16[32,1664]{1,0:T(8,128)(2,1)S(1)}, u32[]{:S(2)}, u32[]{:S(2)}) collective-permute-start(bf16[32,1664]{1,0:T(8,128)(2,1)S(1)} %pad_maximum_fusion), channel_id=1, source_target_pairs={{0,1},{1,0},{2,3},{3,2},{4,5},{5,4},{6,7},{7,6},{8,9},{9,8},{10,11... | collective-permute-start | bytes 319496 | tf_op jit(solution)/shard_map/ppermute | solution.py:405

commit v3 on v2

--- a/solution.py
+++ b/solution.py
@@ -3,6 +3,7 @@
 
 import jax
 import jax.numpy as jnp
+import numpy as np
 from jax import lax
 from jax.experimental import pallas as pl
 from jax.experimental.pallas import tpu as pltpu
@@ -23,7 +24,8 @@
 BF = jnp.bfloat16
 F32 = jnp.float32
 
-HELD, L_LINK, R_LINK, L_IDX, R_IDX, META = 0, 1, 6, 11, 16, 24
+HELD, L_IDX, R_IDX, META = 0, 1, 6, 16
+EDGE, ZERO = SLOTS, SLOTS + 1
 
 
 def nt_dot(a, b):
@@ -71,14 +73,11 @@
 ):
     me = lax.axis_index("tile")
     tables = [
-        pltpu.make_async_copy(count_hbm, count_ref, sems.at[4]),
-        pltpu.make_async_copy(joined_hbm, joined_ref, sems.at[5]),
+        pltpu.make_async_copy(count_hbm, count_ref, sems.at[2]),
+        pltpu.make_async_copy(joined_hbm, joined_ref, sems.at[3]),
     ]
-    firsts = [
-        pltpu.make_async_copy(x_any.at[0], xbuf.at[0], sems.at[0]),
-        pltpu.make_async_copy(g_any.at[0], gbuf.at[0], sems.at[1]),
-    ]
-    for copy in tables + firsts:
+    loads = [pltpu.make_async_copy(x_any, xbuf, sems.at[0]), pltpu.make_async_copy(g_any, gbuf, sems.at[1])]
+    for copy in tables + loads:
         copy.start()
     for copy in tables:
         copy.wait()
@@ -90,43 +89,32 @@
         start = start + jnp.where(e < me, count_ref[0, e], 0)
         held = held + jnp.where(e == me, count_ref[0, e], 0)
     last = held - 1
-    lasts = [
-        pltpu.make_async_copy(x_any.at[last], xbuf.at[1], sems.at[2]),
-        pltpu.make_async_copy(g_any.at[last], gbuf.at[1], sems.at[3]),
-    ]
-    for copy in lasts:
-        copy.start()
-
-    def link(at):
+    def joined_to(at, neighbour):
         inside = jnp.logical_and(at >= 0, at < links)
-        return jnp.where(inside, joined_ref[0, jnp.clip(at, 0, links - 1)], 0)
+        on = joined_ref[0, jnp.clip(at, 0, links - 1)] != 0
+        return jnp.where(jnp.logical_and(inside, on), neighbour, ZERO).astype(jnp.int32)
 
     meta_ref[HELD] = held
-    first_left = link(start - 1)
-    last_right = link(start + last)
     for i in range(SLOTS):
-        live = i < held
-        meta_ref[L_LINK + i] = jnp.where(live, link(start + i - 1), 0)
-        meta_ref[R_LINK + i] = jnp.where(live, link(start + i), 0)
-        meta_ref[L_IDX + i] = jnp.int32(SLOTS if i == 0 else i - 1)
-        meta_ref[R_IDX + i] = jnp.where(i >= last, SLOTS, i + 1).astype(jnp.int32)
-    meta_ref[L_LINK + SLOTS] = last_right
-    meta_ref[R_LINK + SLOTS] = first_left
-    meta_ref[L_IDX + SLOTS] = last
-    meta_ref[R_IDX + SLOTS] = jnp.int32(0)
-
-    for copy in firsts + lasts:
+        left = joined_to(start + i - 1, EDGE if i == 0 else i - 1)
+        right = joined_to(start + i, jnp.where(i >= last, EDGE, i + 1))
+        meta_ref[L_IDX + i] = jnp.where(i < held, left, ZERO).astype(jnp.int32)
+        meta_ref[R_IDX + i] = jnp.where(i < held, right, ZERO).astype(jnp.int32)
+    meta_ref[L_IDX + EDGE] = joined_to(start + last, last)
+    meta_ref[R_IDX + EDGE] = joined_to(start - 1, 0)
+
+    for copy in loads:
         copy.wait()
     even = me % 2 == 0
 
-    def payload(side, x_first, g_col):
+    def payload(slot, x_first, g_col):
         return (
-            nt_dot(edge_select(2 * TH, x_lane(x_first)), xbuf[side]).astype(BF),
-            nt_dot(edge_select(TH, g_lane(g_col)), gbuf[side]).astype(BF),
+            nt_dot(edge_select(2 * TH, x_lane(x_first)), xbuf[slot]).astype(BF),
+            nt_dot(edge_select(TH, g_lane(g_col)), gbuf[slot]).astype(BF),
         )
 
     left_x, left_g = payload(0, 0, 0)
-    right_x, right_g = payload(1, TW - 2, TW - 1)
+    right_x, right_g = payload(last, TW - 2, TW - 1)
 
     @pl.when(even)
     def _():
@@ -182,44 +170,49 @@
     wet_ref[...] = jnp.transpose(we_ref[...])
 
 
-def build_windows(field_ref, win_ref, meta_ref, tiles, transposed):
+def silu_slope(v):
+    sig = sigmoid(v)
+    act = v * sig
+    return act, sig + act * (1.0 - sig)
+
+
+def build_windows(field_ref, win_ref, meta_ref, tiles, first, transposed):
     lane = lax.broadcasted_iota(jnp.int32, (HALF, PIX), 1)
     col = lane % TW
     first_col = col == 0
     last_col = col == TW - 1
     has_above = lane >= TW
     has_below = lane < PIX - TW
+    zero = jnp.zeros((), BF)
     for i in tiles:
         left_at = meta_ref[L_IDX + i]
         right_at = meta_ref[R_IDX + i]
-        left_link = meta_ref[L_LINK + i].astype(F32)
-        right_link = meta_ref[R_LINK + i].astype(F32)
-        lanes = pl.ds(i * PIX, PIX)
+        lanes = pl.ds((i - first) * PIX, PIX)
         for b in range(2):
             rows = pl.ds(b * HALF, HALF)
-            own = field_ref[i, rows, :].astype(F32)
-            left = field_ref[left_at, rows, :].astype(F32) * left_link
-            right = field_ref[right_at, rows, :].astype(F32) * right_link
+            own = field_ref[i, rows, :]
+            left = field_ref[left_at, rows, :]
+            right = field_ref[right_at, rows, :]
             west = jnp.where(first_col, pltpu.roll(left, PIX - TW + 1, 1), pltpu.roll(own, 1, 1))
             east = jnp.where(last_col, pltpu.roll(right, TW - 1, 1), pltpu.roll(own, PIX - 1, 1))
             for v, base in enumerate((west, own, east)):
-                above = jnp.where(has_above, pltpu.roll(base, TW, 1), 0.0)
-                below = jnp.where(has_below, pltpu.roll(base, PIX - TW, 1), 0.0)
+                above = jnp.where(has_above, pltpu.roll(base, TW, 1), zero)
+                below = jnp.where(has_below, pltpu.roll(base, PIX - TW, 1), zero)
                 for u, shifted in enumerate((above, base, below)):
                     tap = 3 * u + v
                     if transposed:
                         tap = TAPS - 1 - tap
-                    win_ref[b, pl.ds(tap * HALF, HALF), lanes] = shifted.astype(BF)
-
-
-CHUNKS = ((0, 2), (2, 2), (4, 1))
+                    win_ref[b, pl.ds(tap * HALF, HALF), lanes] = shifted
+
+
+CHUNKS = ((0, 2), (2, 2))
 
 
 def forward_kernel(
     devices, meta_ref, core_ref, other_ref, hid_in, wr_ref, s1_ref, b1_ref, dense_ref,
     s2_ref, b2_ref, wet_ref, s3_ref, b3_ref, x_ref, g_ref,
-    out_ref, back_ref, errc_ref, slopeb_ref, send_ref, keep_ref,
-    hid_ref, win_ref, hidb_ref,
+    out_ref, back_ref, errc_ref, slopeb_ref, hid_ref, edge_ref, send_ref, keep_ref,
+    win_ref, hidb_ref,
 ):
     me = lax.axis_index("tile")
     held = meta_ref[HELD]
@@ -232,52 +225,38 @@
     shift3 = column(b3_ref)
     core_first = jnp.where(odd == 0, 0, TW - 2)
     other_first = jnp.where(odd == 0, TW - 2, 0)
-    core_g = jnp.where(odd == 0, 0, TW - 1)
-    other_g = jnp.where(odd == 0, TW - 1, 0)
     edge_x = (
         tn_dot(core_ref[: 2 * TH, :], edge_select(2 * TH, x_lane(core_first)))
         + tn_dot(other_ref[: 2 * TH, :], edge_select(2 * TH, x_lane(other_first)))
     ).astype(BF)
-    edge_g = (
-        tn_dot(core_ref[2 * TH :, :], edge_select(TH, g_lane(core_g)))
-        + tn_dot(other_ref[2 * TH :, :], edge_select(TH, g_lane(other_g)))
-    )
+    edge_ref[...] = edge_x
     for i in range(SLOTS):
         hid_ref[i] = hid_in[i]
     pre = nn_dot(wr_ref[...], edge_x) * scale1 + shift1
-    hid_ref[SLOTS] = (pre * sigmoid(pre)).astype(BF)
+    hid_ref[EDGE] = (pre * sigmoid(pre)).astype(BF)
+    hid_ref[ZERO] = jnp.zeros((MID, PIX), BF)
 
     for first, count in CHUNKS:
-        build_windows(hid_ref, win_ref, meta_ref, range(first, first + count), False)
+        build_windows(hid_ref, win_ref, meta_ref, range(first, first + count), 0, False)
         lanes = slice(first * PIX, (first + count) * PIX)
         for b in range(2):
             conv = nn_dot(dense_ref[b], win_ref[b, :, lanes])
             rows = slice(b * HALF, (b + 1) * HALF)
             for k in range(count):
                 at = slice((first + k) * PIX, (first + k + 1) * PIX)
-                v = conv[:, k * PIX : (k + 1) * PIX] * scale2[rows] + shift2[rows]
-                sig = sigmoid(v)
-                act = v * sig
+                act, slope = silu_slope(conv[:, k * PIX : (k + 1) * PIX] * scale2[rows] + shift2[rows])
                 hidb_ref[rows, at] = act.astype(BF)
-                slopeb_ref[rows, at] = (sig + act * (1.0 - sig)) * scale2[rows]
+                slopeb_ref[rows, at] = slope * scale2[rows]
         grown = nn_dot(wet_ref[...], hidb_ref[:, lanes])
         for k in range(count):
             i = first + k
-            if i < SLOTS:
-                tile = x_ref[i].astype(F32)
-                cot = g_ref[i].astype(F32)
-            else:
-                tile = edge_x.astype(F32)
-                cot = edge_g
-            total = grown[:, k * PIX : (k + 1) * PIX] * scale3 + shift3 + tile
-            sig = sigmoid(total)
-            act = total * sig
-            back = cot * (sig + act * (1.0 - sig))
-            if i < SLOTS:
-                live = jnp.where(i < held, 1.0, 0.0).astype(F32)
-                back = back * live
-                out_ref[i] = (act * live).astype(BF)
-                back_ref[i] = back
+            act, slope = silu_slope(
+                grown[:, k * PIX : (k + 1) * PIX] * scale3 + shift3 + x_ref[i].astype(F32)
+            )
+            live = jnp.where(i < held, 1.0, 0.0).astype(F32)
+            back = g_ref[i].astype(F32) * slope * live
+            out_ref[i] = (act * live).astype(BF)
+            back_ref[i] = back
             errc_ref[:, i * PIX : (i + 1) * PIX] = (back * scale3).astype(BF)
 
     own = SLOTS * PIX
@@ -299,23 +278,51 @@
     return blocks
 
 
-def pull_kernel(we_ref, errc_ref, slopeb_ref, errb_ref):
+def pull_kernel(
+    meta_ref, core_ref, other_ref, hid_ref, dense_ref, s2_ref, b2_ref, wet_ref, s3_ref, b3_ref,
+    edge_ref, we_ref, errc_ref, slopeb_ref, errb_ref, win_ref, hidb_ref, slope_ref,
+):
+    odd = lax.axis_index("tile") % 2
+    core_g = jnp.where(odd == 0, 0, TW - 1)
+    other_g = jnp.where(odd == 0, TW - 1, 0)
+    edge_g = (
+        tn_dot(core_ref[2 * TH :, :], edge_select(TH, g_lane(core_g)))
+        + tn_dot(other_ref[2 * TH :, :], edge_select(TH, g_lane(other_g)))
+    )
+    scale2 = column(s2_ref)
+    shift2 = column(b2_ref)
+    scale3 = column(s3_ref)
+    shift3 = column(b3_ref)
+    build_windows(hid_ref, win_ref, meta_ref, (EDGE,), EDGE, False)
+    for b in range(2):
+        conv = nn_dot(dense_ref[b], win_ref[b])
+        rows = slice(b * HALF, (b + 1) * HALF)
+        act, slope = silu_slope(conv * scale2[rows] + shift2[rows])
+        hidb_ref[rows, :] = act.astype(BF)
+        slope_ref[rows, :] = slope * scale2[rows]
     for first, count in CHUNKS:
         lanes = slice(first * PIX, (first + count) * PIX)
         pulled = nn_dot(we_ref[...], errc_ref[:, lanes])
         errb = (pulled * slopeb_ref[:, lanes]).astype(BF)
         for k in range(count):
             errb_ref[first + k] = errb[:, k * PIX : (k + 1) * PIX]
+    grown = nn_dot(wet_ref[...], hidb_ref[...])
+    _, slope = silu_slope(grown * scale3 + shift3 + edge_ref[...].astype(F32))
+    errc = (edge_g * slope * scale3).astype(BF)
+    errb_ref[EDGE] = (nn_dot(we_ref[...], errc) * slope_ref[...]).astype(BF)
+    errb_ref[ZERO] = jnp.zeros((MID, PIX), BF)
 
 
 def backward_kernel(
-    devices, meta_ref, errb_ref, hid_ref, slope_ref, denset_ref, x_ref,
-    erra_ref, send_ref, keep_ref, win_ref, flat_ref, groups_ref,
+    devices, meta_ref, errb_ref, hid_ref, slope_ref, denset_ref, x_ref, place_ref,
+    erra_ref, *rest,
 ):
+    send_refs, keep_refs = rest[:4], rest[4:8]
+    win_ref, flat_ref, groups_ref, kept_ref = rest[8:]
     me = lax.axis_index("tile")
     side = lax.axis_index("slide") % 2
-    for first, count in CHUNKS[:2]:
-        build_windows(errb_ref, win_ref, meta_ref, range(first, first + count), True)
+    for first, count in CHUNKS:
+        build_windows(errb_ref, win_ref, meta_ref, range(first, first + count), 0, True)
         lanes = slice(first * PIX, (first + count) * PIX)
         for b in range(2):
             conv = nn_dot(denset_ref[b], win_ref[b, :, lanes])
@@ -330,30 +337,33 @@
     same = row // GW == col // GW
     for b in range(2):
         rows = slice(b * HALF, (b + 1) * HALF)
-        hid = jnp.concatenate([hid_ref[i, rows, :] for i in range(SLOTS)], axis=1)
-        folded = jnp.zeros((HALF, HALF), F32)
+        hid = jnp.transpose(jnp.concatenate([hid_ref[i, rows, :] for i in range(SLOTS)], axis=1))
         for k in range(TAPS):
-            full = nt_dot(win_ref[b, k * HALF : (k + 1) * HALF, :], hid)
-            kept = jnp.where(same, full, 0.0).astype(BF)
-            place = (col == k * GW + row % GW).astype(F32).astype(BF)
-            folded = folded + nn_dot(kept, place)
-        groups_ref[rows, :] = folded.astype(BF)
+            full = nn_dot(win_ref[b, k * HALF : (k + 1) * HALF, :], hid)
+            kept_ref[:, k * HALF : (k + 1) * HALF] = jnp.where(same, full, 0.0).astype(BF)
+        groups_ref[rows, :] = nn_dot(kept_ref[...], place_ref[...]).astype(BF)
     width = CIN // 2
     tiles = [
         jnp.concatenate([x_ref[i, pl.ds(pl.multiple_of((side ^ dx) * width, width), width), :] for i in range(SLOTS)], axis=1)
         for dx in range(2)
     ]
-    for ref, flip in ((send_ref, 1), (keep_ref, 0)):
+    quarter = HALF // 2
+    for refs, flip in ((send_refs, 1), (keep_refs, 0)):
         blocks = row_blocks(devices, me, flip)
         rows = jnp.concatenate([flat_ref[at, :] for at in blocks], axis=0)
         group_rows = jnp.concatenate([groups_ref[at, :] for at in blocks], axis=0)
         low, high = group_rows[:, :PIX], group_rows[:, PIX:]
         for dx in range(2):
-            ref[dx, :, :width] = nt_dot(rows, tiles[dx]).astype(BF)
-            ref[dx, :, width:] = jnp.where(side == dx, low, high)
-
-
-def grad_kernel(wr_ref, erra_ref, back_ref, grad_ref):
+            part = nt_dot(rows, tiles[dx]).astype(BF)
+            group_part = jnp.where(side == dx, low, high)
+            for dy in range(2):
+                at = slice(dy * quarter, (dy + 1) * quarter)
+                refs[2 * dx + dy][:, :width] = part[at]
+                refs[2 * dx + dy][:, width:] = group_part[at]
+
+
+def grad_kernel(wr_ref, erra_ref, back_ref, act_ref, grad_ref, out_ref):
+    out_ref[...] = act_ref[...]
     for half in range(SLOTS // 2):
         err = jnp.concatenate([erra_ref[2 * half], erra_ref[2 * half + 1]], axis=1)
         pulled = tn_dot(wr_ref[...], err)
@@ -376,8 +386,8 @@
     group_ref[:, PIX:] = high[:, width : width + TAPS * GW - PIX]
 
 
-LIMITS = {"edges": 3, "prep": 13, "forward": 26, "pull": 6, "backward": 16, "grads": 6, "finish": 2}
-WORK = {"edges": 2, "prep": 3, "forward": 7, "pull": 1.5, "backward": 8, "grads": 2, "finish": 1}
+LIMITS = {"edges": 56, "prep": 13, "forward": 26, "pull": 14, "backward": 18, "grads": 9, "finish": 2}
+WORK = {"edges": 2, "prep": 3, "forward": 7, "pull": 2, "backward": 5, "grads": 2, "finish": 1}
 
 
 def call(body, name, out_shape, in_smem, in_any, n_in, scratch=(), out_smem=()):
@@ -405,6 +415,13 @@
     return lax.ppermute(value, axis, [(i, i ^ mask) for i in range(size)])
 
 
+def tap_places():
+    row = np.arange(KDIM)
+    place = np.zeros((KDIM, HALF), np.float32)
+    place[row, row // HALF * GW + row % GW] = 1.0
+    return jnp.asarray(place, BF)
+
+
 def cross(value, devices, slides, tile_mask, slide_mask):
     pairs = [
         (t * slides + k, (t ^ tile_mask) * slides + (k ^ slide_mask))
@@ -446,7 +463,7 @@
         [shape((PAY, CIN), BF), shape((PAY, CIN), BF), shape((META,), jnp.int32)],
         (), (0, 1, 2, 3), 4,
         [pltpu.SMEM(tile_count.shape, jnp.int32), pltpu.SMEM(joined.shape, jnp.int32),
-         pltpu.VMEM((2, CIN, PIX), BF), pltpu.VMEM((2, CIN, PIX), BF), pltpu.SemaphoreType.DMA((6,))],
+         pltpu.VMEM((SLOTS, CIN, PIX), BF), pltpu.VMEM((SLOTS, CIN, PIX), BF), pltpu.SemaphoreType.DMA((4,))],
         (2,),
     )(tile_count, joined, x, g)
     hops = [(i, i + 1) for i in range(1, devices - 1, 2)]
@@ -460,44 +477,51 @@
         (0,), (), 7,
     )(meta, x, w_reduce, w_expand, w_group.T, s1, b1)
 
-    lanes = (SLOTS + 1) * PIX
-    out, back, errc, slope_b, e_send, e_keep = call(
+    lanes = SLOTS * PIX
+    act, back, errc, slope_b, hid, edge, e_send, e_keep = call(
         functools.partial(forward_kernel, devices), "forward",
         [shape((SLOTS, CIN, PIX), BF), shape((SLOTS, CIN, PIX), F32), shape((CIN, lanes), BF),
-         shape((MID, lanes), F32), shape((HALF, CIN), BF), shape((HALF, CIN), BF)],
+         shape((MID, lanes), F32), shape((SLOTS + 2, MID, PIX), BF), shape((CIN, PIX), BF),
+         shape((HALF, CIN), BF), shape((HALF, CIN), BF)],
         (0,), (), 15,
-        [pltpu.VMEM((SLOTS + 1, MID, PIX), BF), pltpu.VMEM((2, KDIM, lanes), BF), pltpu.VMEM((MID, lanes), BF)],
+        [pltpu.VMEM((2, KDIM, lanes), BF), pltpu.VMEM((MID, lanes), BF)],
     )(meta, from_core, from_other, hid, w_reduce, s1, b1, dense, s2, b2, wet, s3, b3, x, g)
 
     e_core = swap(e_send, "tile", 1)
-    (errb,) = call(pull_kernel, "pull", [shape((SLOTS + 1, MID, PIX), BF)], (), (), 3)(w_expand, errc, slope_b)
+    (errb,) = call(
+        pull_kernel, "pull", [shape((SLOTS + 2, MID, PIX), BF)], (0,), (), 14,
+        [pltpu.VMEM((2, KDIM, PIX), BF), pltpu.VMEM((MID, PIX), BF), pltpu.VMEM((MID, PIX), F32)],
+    )(meta, from_core, from_other, hid, dense, s2, b2, wet, s3, b3, edge, w_expand, errc, slope_b)
     e_part = add_pair(e_keep, e_core)
     errb, e_part = lax.optimization_barrier((errb, e_part))
     e_part = halve(e_part, 2)
 
-    erra, r_send, r_keep = call(
-        functools.partial(backward_kernel, devices), "backward",
-        [shape((SLOTS, MID, PIX), BF), shape((2, HALF, CIN // 2 + PIX), BF), shape((2, HALF, CIN // 2 + PIX), BF)],
-        (0,), (), 6,
-        [pltpu.VMEM((2, KDIM, SLOTS * PIX), BF), pltpu.VMEM((MID, SLOTS * PIX), BF), pltpu.VMEM((MID, HALF), BF)],
-    )(meta, errb, hid, slope_a, denset, x)
-
-    (grad_in,) = call(
-        grad_kernel, "grads", [shape((SLOTS, CIN, PIX), BF)], (), (), 3,
-    )(w_reduce, erra, back)
-
-    r_core = swap(r_send, "tile", 1)
-    r_part = add_pair(r_keep, r_core)
-    quarter = HALF // 2
-    r_part = add_all(
-        r_part[0, :quarter],
-        cross(r_part[0, quarter:], devices, slides, 2, 0),
-        cross(r_part[1, :quarter], devices, slides, 0, 1),
-        cross(r_part[1, quarter:], devices, slides, 2, 1),
-    )
+    piece = [shape((HALF // 2, CIN // 2 + PIX), BF)] * 8
+    erra, *pieces = call(
+        functools.partial(backward_kernel, devices), "backward", [shape((SLOTS, MID, PIX), BF)] + piece,
+        (0,), (), 7,
+        [pltpu.VMEM((2, KDIM, lanes), BF), pltpu.VMEM((MID, lanes), BF), pltpu.VMEM((MID, HALF), BF),
+         pltpu.VMEM((HALF, KDIM), BF)],
+    )(meta, errb, hid, slope_a, denset, x, tap_places())
+    (grad_in, out) = call(
+        grad_kernel, "grads", [shape((SLOTS, CIN, PIX), BF), shape((SLOTS, CIN, PIX), BF)], (), (), 4,
+    )(w_reduce, erra, back, act)
+
+    r_core = [swap(value, "tile", 1) for value in pieces[:4]]
+    *r_core, e_part = lax.optimization_barrier((*r_core, e_part))
+    near, far_y, far_x, far_xy = (add_pair(a, b) for a, b in zip(pieces[4:], r_core))
+    one = cross(far_y, devices, slides, 2, 0)
+    two = cross(far_x, devices, slides, 0, 1)
+    three = cross(far_xy, devices, slides, 2, 1)
     mask = 4
     while mask < devices:
+        if 2 * mask == devices:
+            e_part, two = lax.optimization_barrier((e_part, two))
         e_part = halve(e_part, mask)
+        mask *= 2
+    r_part = add_all(near, one, two, three)
+    mask = 4
+    while mask < devices:
         r_part = halve(r_part, mask)
         mask *= 2
     mask = 2

time: 65 us -> 58.7 us (0.903)
  local copies, waits for them, and re-layouts: 3.9 us -> 0.75 us
  starting transfers between devices: 22.7 us -> 20.6 us
  Pallas kernels: 24 us -> 23.1 us
    unnamed x30 -> x28, local copies, waits for them, and re-layouts: 3.81 us -> 0.71 us
    pallas_call x2, Pallas kernels: 2.72 us -> 5.22 us  [the longest x1 3.13 us: shards(): call(pull_kernel, 'pull', [shape((SLOTS + 2, MID, PIX), BF)], (0,), (), 1...]
    ppermute x9 -> x12, waiting for transfers between devices: 12 us -> 9.63 us  [swap(): return lax.ppermute(value, axis, [(i, i ^ mask) for i in range(size)])]
    ppermute x3, waiting for transfers between devices: 0.6 us -> 2.93 us  [cross(): return lax.ppermute(value, ('tile', 'slide'), pairs)]
    pallas_call x1, Pallas kernels: 7.62 us -> 5.3 us  [shards(): call(functools.partial(backward_kernel, devices), 'backward', [shape((SLO...]
    ppermute x9 -> x12, starting transfers between devices: 18.5 us -> 16.2 us  [swap(): return lax.ppermute(value, axis, [(i, i ^ mask) for i in range(size)])]
    pallas_call x1, Pallas kernels: 8.28 us -> 6.15 us  [shards(): call(functools.partial(forward_kernel, devices), 'forward', [shape((SLOTS...]
    pallas_call x1, Pallas kernels: 1.74 us -> 2.85 us  [shards(): call(edge_kernel, 'edges', [shape((PAY, CIN), BF), shape((PAY, CIN), BF),...]
  transfers between devices with their start and end apart: 13 -> 16, of which waited for: 7 -> 11; matrix products, arithmetic and copies ran while one was open for 1% -> 0% of each run, Pallas kernels for 9% -> 23%
where the time goes in v3:
time: 58.7 us; the launch traced here: 58.6 us
  Pallas kernels  23.1 us (39%)
  starting transfers between devices  20.6 us (35%)
  waiting for transfers between devices  12.6 us (21%)
  between operations  0.97 us (2%)
  local copies, waits for them, and re-layouts  0.75 us (1%)
  other arithmetic  0.59 us (1%)
    ppermute x12, starting transfers between devices, swap(): return lax.ppermute(value, axis, [(i, i ^ mask) for i in range(size)])  16.2 us
    ppermute x12, waiting for transfers between devices, swap(): return lax.ppermute(value, axis, [(i, i ^ mask) for i in range(size)])  9.63 us
    pallas_call x1, Pallas kernels, shards(): call(functools.partial(forward_kernel, devices), 'forward', [shape((SLOTS...  6.15 us
    pallas_call x1, Pallas kernels, shards(): call(functools.partial(backward_kernel, devices), 'backward', [shape((SLO...  5.3 us
    ppermute x3, starting transfers between devices, cross(): return lax.ppermute(value, ('tile', 'slide'), pairs)  3.69 us
    pallas_call x1, Pallas kernels, shards(): call(pull_kernel, 'pull', [shape((SLOTS + 2, MID, PIX), BF)], (0,), (), 1...  3.13 us
    ppermute x3, waiting for transfers between devices, cross(): return lax.ppermute(value, ('tile', 'slide'), pairs)  2.93 us
    pallas_call x1, Pallas kernels, shards(): call(edge_kernel, 'edges', [shape((PAY, CIN), BF), shape((PAY, CIN), BF),...  2.85 us
  transfers between devices with their start and end apart: 16, of which 11 were waited for; matrix products, arithmetic and copies ran while one was open for 0% of the time, Pallas kernels for 23%

profile of v3, /device:TPU:0, one launch (start us, length us, event | category | flops | bytes accessed | tf_op | source)
XLA Modules:
  0.0 58.6 jit_solution(10455816650206225502)
XLA Ops:
  0.6 0.0 copy-start
  0.6 0.0 copy-start.8
  0.7 0.0 copy-start.9
  0.7 0.0 copy-start.10
  0.7 0.0 copy-start.11
  0.7 0.0 copy-start.12
  0.7 2.8 %edges.1 = (bf16[48,1024]{1,0:T(8,128)(2,1)}, bf16[48,1024]{1,0:T(8,128)(2,1)}, s32[16]{0:T(128)}) custom-call(s32[1,16]{1,0:T(1,128)} %count_hbm.1, s32[1,31]{1,0:T(1,128)} %joined_hbm.1, bf16[4,1024,128]{2,1,0:T(8,128)(2,1)} %bitcast.21, bf16[4,1024,128]{2,1,0:T(8,128)(2,1)} %bitcast.19), custom_call_target="tpu_custom_call" | custom-call | flops 2200000000 | bytes 1048576 | tf_op jit(solution)/shard_map/edges/pallas_call | solution.py:461
  3.5 0.5 collective-permute-start
  4.1 0.7 %collective-permute-start.1 = (bf16[48,1024]{1,0:T(8,128)(2,1)}, bf16[48,1024]{1,0:T(8,128)(2,1)S(1)}, u32[]{:S(2)}, u32[]{:S(2)}) collective-permute-start(bf16[48,1024]{1,0:T(8,128)(2,1)} %get-tuple-element.46), channel_id=1, source_target_pairs={{2,4},{6,8},{10,12},{14,16},{18,20},{22,24},{26,28},{4,2},{8,6},{1... | collective-permute-start | bytes 294920 | tf_op jit(solution)/shard_map/ppermute | solution.py:470
  4.7 0.0 copy-done
  4.7 0.0 copy-done.8
  4.8 0.0 copy-done.9
  4.8 0.0 copy-done.10
  4.8 0.0 copy-done.11
  4.8 0.0 copy-start.5
  4.8 0.6 %copy-done.5 = s32[16]{0:T(128)S(1)} copy-done((s32[16]{0:T(128)S(1)}, s32[16]{0:T(128)}, u32[]{:S(2)}) %copy-start.5) | copy-done | bytes 88
  5.5 0.0 copy-start.6
  5.5 0.0 copy-start.7
  5.5 2.8 %prep.1 = (bf16[4,512,128]{2,1,0:T(8,128)(2,1)S(1)}, f32[4,512,128]{2,1,0:T(8,128)S(1)}, bf16[2,256,2304]{2,1,0:T(8,128)(2,1)S(1)}, bf16[2,256,2304]{2,1,0:T(8,128)(2,1)S(1)}, bf16[1024,512]{1,0:T(8,128)(2,1)S(1)}) custom-call(s32[16]{0:T(128)S(1)} %copy-done.5, bf16[4,1024,128]{2,1,0:T(8,128)(2,1)S(1)} %bitcast.22, bf16[512,1024]{1,0:T(8,128)(2,1)S(1)} %copy-done.9, ...), custom_call_target="tpu_custom_call" | custom-call | flops 3300000000 | bytes 1048576 | tf_op jit(solution)/shard_map/prep/pallas_call | solution.py:473
  8.3 0.0 collective-permute-done.core_ref
  8.4 0.0 collective-permute-done.1.other_ref
  8.4 0.0 copy-done.1
  8.4 0.0 copy-done.2
  8.4 0.0 copy-done.3
  8.4 0.0 copy-done.4
  8.4 0.0 copy-done.6
  8.4 0.0 copy-done.7
  8.4 6.2 %forward.1 = (bf16[4,1024,128]{2,1,0:T(8,128)(2,1)S(1)}, f32[4,1024,128]{2,1,0:T(8,128)S(1)}, bf16[1024,512]{1,0:T(8,128)(2,1)S(1)}, f32[512,512]{1,0:T(8,128)S(...) custom-call(s32[16]{0:T(128)S(1)} %copy-done.6, ...), custom_call_target="tpu_custom_call" | custom-call | flops 7699999744 | bytes 1048576 | tf_op jit(solution)/shard_map/forward/pallas_call | solution.py:481
  14.6 4.0 %collective-permute-start.2 = (bf16[256,1024]{1,0:T(8,128)(2,1)S(1)}, bf16[256,1024]{1,0:T(8,128)(2,1)S(1)}, u32[]{:S(2)}, u32[]{:S(2)}) collective-permute-start(bf16[256,1024]{1,0:T(8,128)(2,1)S(1)} %get-tuple-element.55), channel_id=1, source_target_pairs={{0,2},{2,0},{4,6},{6,4},{8,10},{10,8},{12,14},{14,12},{16,18},{18,... | collective-permute-start | bytes 1572872 | tf_op jit(solution)/shard_map/ppermute | solution.py:415
  18.5 3.1 %pull.1.errb_ref = bf16[6,512,128]{2,1,0:T(8,128)(2,1)S(1)} custom-call(s32[16]{0:T(128)S(1)} %copy-done.6, bf16[48,1024]{1,0:T(8,128)(2,1)S(1)} %collective-permute-done.core_ref, bf16[48,1024]{1,0:T(8,128)(2,1)S(1)} %collective-permute-done.1.other_ref, bf16[6,512,128]{2,1,0:T(8,128)(2,1)S(1)} %get-tuple-element.50.hid_ref, ...), custom_call_target="tpu_custom_call" | custom-call | flops 2200000000 | bytes 1048576 | tf_op jit(solution)/shard_map/pull/pallas_call | solution.py:491
  21.7 0.0 collective-permute-done.2
  21.7 0.2 add_convert_fusion
  21.9 1.9 %collective-permute-start.7 = (bf16[128,1024]{1,0:T(8,128)(2,1)S(1)}, bf16[128,1024]{1,0:T(8,128)(2,1)S(1)}, u32[]{:S(2)}, u32[]{:S(2)}) collective-permute-start(bf16[128,1024]{1,0:T(8,128)(2,1)S(1)} %slice.31), channel_id=1, source_target_pairs={{0,4},{2,6},{4,0},{6,2},{8,12},{10,14},{12,8},{14,10},{16,20},{18,... | collective-permute-start | bytes 786440 | tf_op jit(solution)/shard_map/ppermute | solution.py:415
  23.8 0.0 copy-done.13
  23.8 5.3 %backward.1 = (bf16[4,512,128]{2,1,0:T(8,128)(2,1)S(1)}, bf16[128,640]{1,0:T(8,128)(2,1)S(1)}, bf16[128,640]{1,0:T(8,128)(2,1)S(1)}, bf16[128,640]{1,0:T(8,128)(...) custom-call(s32[16]{0:T(128)S(1)} %copy-done.6, ...), custom_call_target="tpu_custom_call" | custom-call | flops 5500000256 | bytes 1048576 | tf_op jit(solution)/shard_map/backward/pallas_call | solution.py:500
  29.1 0.1 collective-permute-start.3
  29.2 0.5 collective-permute-start.4
  29.7 0.1 collective-permute-start.5
  29.8 0.4 collective-permute-start.6
  30.2 0.1 collective-permute-done.7
  30.3 0.1 add_convert_fusion.1
  30.4 0.2 collective-permute-done.3
  30.6 0.2 collective-permute-done.4
  30.8 0.3 collective-permute-done.5
  31.1 0.2 collective-permute-done.6
  31.4 0.9 %collective-permute-start.11 = (bf16[128,640]{1,0:T(8,128)(2,1)S(1)}, bf16[128,640]{1,0:T(8,128)(2,1)S(1)}, u32[]{:S(2)}, u32[]{:S(2)}) collective-permute-start(bf16[128,640]{1,0:T(8,128)(2,1)S(1)} %add_convert_fusion.4), channel_id=1, source_target_pairs={{0,4},{1,5},{2,6},{3,7},{4,0},{5,1},{6,2},{7,3},{8,12},{9,13},{10,... | collective-permute-start | bytes 491528 | tf_op jit(solution)/shard_map/ppermute | solution.py:431
  32.3 2.2 %collective-permute-start.12 = (bf16[128,640]{1,0:T(8,128)(2,1)S(1)}, bf16[128,640]{1,0:T(8,128)(2,1)S(1)}, u32[]{:S(2)}, u32[]{:S(2)}) collective-permute-start(bf16[128,640]{1,0:T(8,128)(2,1)S(1)} %add_convert_fusion.3), channel_id=1, source_target_pairs={{0,5},{1,4},{2,7},{3,6},{4,1},{5,0},{6,3},{7,2},{8,13},{9,12},{10,... | collective-permute-start | bytes 491528 | tf_op jit(solution)/shard_map/ppermute | solution.py:431
  34.5 1.6 %collective-permute-start.8 = (bf16[64,1024]{1,0:T(8,128)(2,1)S(1)}, bf16[64,1024]{1,0:T(8,128)(2,1)S(1)}, u32[]{:S(2)}, u32[]{:S(2)}) collective-permute-start(bf16[64,1024]{1,0:T(8,128)(2,1)S(1)} %slice.33), channel_id=1, source_target_pairs={{0,8},{2,10},{4,12},{6,14},{8,0},{10,2},{12,4},{14,6},{16,24},{18,... | collective-permute-start | bytes 393224 | tf_op jit(solution)/shard_map/ppermute | solution.py:415
  36.2 0.6 %collective-permute-start.9 = (bf16[128,640]{1,0:T(8,128)(2,1)S(1)}, bf16[128,640]{1,0:T(8,128)(2,1)S(1)}, u32[]{:S(2)}, u32[]{:S(2)}) collective-permute-start(bf16[128,640]{1,0:T(8,128)(2,1)S(1)} %add_convert_fusion.6), channel_id=1, source_target_pairs={{0,1},{1,0},{2,3},{3,2},{4,5},{5,4},{6,7},{7,6},{8,9},{9,8},{10,11... | collective-permute-start | bytes 491528 | tf_op jit(solution)/shard_map/ppermute | solution.py:431
  36.8 2.9 %collective-permute-done.8 = bf16[64,1024]{1,0:T(8,128)(2,1)S(1)} collective-permute-done((bf16[64,1024]{1,0:T(8,128)(2,1)S(1)}, bf16[64,1024]{1,0:T(8,128)(2,1)S(1)}, u32[]{:S(2)}, u32[]{:S(2)}) %collective-permute-start.8) | collective-permute-done | bytes 131104 | tf_op jit(solution)/shard_map/ppermute | solution.py:415
  39.8 2.9 %collective-permute-done.9 = bf16[128,640]{1,0:T(8,128)(2,1)S(1)} collective-permute-done((bf16[128,640]{1,0:T(8,128)(2,1)S(1)}, bf16[128,640]{1,0:T(8,128)(2,1)S(1)}, u32[]{:S(2)}, u32[]{:S(2)}) %collective-permute-start.9) | collective-permute-done | bytes 163872 | tf_op jit(solution)/shard_map/ppermute | solution.py:431
  42.7 0.0 collective-permute-done.11
  42.7 0.0 collective-permute-done.12
  42.7 0.1 add_convert_fusion.2
  42.8 1.6 %collective-permute-start.13 = (bf16[64,640]{1,0:T(8,128)(2,1)S(1)}, bf16[64,640]{1,0:T(8,128)(2,1)S(1)}, u32[]{:S(2)}, u32[]{:S(2)}) collective-permute-start(bf16[64,640]{1,0:T(8,128)(2,1)S(1)} %slice.41), channel_id=1, source_target_pairs={{0,8},{2,10},{4,12},{6,14},{8,0},{10,2},{12,4},{14,6},{16,24},{18,... | collective-permute-start | bytes 245768 | tf_op jit(solution)/shard_map/ppermute | solution.py:415
  44.5 1.5 %collective-permute-start.10 = (bf16[32,1024]{1,0:T(8,128)(2,1)S(1)}, bf16[32,1024]{1,0:T(8,128)(2,1)S(1)}, u32[]{:S(2)}, u32[]{:S(2)}) collective-permute-start(bf16[32,1024]{1,0:T(8,128)(2,1)S(1)} %slice.35), channel_id=1, source_target_pairs={{0,16},{2,18},{4,20},{6,22},{8,24},{10,26},{12,28},{14,30},{16,0},... | collective-permute-start | bytes 196616 | tf_op jit(solution)/shard_map/ppermute | solution.py:415
  46.0 2.0 %collective-permute-done.13 = bf16[64,640]{1,0:T(8,128)(2,1)S(1)} collective-permute-done((bf16[64,640]{1,0:T(8,128)(2,1)S(1)}, bf16[64,640]{1,0:T(8,128)(2,1)S(1)}, u32[]{:S(2)}, u32[]{:S(2)}) %collective-permute-start.13) | collective-permute-done | bytes 81952 | tf_op jit(solution)/shard_map/ppermute | solution.py:415
  48.1 2.0 %collective-permute-start.14 = (bf16[32,640]{1,0:T(8,128)(2,1)S(1)}, bf16[32,640]{1,0:T(8,128)(2,1)S(1)}, u32[]{:S(2)}, u32[]{:S(2)}) collective-permute-start(bf16[32,640]{1,0:T(8,128)(2,1)S(1)} %slice.43), channel_id=1, source_target_pairs={{0,16},{2,18},{4,20},{6,22},{8,24},{10,26},{12,28},{14,30},{16,0},... | collective-permute-start | bytes 122888 | tf_op jit(solution)/shard_map/ppermute | solution.py:415
  50.0 1.2 %collective-permute-done.10 = bf16[32,1024]{1,0:T(8,128)(2,1)S(1)} collective-permute-done((bf16[32,1024]{1,0:T(8,128)(2,1)S(1)}, bf16[32,1024]{1,0:T(8,128)(2,1)S(1)}, u32[]{:S(2)}, u32[]{:S(2)}) %collective-permute-start.10) | collective-permute-done | bytes 65568 | tf_op jit(solution)/shard_map/ppermute | solution.py:415
  51.2 1.8 %collective-permute-done.14 = bf16[32,640]{1,0:T(8,128)(2,1)S(1)} collective-permute-done((bf16[32,640]{1,0:T(8,128)(2,1)S(1)}, bf16[32,640]{1,0:T(8,128)(2,1)S(1)}, u32[]{:S(2)}, u32[]{:S(2)}) %collective-permute-start.14) | collective-permute-done | bytes 40992 | tf_op jit(solution)/shard_map/ppermute | solution.py:415
  53.1 2.0 %collective-permute-start.15 = (bf16[32,1664]{1,0:T(8,128)(2,1)S(1)}, bf16[32,1664]{1,0:T(8,128)(2,1)S(1)}, u32[]{:S(2)}, u32[]{:S(2)}) collective-permute-start(bf16[32,1664]{1,0:T(8,128)(2,1)S(1)} %pad_maximum_fusion), channel_id=1, source_target_pairs={{0,1},{1,0},{2,3},{3,2},{4,5},{5,4},{6,7},{7,6},{8,9},{9,8},{10,11... | collective-permute-start | bytes 319496 | tf_op jit(solution)/shard_map/ppermute | solution.py:415
  55.1 2.1 %grads.1 = (bf16[4,1024,128]{2,1,0:T(8,128)(2,1)}, bf16[4,1024,128]{2,1,0:T(8,128)(2,1)}) custom-call(bf16[512,1024]{1,0:T(8,128)(2,1)S(1)} %copy-done.9, bf16[4,512,128]{2,1,0:T(8,128)(2,1)S(1)} %get-tuple-element.59.erra_ref, f32[4,1024,128]{2,1,0:T(8,128)S(1)} %get-tuple-element.60.back_ref, bf16[4,1024,128]{2,1,0:T(8,128)(2,1)S(1)} %get-tuple-element.61.act_ref), custom_call_target="tpu_custom_call" | custom-call | flops 2200000000 | bytes 1048576 | tf_op jit(solution)/shard_map/grads/pallas_call | solution.py:506
  57.2 0.7 %collective-permute-done.15.got_ref = bf16[32,1664]{1,0:T(8,128)(2,1)S(1)} collective-permute-done((bf16[32,1664]{1,0:T(8,128)(2,1)S(1)}, bf16[32,1664]{1,0:T(8,128)(2,1)S(1)}, u32[]{:S(2)}, u32[]{:S(2)}) %collective-permute-start.15) | collective-permute-done | bytes 106528 | tf_op jit(solution)/shard_map/ppermute | solution.py:415
  57.8 0.7 %finish.1 = (f32[32,1024]{1,0:T(8,128)}, f32[32,144]{1,0:T(8,128)}, f32[32,1024]{1,0:T(8,128)}) custom-call(bf16[32,1024]{1,0:T(8,128)(2,1)S(1)} %add_convert_fusion.9.e_ref, bf16[32,640]{1,0:T(8,128)(2,1)S(1)} %add_convert_fusion.10.r_ref, bf16[32,1664]{1,0:T(8,128)(2,1)S(1)} %collective-permute-done.15.got_ref), custom_call_target="tpu_custom_call" | custom-call | flops 1100000000 | bytes 1048576 | tf_op jit(solution)/shard_map/finish/pallas_call | solution.py:534
  (19 shorter events, 0.3 us)
Async XLA Ops:
  0.6 4.1 %copy-start = (bf16[512,1024]{1,0:T(8,128)(2,1)S(1)}, bf16[512,1024]{1,0:T(8,128)(2,1)}, u32[]{:S(2)}) copy-start(bf16[512,1024]{1,0:T(8,128)(2,1)} %we_ref.3) | copy-start | bytes 3145732
  0.6 4.1 %copy-start.8 = (bf16[1,4,1024,128]{3,2,1,0:T(8,128)(2,1)S(1)}, bf16[1,4,1024,128]{3,2,1,0:T(8,128)(2,1)}, u32[]{:S(2)}) copy-start(bf16[1,4,1024,128]{3,2,1,0:T(8,128)(2,1)} %param.14) | copy-start | bytes 3145732
  0.7 4.1 %copy-start.9 = (bf16[512,1024]{1,0:T(8,128)(2,1)S(1)}, bf16[512,1024]{1,0:T(8,128)(2,1)}, u32[]{:S(2)}) copy-start(bf16[512,1024]{1,0:T(8,128)(2,1)} %wr_ref.5) | copy-start | bytes 3145732
  0.7 4.1 %copy-start.10 = (bf16[512,144]{0,1:T(8,128)(2,1)S(1)}, bf16[512,144]{0,1:T(8,128)(2,1)}, u32[]{:S(2)}) copy-start(bf16[512,144]{0,1:T(8,128)(2,1)} %param.17) | copy-start | bytes 442372
  0.7 4.1 %copy-start.11 = (f32[512]{0:T(512)S(1)}, f32[512]{0:T(512)}, u32[]{:S(2)}) copy-start(f32[512]{0:T(512)} %param.19) | copy-start | bytes 6148
  0.7 4.1 %copy-start.12 = (f32[512]{0:T(512)S(1)}, f32[512]{0:T(512)}, u32[]{:S(2)}) copy-start(f32[512]{0:T(512)} %param.20) | copy-start | bytes 6148
  3.5 4.8 %collective-permute-start = (bf16[48,1024]{1,0:T(8,128)(2,1)}, bf16[48,1024]{1,0:T(8,128)(2,1)S(1)}, u32[]{:S(2)}, u32[]{:S(2)}) collective-permute-start(bf16[48,1024]{1,0:T(8,128)(2,1)} %get-tuple-element.45), channel_id=1, source_target_pairs={{0,2},{2,0},{4,6},{6,4},{8,10},{10,8},{12,14},{14,12},{16,18},{18,... | collective-permute-start | bytes 294920 | tf_op jit(solution)/shard_map/ppermute | solution.py:415
  4.1 4.3 %collective-permute-start.1 = (bf16[48,1024]{1,0:T(8,128)(2,1)}, bf16[48,1024]{1,0:T(8,128)(2,1)S(1)}, u32[]{:S(2)}, u32[]{:S(2)}) collective-permute-start(bf16[48,1024]{1,0:T(8,128)(2,1)} %get-tuple-element.46), channel_id=1, source_target_pairs={{2,4},{6,8},{10,12},{14,16},{18,20},{22,24},{26,28},{4,2},{8,6},{1... | collective-permute-start | bytes 294920 | tf_op jit(solution)/shard_map/ppermute | solution.py:470
  4.8 0.7 %copy-start.5 = (s32[16]{0:T(128)S(1)}, s32[16]{0:T(128)}, u32[]{:S(2)}) copy-start(s32[16]{0:T(128)} %get-tuple-element.44.meta_ref) | copy-start | bytes 196
  5.5 2.9 %copy-start.1 = (f32[1024]{0:T(1024)S(1)}, f32[1024]{0:T(1024)}, u32[]{:S(2)}) copy-start(f32[1024]{0:T(1024)} %param.23) | copy-start | bytes 12292
  5.5 2.9 %copy-start.2 = (f32[1024]{0:T(1024)S(1)}, f32[1024]{0:T(1024)}, u32[]{:S(2)}) copy-start(f32[1024]{0:T(1024)} %param.24) | copy-start | bytes 12292
  5.5 2.9 %copy-start.3 = (f32[512]{0:T(512)S(1)}, f32[512]{0:T(512)}, u32[]{:S(2)}) copy-start(f32[512]{0:T(512)} %param.21) | copy-start | bytes 6148
  5.5 2.9 %copy-start.4 = (f32[512]{0:T(512)S(1)}, f32[512]{0:T(512)}, u32[]{:S(2)}) copy-start(f32[512]{0:T(512)} %param.22) | copy-start | bytes 6148
  5.5 2.9 %copy-start.6 = (s32[16]{0:T(128)S(1)}, s32[16]{0:T(128)}, u32[]{:S(2)}) copy-start(s32[16]{0:T(128)} %get-tuple-element.44.meta_ref) | copy-start | bytes 196
  5.5 2.9 %copy-start.7 = (bf16[1,4,1024,128]{3,2,1,0:T(8,128)(2,1)S(1)}, bf16[1,4,1024,128]{3,2,1,0:T(8,128)(2,1)}, u32[]{:S(2)}) copy-start(bf16[1,4,1024,128]{3,2,1,0:T(8,128)(2,1)} %param.15) | copy-start | bytes 3145732
  14.6 7.1 %collective-permute-start.2 = (bf16[256,1024]{1,0:T(8,128)(2,1)S(1)}, bf16[256,1024]{1,0:T(8,128)(2,1)S(1)}, u32[]{:S(2)}, u32[]{:S(2)}) collective-permute-start(bf16[256,1024]{1,0:T(8,128)(2,1)S(1)} %get-tuple-element.55), channel_id=1, source_target_pairs={{0,2},{2,0},{4,6},{6,4},{8,10},{10,8},{12,14},{14,12},{16,18},{18,... | collective-permute-start | bytes 1572872 | tf_op jit(solution)/shard_map/ppermute | solution.py:415
  18.5 5.3 %copy-start.13 = (bf16[2304,256]{1,0:T(8,128)(2,1)S(1)}, bf16[2304,256]{1,0:T(8,128)(2,1)}, u32[]{:S(2)}) copy-start(bf16[2304,256]{1,0:T(8,128)(2,1)} %constant.2.clone.place_ref) | copy-start | bytes 3538948
  21.9 8.4 %collective-permute-start.7 = (bf16[128,1024]{1,0:T(8,128)(2,1)S(1)}, bf16[128,1024]{1,0:T(8,128)(2,1)S(1)}, u32[]{:S(2)}, u32[]{:S(2)}) collective-permute-start(bf16[128,1024]{1,0:T(8,128)(2,1)S(1)} %slice.31), channel_id=1, source_target_pairs={{0,4},{2,6},{4,0},{6,2},{8,12},{10,14},{12,8},{14,10},{16,20},{18,... | collective-permute-start | bytes 786440 | tf_op jit(solution)/shard_map/ppermute | solution.py:415
  29.1 1.5 %collective-permute-start.3 = (bf16[128,640]{1,0:T(8,128)(2,1)S(1)}, bf16[128,640]{1,0:T(8,128)(2,1)S(1)}, u32[]{:S(2)}, u32[]{:S(2)}) collective-permute-start(bf16[128,640]{1,0:T(8,128)(2,1)S(1)} %get-tuple-element.64), channel_id=1, source_target_pairs={{0,2},{2,0},{4,6},{6,4},{8,10},{10,8},{12,14},{14,12},{16,18},{18,... | collective-permute-start | bytes 491528 | tf_op jit(solution)/shard_map/ppermute | solution.py:415
  29.2 1.6 %collective-permute-start.4 = (bf16[128,640]{1,0:T(8,128)(2,1)S(1)}, bf16[128,640]{1,0:T(8,128)(2,1)S(1)}, u32[]{:S(2)}, u32[]{:S(2)}) collective-permute-start(bf16[128,640]{1,0:T(8,128)(2,1)S(1)} %get-tuple-element.65), channel_id=1, source_target_pairs={{0,2},{2,0},{4,6},{6,4},{8,10},{10,8},{12,14},{14,12},{16,18},{18,... | collective-permute-start | bytes 491528 | tf_op jit(solution)/shard_map/ppermute | solution.py:415
  29.7 1.4 %collective-permute-start.5 = (bf16[128,640]{1,0:T(8,128)(2,1)S(1)}, bf16[128,640]{1,0:T(8,128)(2,1)S(1)}, u32[]{:S(2)}, u32[]{:S(2)}) collective-permute-start(bf16[128,640]{1,0:T(8,128)(2,1)S(1)} %get-tuple-element.66), channel_id=1, source_target_pairs={{0,2},{2,0},{4,6},{6,4},{8,10},{10,8},{12,14},{14,12},{16,18},{18,... | collective-permute-start | bytes 491528 | tf_op jit(solution)/shard_map/ppermute | solution.py:415
  29.8 1.6 %collective-permute-start.6 = (bf16[128,640]{1,0:T(8,128)(2,1)S(1)}, bf16[128,640]{1,0:T(8,128)(2,1)S(1)}, u32[]{:S(2)}, u32[]{:S(2)}) collective-permute-start(bf16[128,640]{1,0:T(8,128)(2,1)S(1)} %get-tuple-element.67), channel_id=1, source_target_pairs={{0,2},{2,0},{4,6},{6,4},{8,10},{10,8},{12,14},{14,12},{16,18},{18,... | collective-permute-start | bytes 491528 | tf_op jit(solution)/shard_map/ppermute | solution.py:415
  31.4 11.3 %collective-permute-start.11 = (bf16[128,640]{1,0:T(8,128)(2,1)S(1)}, bf16[128,640]{1,0:T(8,128)(2,1)S(1)}, u32[]{:S(2)}, u32[]{:S(2)}) collective-permute-start(bf16[128,640]{1,0:T(8,128)(2,1)S(1)} %add_convert_fusion.4), channel_id=1, source_target_pairs={{0,4},{1,5},{2,6},{3,7},{4,0},{5,1},{6,2},{7,3},{8,12},{9,13},{10,... | collective-permute-start | bytes 491528 | tf_op jit(solution)/shard_map/ppermute | solution.py:431
  32.3 10.3 %collective-permute-start.12 = (bf16[128,640]{1,0:T(8,128)(2,1)S(1)}, bf16[128,640]{1,0:T(8,128)(2,1)S(1)}, u32[]{:S(2)}, u32[]{:S(2)}) collective-permute-start(bf16[128,640]{1,0:T(8,128)(2,1)S(1)} %add_convert_fusion.3), channel_id=1, source_target_pairs={{0,5},{1,4},{2,7},{3,6},{4,1},{5,0},{6,3},{7,2},{8,13},{9,12},{10,... | collective-permute-start | bytes 491528 | tf_op jit(solution)/shard_map/ppermute | solution.py:431
  34.5 5.2 %collective-permute-start.8 = (bf16[64,1024]{1,0:T(8,128)(2,1)S(1)}, bf16[64,1024]{1,0:T(8,128)(2,1)S(1)}, u32[]{:S(2)}, u32[]{:S(2)}) collective-permute-start(bf16[64,1024]{1,0:T(8,128)(2,1)S(1)} %slice.33), channel_id=1, source_target_pairs={{0,8},{2,10},{4,12},{6,14},{8,0},{10,2},{12,4},{14,6},{16,24},{18,... | collective-permute-start | bytes 393224 | tf_op jit(solution)/shard_map/ppermute | solution.py:415
  36.2 6.5 %collective-permute-start.9 = (bf16[128,640]{1,0:T(8,128)(2,1)S(1)}, bf16[128,640]{1,0:T(8,128)(2,1)S(1)}, u32[]{:S(2)}, u32[]{:S(2)}) collective-permute-start(bf16[128,640]{1,0:T(8,128)(2,1)S(1)} %add_convert_fusion.6), channel_id=1, source_target_pairs={{0,1},{1,0},{2,3},{3,2},{4,5},{5,4},{6,7},{7,6},{8,9},{9,8},{10,11... | collective-permute-start | bytes 491528 | tf_op jit(solution)/shard_map/ppermute | solution.py:431
  42.8 5.2 %collective-permute-start.13 = (bf16[64,640]{1,0:T(8,128)(2,1)S(1)}, bf16[64,640]{1,0:T(8,128)(2,1)S(1)}, u32[]{:S(2)}, u32[]{:S(2)}) collective-permute-start(bf16[64,640]{1,0:T(8,128)(2,1)S(1)} %slice.41), channel_id=1, source_target_pairs={{0,8},{2,10},{4,12},{6,14},{8,0},{10,2},{12,4},{14,6},{16,24},{18,... | collective-permute-start | bytes 245768 | tf_op jit(solution)/shard_map/ppermute | solution.py:415
  44.5 6.7 %collective-permute-start.10 = (bf16[32,1024]{1,0:T(8,128)(2,1)S(1)}, bf16[32,1024]{1,0:T(8,128)(2,1)S(1)}, u32[]{:S(2)}, u32[]{:S(2)}) collective-permute-start(bf16[32,1024]{1,0:T(8,128)(2,1)S(1)} %slice.35), channel_id=1, source_target_pairs={{0,16},{2,18},{4,20},{6,22},{8,24},{10,26},{12,28},{14,30},{16,0},... | collective-permute-start | bytes 196616 | tf_op jit(solution)/shard_map/ppermute | solution.py:415
  48.1 5.0 %collective-permute-start.14 = (bf16[32,640]{1,0:T(8,128)(2,1)S(1)}, bf16[32,640]{1,0:T(8,128)(2,1)S(1)}, u32[]{:S(2)}, u32[]{:S(2)}) collective-permute-start(bf16[32,640]{1,0:T(8,128)(2,1)S(1)} %slice.43), channel_id=1, source_target_pairs={{0,16},{2,18},{4,20},{6,22},{8,24},{10,26},{12,28},{14,30},{16,0},... | collective-permute-start | bytes 122888 | tf_op jit(solution)/shard_map/ppermute | solution.py:415
  53.1 4.8 %collective-permute-start.15 = (bf16[32,1664]{1,0:T(8,128)(2,1)S(1)}, bf16[32,1664]{1,0:T(8,128)(2,1)S(1)}, u32[]{:S(2)}, u32[]{:S(2)}) collective-permute-start(bf16[32,1664]{1,0:T(8,128)(2,1)S(1)} %pad_maximum_fusion), channel_id=1, source_target_pairs={{0,1},{1,0},{2,3},{3,2},{4,5},{5,4},{6,7},{7,6},{8,9},{9,8},{10,11... | collective-permute-start | bytes 319496 | tf_op jit(solution)/shard_map/ppermute | solution.py:415

commit v4 on v3

--- a/solution.py
+++ b/solution.py
@@ -320,7 +320,6 @@
     send_refs, keep_refs = rest[:4], rest[4:8]
     win_ref, flat_ref, groups_ref, kept_ref = rest[8:]
     me = lax.axis_index("tile")
-    side = lax.axis_index("slide") % 2
     for first, count in CHUNKS:
         build_windows(errb_ref, win_ref, meta_ref, range(first, first + count), 0, True)
         lanes = slice(first * PIX, (first + count) * PIX)
@@ -342,24 +341,17 @@
             full = nn_dot(win_ref[b, k * HALF : (k + 1) * HALF, :], hid)
             kept_ref[:, k * HALF : (k + 1) * HALF] = jnp.where(same, full, 0.0).astype(BF)
         groups_ref[rows, :] = nn_dot(kept_ref[...], place_ref[...]).astype(BF)
-    width = CIN // 2
-    tiles = [
-        jnp.concatenate([x_ref[i, pl.ds(pl.multiple_of((side ^ dx) * width, width), width), :] for i in range(SLOTS)], axis=1)
-        for dx in range(2)
-    ]
-    quarter = HALF // 2
+    tiles = jnp.concatenate([x_ref[i] for i in range(SLOTS)], axis=1)
+    count = HALF // 4
     for refs, flip in ((send_refs, 1), (keep_refs, 0)):
         blocks = row_blocks(devices, me, flip)
         rows = jnp.concatenate([flat_ref[at, :] for at in blocks], axis=0)
         group_rows = jnp.concatenate([groups_ref[at, :] for at in blocks], axis=0)
-        low, high = group_rows[:, :PIX], group_rows[:, PIX:]
-        for dx in range(2):
-            part = nt_dot(rows, tiles[dx]).astype(BF)
-            group_part = jnp.where(side == dx, low, high)
-            for dy in range(2):
-                at = slice(dy * quarter, (dy + 1) * quarter)
-                refs[2 * dx + dy][:, :width] = part[at]
-                refs[2 * dx + dy][:, width:] = group_part[at]
+        part = nt_dot(rows, tiles).astype(BF)
+        for k in range(4):
+            at = slice(k * count, (k + 1) * count)
+            refs[k][:, :CIN] = part[at]
+            refs[k][:, CIN:] = group_rows[at]
 
 
 def grad_kernel(wr_ref, erra_ref, back_ref, act_ref, grad_ref, out_ref):
@@ -372,18 +364,12 @@
             grad_ref[i] = (pulled[:, k * PIX : (k + 1) * PIX] + back_ref[i]).astype(BF)
 
 
-def finish_kernel(norm, e_ref, r_ref, got_ref, reduce_ref, group_ref, expand_ref):
-    width = CIN // 2
-    own = r_ref[...].astype(F32) * norm
-    other = got_ref[:, CIN:].astype(F32) * norm
-    expand_ref[...] = (e_ref[...].astype(F32) + got_ref[:, :CIN].astype(F32)) * norm
-    even = lax.axis_index("slide") % 2 == 0
-    low = jnp.where(even, own, other)
-    high = jnp.where(even, other, own)
-    reduce_ref[:, :width] = low[:, :width]
-    reduce_ref[:, width:] = high[:, :width]
-    group_ref[:, :PIX] = low[:, width:]
-    group_ref[:, PIX:] = high[:, width : width + TAPS * GW - PIX]
+def finish_kernel(norm, ea_ref, eb_ref, *refs):
+    parts, (reduce_ref, group_ref, expand_ref) = refs[:4], refs[4:]
+    expand_ref[...] = (ea_ref[...].astype(F32) + eb_ref[...].astype(F32)) * norm
+    total = sum(part[...].astype(F32) for part in parts) * norm
+    reduce_ref[...] = total[:, :CIN]
+    group_ref[...] = total[:, CIN : CIN + TAPS * GW]
 
 
 LIMITS = {"edges": 56, "prep": 13, "forward": 26, "pull": 14, "backward": 18, "grads": 9, "finish": 2}
@@ -431,6 +417,13 @@
     return lax.ppermute(value, ("tile", "slide"), pairs)
 
 
+def spread(part, devices, slides):
+    rows = part.shape[0] // 4
+    return [part[:rows]] + [
+        cross(part[k * rows : (k + 1) * rows], devices, slides, 2 * (k // 2 + 2 * (k % 2)), 0) for k in (1, 2, 3)
+    ]
+
+
 def add_all(first, *others):
     total = first.astype(F32)
     for other in others:
@@ -496,7 +489,7 @@
     errb, e_part = lax.optimization_barrier((errb, e_part))
     e_part = halve(e_part, 2)
 
-    piece = [shape((HALF // 2, CIN // 2 + PIX), BF)] * 8
+    piece = [shape((HALF // 4, CIN + HALF), BF)] * 8
     erra, *pieces = call(
         functools.partial(backward_kernel, devices), "backward", [shape((SLOTS, MID, PIX), BF)] + piece,
         (0,), (), 7,
@@ -509,32 +502,40 @@
 
     r_core = [swap(value, "tile", 1) for value in pieces[:4]]
     *r_core, e_part = lax.optimization_barrier((*r_core, e_part))
-    near, far_y, far_x, far_xy = (add_pair(a, b) for a, b in zip(pieces[4:], r_core))
-    one = cross(far_y, devices, slides, 2, 0)
-    two = cross(far_x, devices, slides, 0, 1)
-    three = cross(far_xy, devices, slides, 2, 1)
+    r_parts = [add_pair(a, b) for a, b in zip(pieces[4:], r_core)]
+    r_parts = [r_parts[0]] + [cross(r_parts[k], devices, slides, 2 * (k // 2 + 2 * (k % 2)), 0) for k in (1, 2, 3)]
     mask = 4
     while mask < devices:
-        if 2 * mask == devices:
-            e_part, two = lax.optimization_barrier((e_part, two))
         e_part = halve(e_part, mask)
         mask *= 2
-    r_part = add_all(near, one, two, three)
-    mask = 4
-    while mask < devices:
+    r_part = add_all(*r_parts)
+    mask = 8
+    while 2 * mask < devices:
         r_part = halve(r_part, mask)
         mask *= 2
-    mask = 2
-    while mask < slides:
-        e_part = add_pair(e_part, swap(e_part, "slide", mask))
-        r_part = add_pair(r_part, swap(r_part, "slide", mask))
-        mask *= 2
-    got = swap(jnp.concatenate([e_part, r_part], axis=1), "slide", 1)
+    mine, theirs = r_part[:per], r_part[per:]
+    both = cross(jnp.concatenate([mine, e_part], axis=1), devices, slides, 0, 1)
+    e_other = both[:, CIN + HALF :]
+    finals = [
+        mine,
+        both[:, : CIN + HALF],
+        cross(theirs, devices, slides, devices // 2, 0),
+        cross(theirs, devices, slides, devices // 2, 1),
+    ]
+    if slides > 2:
+        e_part, e_other = add_pair(e_part, e_other), jnp.zeros_like(e_part)
+        total = add_all(*finals)
+        mask = 2
+        while mask < slides:
+            e_part = add_pair(e_part, swap(e_part, "slide", mask))
+            total = add_pair(total, swap(total, "slide", mask))
+            mask *= 2
+        finals = [total] + [jnp.zeros_like(total)] * 3
     norm = 1.0 / math.sqrt(slides * LIVE_DEV * devices * PIX)
     grad_reduce, grad_group, grad_expand = call(
         functools.partial(finish_kernel, norm), "finish",
-        [shape((per, CIN), F32), shape((per, TAPS * GW), F32), shape((per, CIN), F32)], (), (), 3,
-    )(e_part, r_part, got)
+        [shape((per, CIN), F32), shape((per, TAPS * GW), F32), shape((per, CIN), F32)], (), (), 6,
+    )(e_part, e_other, *finals)
     return (out[None], grad_in[None], grad_reduce, grad_group, grad_expand)
 
 

time: 58.7 us -> 56.6 us (0.964)
  waiting for transfers between devices: 12.6 us -> 10.5 us
    ppermute x3 -> x6, starting transfers between devices: 3.69 us -> 9.31 us  [cross(): return lax.ppermute(value, ('tile', 'slide'), pairs)]
    ppermute x12 -> x9, starting transfers between devices: 16.2 us -> 10.6 us  [swap(): return lax.ppermute(value, axis, [(i, i ^ mask) for i in range(size)])]
    ppermute x12 -> x9, waiting for transfers between devices: 9.63 us -> 5.53 us  [swap(): return lax.ppermute(value, axis, [(i, i ^ mask) for i in range(size)])]
    ppermute x3 -> x6, waiting for transfers between devices: 2.93 us -> 4.95 us  [cross(): return lax.ppermute(value, ('tile', 'slide'), pairs)]
  transfers between devices with their start and end apart: 16 -> 16, of which waited for: 11 -> 9; matrix products, arithmetic and copies ran while one was open for 0% -> 1% of each run, Pallas kernels for 23% -> 24%
where the time goes in v4:
time: 56.6 us; the launch traced here: 56.5 us
  Pallas kernels  23.1 us (41%)
  starting transfers between devices  20.6 us (36%)
  waiting for transfers between devices  10.5 us (19%)
  between operations  0.98 us (2%)
  local copies, waits for them, and re-layouts  0.77 us (1%)
    ppermute x9, starting transfers between devices, swap(): return lax.ppermute(value, axis, [(i, i ^ mask) for i in range(size)])  10.6 us
    ppermute x6, starting transfers between devices, cross(): return lax.ppermute(value, ('tile', 'slide'), pairs)  9.31 us
    pallas_call x1, Pallas kernels, shards(): call(functools.partial(forward_kernel, devices), 'forward', [shape((SLOTS...  6.16 us
    ppermute x9, waiting for transfers between devices, swap(): return lax.ppermute(value, axis, [(i, i ^ mask) for i in range(size)])  5.53 us
    pallas_call x1, Pallas kernels, shards(): call(functools.partial(backward_kernel, devices), 'backward', [shape((SLO...  5.3 us
    ppermute x6, waiting for transfers between devices, cross(): return lax.ppermute(value, ('tile', 'slide'), pairs)  4.95 us
    pallas_call x1, Pallas kernels, shards(): call(pull_kernel, 'pull', [shape((SLOTS + 2, MID, PIX), BF)], (0,), (), 1...  3.13 us
    pallas_call x1, Pallas kernels, shards(): call(edge_kernel, 'edges', [shape((PAY, CIN), BF), shape((PAY, CIN), BF),...  2.85 us
  transfers between devices with their start and end apart: 16, of which 9 were waited for; matrix products, arithmetic and copies ran while one was open for 1% of the time, Pallas kernels for 24%

profile of v4, /device:TPU:0, one launch (start us, length us, event | category | flops | bytes accessed | tf_op | source)
XLA Modules:
  0.0 56.5 jit_solution(9019596389613186070)
XLA Ops:
  0.6 0.0 copy-start
  0.6 0.0 copy-start.8
  0.7 0.0 copy-start.9
  0.7 0.0 copy-start.10
  0.7 0.0 copy-start.11
  0.7 0.0 copy-start.12
  0.7 2.8 %edges.1 = (bf16[48,1024]{1,0:T(8,128)(2,1)}, bf16[48,1024]{1,0:T(8,128)(2,1)}, s32[16]{0:T(128)}) custom-call(s32[1,16]{1,0:T(1,128)} %count_hbm.1, s32[1,31]{1,0:T(1,128)} %joined_hbm.1, bf16[4,1024,128]{2,1,0:T(8,128)(2,1)} %bitcast.21, bf16[4,1024,128]{2,1,0:T(8,128)(2,1)} %bitcast.19), custom_call_target="tpu_custom_call" | custom-call | flops 2200000000 | bytes 1048576 | tf_op jit(solution)/shard_map/edges/pallas_call | solution.py:454
  3.5 0.5 collective-permute-start
  4.1 0.7 %collective-permute-start.1 = (bf16[48,1024]{1,0:T(8,128)(2,1)}, bf16[48,1024]{1,0:T(8,128)(2,1)S(1)}, u32[]{:S(2)}, u32[]{:S(2)}) collective-permute-start(bf16[48,1024]{1,0:T(8,128)(2,1)} %get-tuple-element.44), channel_id=1, source_target_pairs={{2,4},{6,8},{10,12},{14,16},{18,20},{22,24},{26,28},{4,2},{8,6},{1... | collective-permute-start | bytes 294920 | tf_op jit(solution)/shard_map/ppermute | solution.py:463
  4.7 0.0 copy-done
  4.7 0.0 copy-done.8
  4.8 0.0 copy-done.9
  4.8 0.0 copy-done.10
  4.8 0.0 copy-done.11
  4.8 0.0 copy-done.12
  4.8 0.0 copy-start.5
  4.8 0.6 %copy-done.5 = s32[16]{0:T(128)S(1)} copy-done((s32[16]{0:T(128)S(1)}, s32[16]{0:T(128)}, u32[]{:S(2)}) %copy-start.5) | copy-done | bytes 88
  5.5 0.0 copy-start.6
  5.5 0.0 copy-start.7
  5.5 2.8 %prep.1 = (bf16[4,512,128]{2,1,0:T(8,128)(2,1)S(1)}, f32[4,512,128]{2,1,0:T(8,128)S(1)}, bf16[2,256,2304]{2,1,0:T(8,128)(2,1)S(1)}, bf16[2,256,2304]{2,1,0:T(8,128)(2,1)S(1)}, bf16[1024,512]{1,0:T(8,128)(2,1)S(1)}) custom-call(s32[16]{0:T(128)S(1)} %copy-done.5, bf16[4,1024,128]{2,1,0:T(8,128)(2,1)S(1)} %bitcast.22, bf16[512,1024]{1,0:T(8,128)(2,1)S(1)} %copy-done.9, ...), custom_call_target="tpu_custom_call" | custom-call | flops 3300000000 | bytes 1048576 | tf_op jit(solution)/shard_map/prep/pallas_call | solution.py:466
  8.3 0.0 collective-permute-done.core_ref
  8.4 0.0 collective-permute-done.1.other_ref
  8.4 0.0 copy-done.1
  8.4 0.0 copy-done.2
  8.4 0.0 copy-done.3
  8.4 0.0 copy-done.4
  8.4 0.0 copy-done.6
  8.4 0.0 copy-done.7
  8.4 6.2 %forward.1 = (bf16[4,1024,128]{2,1,0:T(8,128)(2,1)S(1)}, f32[4,1024,128]{2,1,0:T(8,128)S(1)}, bf16[1024,512]{1,0:T(8,128)(2,1)S(1)}, f32[512,512]{1,0:T(8,128)S(...) custom-call(s32[16]{0:T(128)S(1)} %copy-done.6, ...), custom_call_target="tpu_custom_call" | custom-call | flops 7699999744 | bytes 1048576 | tf_op jit(solution)/shard_map/forward/pallas_call | solution.py:474
  14.6 3.9 %collective-permute-start.2 = (bf16[256,1024]{1,0:T(8,128)(2,1)S(1)}, bf16[256,1024]{1,0:T(8,128)(2,1)S(1)}, u32[]{:S(2)}, u32[]{:S(2)}) collective-permute-start(bf16[256,1024]{1,0:T(8,128)(2,1)S(1)} %get-tuple-element.53), channel_id=1, source_target_pairs={{0,2},{2,0},{4,6},{6,4},{8,10},{10,8},{12,14},{14,12},{16,18},{18,... | collective-permute-start | bytes 1572872 | tf_op jit(solution)/shard_map/ppermute | solution.py:401
  18.5 3.1 %pull.1.errb_ref = bf16[6,512,128]{2,1,0:T(8,128)(2,1)S(1)} custom-call(s32[16]{0:T(128)S(1)} %copy-done.6, bf16[48,1024]{1,0:T(8,128)(2,1)S(1)} %collective-permute-done.core_ref, bf16[48,1024]{1,0:T(8,128)(2,1)S(1)} %collective-permute-done.1.other_ref, bf16[6,512,128]{2,1,0:T(8,128)(2,1)S(1)} %get-tuple-element.48.hid_ref, ...), custom_call_target="tpu_custom_call" | custom-call | flops 2200000000 | bytes 1048576 | tf_op jit(solution)/shard_map/pull/pallas_call | solution.py:484
  21.7 0.0 collective-permute-done.2
  21.7 0.2 add_convert_fusion
  21.9 1.9 %collective-permute-start.7 = (bf16[128,1024]{1,0:T(8,128)(2,1)S(1)}, bf16[128,1024]{1,0:T(8,128)(2,1)S(1)}, u32[]{:S(2)}, u32[]{:S(2)}) collective-permute-start(bf16[128,1024]{1,0:T(8,128)(2,1)S(1)} %slice.31), channel_id=1, source_target_pairs={{0,4},{2,6},{4,0},{6,2},{8,12},{10,14},{12,8},{14,10},{16,20},{18,... | collective-permute-start | bytes 786440 | tf_op jit(solution)/shard_map/ppermute | solution.py:401
  23.8 5.3 %backward.1 = (bf16[4,512,128]{2,1,0:T(8,128)(2,1)S(1)}, bf16[64,1280]{1,0:T(8,128)(2,1)S(1)}, bf16[64,1280]{1,0:T(8,128)(2,1)S(1)}, bf16[64,1280]{1,0:T(8,128)(...) custom-call(s32[16]{0:T(128)S(1)} %copy-done.6, ...), custom_call_target="tpu_custom_call" | custom-call | flops 5500000256 | bytes 1048576 | tf_op jit(solution)/shard_map/backward/pallas_call | solution.py:493
  29.1 0.1 collective-permute-start.3
  29.2 0.5 collective-permute-start.4
  29.7 0.1 collective-permute-start.5
  29.8 0.4 collective-permute-start.6
  30.2 0.1 collective-permute-done.7
  30.3 0.1 add_convert_fusion.1
  30.4 0.2 collective-permute-done.3
  30.6 0.2 collective-permute-done.4
  30.8 0.3 collective-permute-done.5
  31.1 0.2 collective-permute-done.6
  31.4 1.6 %collective-permute-start.10 = (bf16[64,1280]{1,0:T(8,128)(2,1)S(1)}, bf16[64,1280]{1,0:T(8,128)(2,1)S(1)}, u32[]{:S(2)}, u32[]{:S(2)}) collective-permute-start(bf16[64,1280]{1,0:T(8,128)(2,1)S(1)} %add_convert_fusion.5), channel_id=1, source_target_pairs={{0,8},{1,9},{2,10},{3,11},{4,12},{5,13},{6,14},{7,15},{8,0},{9,1},... | collective-permute-start | bytes 491528 | tf_op jit(solution)/shard_map/ppermute | solution.py:417
  33.1 0.9 %collective-permute-start.11 = (bf16[64,1280]{1,0:T(8,128)(2,1)S(1)}, bf16[64,1280]{1,0:T(8,128)(2,1)S(1)}, u32[]{:S(2)}, u32[]{:S(2)}) collective-permute-start(bf16[64,1280]{1,0:T(8,128)(2,1)S(1)} %add_convert_fusion.4), channel_id=1, source_target_pairs={{0,4},{1,5},{2,6},{3,7},{4,0},{5,1},{6,2},{7,3},{8,12},{9,13},{10,... | collective-permute-start | bytes 491528 | tf_op jit(solution)/shard_map/ppermute | solution.py:417
  34.0 0.5 collective-permute-start.8
  34.6 2.2 %collective-permute-start.12 = (bf16[64,1280]{1,0:T(8,128)(2,1)S(1)}, bf16[64,1280]{1,0:T(8,128)(2,1)S(1)}, u32[]{:S(2)}, u32[]{:S(2)}) collective-permute-start(bf16[64,1280]{1,0:T(8,128)(2,1)S(1)} %add_convert_fusion.3), channel_id=1, source_target_pairs={{0,12},{1,13},{2,14},{3,15},{4,8},{5,9},{6,10},{7,11},{8,4},{9,5},... | collective-permute-start | bytes 491528 | tf_op jit(solution)/shard_map/ppermute | solution.py:417
  36.8 4.5 %collective-permute-done.8 = bf16[64,1024]{1,0:T(8,128)(2,1)S(1)} collective-permute-done((bf16[64,1024]{1,0:T(8,128)(2,1)S(1)}, bf16[64,1024]{1,0:T(8,128)(2,1)S(1)}, u32[]{:S(2)}, u32[]{:S(2)}) %collective-permute-start.8) | collective-permute-done | bytes 131104 | tf_op jit(solution)/shard_map/ppermute | solution.py:401
  41.3 2.6 %collective-permute-start.9 = (bf16[32,1024]{1,0:T(8,128)(2,1)S(1)}, bf16[32,1024]{1,0:T(8,128)(2,1)S(1)}, u32[]{:S(2)}, u32[]{:S(2)}) collective-permute-start(bf16[32,1024]{1,0:T(8,128)(2,1)S(1)} %slice.41), channel_id=1, source_target_pairs={{0,16},{2,18},{4,20},{6,22},{8,24},{10,26},{12,28},{14,30},{16,0},... | collective-permute-start | bytes 196616 | tf_op jit(solution)/shard_map/ppermute | solution.py:401
  44.0 0.0 collective-permute-done.10
  44.0 0.0 collective-permute-done.11
  44.0 0.8 %collective-permute-done.12 = bf16[64,1280]{1,0:T(8,128)(2,1)S(1)} collective-permute-done((bf16[64,1280]{1,0:T(8,128)(2,1)S(1)}, bf16[64,1280]{1,0:T(8,128)(2,1)S(1)}, u32[]{:S(2)}, u32[]{:S(2)}) %collective-permute-start.12) | collective-permute-done | bytes 163872 | tf_op jit(solution)/shard_map/ppermute | solution.py:417
  44.8 0.1 add_convert_fusion.2
  44.9 2.8 %collective-permute-start.14 = (bf16[32,1280]{1,0:T(8,128)(2,1)S(1)}, bf16[32,1280]{1,0:T(8,128)(2,1)S(1)}, u32[]{:S(2)}, u32[]{:S(2)}) collective-permute-start(bf16[32,1280]{1,0:T(8,128)(2,1)S(1)} %get-tuple-element.79), channel_id=1, source_target_pairs={{0,16},{1,17},{2,18},{3,19},{4,20},{5,21},{6,22},{7,23},{8,24},{9,... | collective-permute-start | bytes 245768 | tf_op jit(solution)/shard_map/ppermute | solution.py:417
  47.7 1.1 %collective-permute-start.15 = (bf16[32,1280]{1,0:T(8,128)(2,1)S(1)}, bf16[32,1280]{1,0:T(8,128)(2,1)S(1)}, u32[]{:S(2)}, u32[]{:S(2)}) collective-permute-start(bf16[32,1280]{1,0:T(8,128)(2,1)S(1)} %get-tuple-element.79), channel_id=1, source_target_pairs={{0,17},{1,16},{2,19},{3,18},{4,21},{5,20},{6,23},{7,22},{8,25},{9,... | collective-permute-start | bytes 245768 | tf_op jit(solution)/shard_map/ppermute | solution.py:417
  48.8 0.0 collective-permute-done.9
  48.9 0.6 %collective-permute-start.13 = (bf16[32,2304]{1,0:T(8,128)(2,1)S(1)}, bf16[32,2304]{1,0:T(8,128)(2,1)S(1)}, u32[]{:S(2)}, u32[]{:S(2)}) collective-permute-start(bf16[32,2304]{1,0:T(8,128)(2,1)S(1)} %pad_maximum_fusion), channel_id=1, source_target_pairs={{0,1},{1,0},{2,3},{3,2},{4,5},{5,4},{6,7},{7,6},{8,9},{9,8},{10,11... | collective-permute-start | bytes 442376 | tf_op jit(solution)/shard_map/ppermute | solution.py:417
  49.5 2.1 %grads.1 = (bf16[4,1024,128]{2,1,0:T(8,128)(2,1)}, bf16[4,1024,128]{2,1,0:T(8,128)(2,1)}) custom-call(bf16[512,1024]{1,0:T(8,128)(2,1)S(1)} %copy-done.9, bf16[4,512,128]{2,1,0:T(8,128)(2,1)S(1)} %get-tuple-element.57.erra_ref, f32[4,1024,128]{2,1,0:T(8,128)S(1)} %get-tuple-element.58.back_ref, bf16[4,1024,128]{2,1,0:T(8,128)(2,1)S(1)} %get-tuple-element.59.act_ref), custom_call_target="tpu_custom_call" | custom-call | flops 2200000000 | bytes 1048576 | tf_op jit(solution)/shard_map/grads/pallas_call | solution.py:499
  51.6 2.9 %collective-permute-done.13 = bf16[32,2304]{1,0:T(8,128)(2,1)S(1)} collective-permute-done((bf16[32,2304]{1,0:T(8,128)(2,1)S(1)}, bf16[32,2304]{1,0:T(8,128)(2,1)S(1)}, u32[]{:S(2)}, u32[]{:S(2)}) %collective-permute-start.13) | collective-permute-done | bytes 147488 | tf_op jit(solution)/shard_map/ppermute | solution.py:417
  54.5 0.0 collective-permute-done.14.refs_2_
  54.5 1.3 %collective-permute-done.15.refs_3_ = bf16[32,1280]{1,0:T(8,128)(2,1)S(1)} collective-permute-done((bf16[32,1280]{1,0:T(8,128)(2,1)S(1)}, bf16[32,1280]{1,0:T(8,128)(2,1)S(1)}, u32[]{:S(2)}, u32[]{:S(2)}) %collective-permute-start.15) | collective-permute-done | bytes 81952 | tf_op jit(solution)/shard_map/ppermute | solution.py:417
  55.8 0.7 %finish.1 = (f32[32,1024]{1,0:T(8,128)}, f32[32,144]{1,0:T(8,128)}, f32[32,1024]{1,0:T(8,128)}) custom-call(bf16[32,1024]{1,0:T(8,128)(2,1)S(1)} %add_convert_fusion.8.ea_ref, bf16[32,1024]{1,0:T(8,128)(2,1)S(1)} %slice.43.eb_ref, bf16[32,1280]{1,0:T(8,128)(2,1)S(1)} %get-tuple-element.80.refs_0_, bf16[32,1280]{1,0:T(8,128)(2,1)S(1)} %slice.44.refs_1_, ...), custom_call_target="tpu_custom_call" | custom-call | flops 1100000000 | bytes 1048576 | tf_op jit(solution)/shard_map/finish/pallas_call | solution.py:535
  (18 shorter events, 0.3 us)
Async XLA Ops:
  0.6 4.1 %copy-start = (bf16[512,1024]{1,0:T(8,128)(2,1)S(1)}, bf16[512,1024]{1,0:T(8,128)(2,1)}, u32[]{:S(2)}) copy-start(bf16[512,1024]{1,0:T(8,128)(2,1)} %we_ref.3) | copy-start | bytes 3145732
  0.6 4.1 %copy-start.8 = (bf16[1,4,1024,128]{3,2,1,0:T(8,128)(2,1)S(1)}, bf16[1,4,1024,128]{3,2,1,0:T(8,128)(2,1)}, u32[]{:S(2)}) copy-start(bf16[1,4,1024,128]{3,2,1,0:T(8,128)(2,1)} %param.14) | copy-start | bytes 3145732
  0.7 4.1 %copy-start.9 = (bf16[512,1024]{1,0:T(8,128)(2,1)S(1)}, bf16[512,1024]{1,0:T(8,128)(2,1)}, u32[]{:S(2)}) copy-start(bf16[512,1024]{1,0:T(8,128)(2,1)} %wr_ref.5) | copy-start | bytes 3145732
  0.7 4.1 %copy-start.10 = (bf16[512,144]{0,1:T(8,128)(2,1)S(1)}, bf16[512,144]{0,1:T(8,128)(2,1)}, u32[]{:S(2)}) copy-start(bf16[512,144]{0,1:T(8,128)(2,1)} %param.17) | copy-start | bytes 442372
  0.7 4.1 %copy-start.11 = (f32[512]{0:T(512)S(1)}, f32[512]{0:T(512)}, u32[]{:S(2)}) copy-start(f32[512]{0:T(512)} %param.19) | copy-start | bytes 6148
  0.7 4.1 %copy-start.12 = (f32[512]{0:T(512)S(1)}, f32[512]{0:T(512)}, u32[]{:S(2)}) copy-start(f32[512]{0:T(512)} %param.20) | copy-start | bytes 6148
  3.5 4.8 %collective-permute-start = (bf16[48,1024]{1,0:T(8,128)(2,1)}, bf16[48,1024]{1,0:T(8,128)(2,1)S(1)}, u32[]{:S(2)}, u32[]{:S(2)}) collective-permute-start(bf16[48,1024]{1,0:T(8,128)(2,1)} %get-tuple-element.43), channel_id=1, source_target_pairs={{0,2},{2,0},{4,6},{6,4},{8,10},{10,8},{12,14},{14,12},{16,18},{18,... | collective-permute-start | bytes 294920 | tf_op jit(solution)/shard_map/ppermute | solution.py:401
  4.1 4.3 %collective-permute-start.1 = (bf16[48,1024]{1,0:T(8,128)(2,1)}, bf16[48,1024]{1,0:T(8,128)(2,1)S(1)}, u32[]{:S(2)}, u32[]{:S(2)}) collective-permute-start(bf16[48,1024]{1,0:T(8,128)(2,1)} %get-tuple-element.44), channel_id=1, source_target_pairs={{2,4},{6,8},{10,12},{14,16},{18,20},{22,24},{26,28},{4,2},{8,6},{1... | collective-permute-start | bytes 294920 | tf_op jit(solution)/shard_map/ppermute | solution.py:463
  4.8 0.7 %copy-start.5 = (s32[16]{0:T(128)S(1)}, s32[16]{0:T(128)}, u32[]{:S(2)}) copy-start(s32[16]{0:T(128)} %get-tuple-element.42.meta_ref) | copy-start | bytes 196
  5.5 2.9 %copy-start.1 = (f32[1024]{0:T(1024)S(1)}, f32[1024]{0:T(1024)}, u32[]{:S(2)}) copy-start(f32[1024]{0:T(1024)} %param.23) | copy-start | bytes 12292
  5.5 2.9 %copy-start.2 = (f32[1024]{0:T(1024)S(1)}, f32[1024]{0:T(1024)}, u32[]{:S(2)}) copy-start(f32[1024]{0:T(1024)} %param.24) | copy-start | bytes 12292
  5.5 2.9 %copy-start.3 = (f32[512]{0:T(512)S(1)}, f32[512]{0:T(512)}, u32[]{:S(2)}) copy-start(f32[512]{0:T(512)} %param.21) | copy-start | bytes 6148
  5.5 2.9 %copy-start.4 = (f32[512]{0:T(512)S(1)}, f32[512]{0:T(512)}, u32[]{:S(2)}) copy-start(f32[512]{0:T(512)} %param.22) | copy-start | bytes 6148
  5.5 2.9 %copy-start.6 = (s32[16]{0:T(128)S(1)}, s32[16]{0:T(128)}, u32[]{:S(2)}) copy-start(s32[16]{0:T(128)} %get-tuple-element.42.meta_ref) | copy-start | bytes 196
  5.5 2.9 %copy-start.7 = (bf16[1,4,1024,128]{3,2,1,0:T(8,128)(2,1)S(1)}, bf16[1,4,1024,128]{3,2,1,0:T(8,128)(2,1)}, u32[]{:S(2)}) copy-start(bf16[1,4,1024,128]{3,2,1,0:T(8,128)(2,1)} %param.15) | copy-start | bytes 3145732
  14.6 7.1 %collective-permute-start.2 = (bf16[256,1024]{1,0:T(8,128)(2,1)S(1)}, bf16[256,1024]{1,0:T(8,128)(2,1)S(1)}, u32[]{:S(2)}, u32[]{:S(2)}) collective-permute-start(bf16[256,1024]{1,0:T(8,128)(2,1)S(1)} %get-tuple-element.53), channel_id=1, source_target_pairs={{0,2},{2,0},{4,6},{6,4},{8,10},{10,8},{12,14},{14,12},{16,18},{18,... | collective-permute-start | bytes 1572872 | tf_op jit(solution)/shard_map/ppermute | solution.py:401
  18.5 5.3 %copy-start.13 = (bf16[2304,256]{1,0:T(8,128)(2,1)S(1)}, bf16[2304,256]{1,0:T(8,128)(2,1)}, u32[]{:S(2)}) copy-start(bf16[2304,256]{1,0:T(8,128)(2,1)} %constant.2.clone.place_ref) | copy-start | bytes 3538948
  21.9 8.4 %collective-permute-start.7 = (bf16[128,1024]{1,0:T(8,128)(2,1)S(1)}, bf16[128,1024]{1,0:T(8,128)(2,1)S(1)}, u32[]{:S(2)}, u32[]{:S(2)}) collective-permute-start(bf16[128,1024]{1,0:T(8,128)(2,1)S(1)} %slice.31), channel_id=1, source_target_pairs={{0,4},{2,6},{4,0},{6,2},{8,12},{10,14},{12,8},{14,10},{16,20},{18,... | collective-permute-start | bytes 786440 | tf_op jit(solution)/shard_map/ppermute | solution.py:401
  29.1 1.5 %collective-permute-start.3 = (bf16[64,1280]{1,0:T(8,128)(2,1)S(1)}, bf16[64,1280]{1,0:T(8,128)(2,1)S(1)}, u32[]{:S(2)}, u32[]{:S(2)}) collective-permute-start(bf16[64,1280]{1,0:T(8,128)(2,1)S(1)} %get-tuple-element.62), channel_id=1, source_target_pairs={{0,2},{2,0},{4,6},{6,4},{8,10},{10,8},{12,14},{14,12},{16,18},{18,... | collective-permute-start | bytes 491528 | tf_op jit(solution)/shard_map/ppermute | solution.py:401
  29.2 1.6 %collective-permute-start.4 = (bf16[64,1280]{1,0:T(8,128)(2,1)S(1)}, bf16[64,1280]{1,0:T(8,128)(2,1)S(1)}, u32[]{:S(2)}, u32[]{:S(2)}) collective-permute-start(bf16[64,1280]{1,0:T(8,128)(2,1)S(1)} %get-tuple-element.63), channel_id=1, source_target_pairs={{0,2},{2,0},{4,6},{6,4},{8,10},{10,8},{12,14},{14,12},{16,18},{18,... | collective-permute-start | bytes 491528 | tf_op jit(solution)/shard_map/ppermute | solution.py:401
  29.7 1.4 %collective-permute-start.5 = (bf16[64,1280]{1,0:T(8,128)(2,1)S(1)}, bf16[64,1280]{1,0:T(8,128)(2,1)S(1)}, u32[]{:S(2)}, u32[]{:S(2)}) collective-permute-start(bf16[64,1280]{1,0:T(8,128)(2,1)S(1)} %get-tuple-element.64), channel_id=1, source_target_pairs={{0,2},{2,0},{4,6},{6,4},{8,10},{10,8},{12,14},{14,12},{16,18},{18,... | collective-permute-start | bytes 491528 | tf_op jit(solution)/shard_map/ppermute | solution.py:401
  29.8 1.6 %collective-permute-start.6 = (bf16[64,1280]{1,0:T(8,128)(2,1)S(1)}, bf16[64,1280]{1,0:T(8,128)(2,1)S(1)}, u32[]{:S(2)}, u32[]{:S(2)}) collective-permute-start(bf16[64,1280]{1,0:T(8,128)(2,1)S(1)} %get-tuple-element.65), channel_id=1, source_target_pairs={{0,2},{2,0},{4,6},{6,4},{8,10},{10,8},{12,14},{14,12},{16,18},{18,... | collective-permute-start | bytes 491528 | tf_op jit(solution)/shard_map/ppermute | solution.py:401
  31.4 12.6 %collective-permute-start.10 = (bf16[64,1280]{1,0:T(8,128)(2,1)S(1)}, bf16[64,1280]{1,0:T(8,128)(2,1)S(1)}, u32[]{:S(2)}, u32[]{:S(2)}) collective-permute-start(bf16[64,1280]{1,0:T(8,128)(2,1)S(1)} %add_convert_fusion.5), channel_id=1, source_target_pairs={{0,8},{1,9},{2,10},{3,11},{4,12},{5,13},{6,14},{7,15},{8,0},{9,1},... | collective-permute-start | bytes 491528 | tf_op jit(solution)/shard_map/ppermute | solution.py:417
  33.1 10.9 %collective-permute-start.11 = (bf16[64,1280]{1,0:T(8,128)(2,1)S(1)}, bf16[64,1280]{1,0:T(8,128)(2,1)S(1)}, u32[]{:S(2)}, u32[]{:S(2)}) collective-permute-start(bf16[64,1280]{1,0:T(8,128)(2,1)S(1)} %add_convert_fusion.4), channel_id=1, source_target_pairs={{0,4},{1,5},{2,6},{3,7},{4,0},{5,1},{6,2},{7,3},{8,12},{9,13},{10,... | collective-permute-start | bytes 491528 | tf_op jit(solution)/shard_map/ppermute | solution.py:417
  34.0 7.3 %collective-permute-start.8 = (bf16[64,1024]{1,0:T(8,128)(2,1)S(1)}, bf16[64,1024]{1,0:T(8,128)(2,1)S(1)}, u32[]{:S(2)}, u32[]{:S(2)}) collective-permute-start(bf16[64,1024]{1,0:T(8,128)(2,1)S(1)} %slice.33), channel_id=1, source_target_pairs={{0,8},{2,10},{4,12},{6,14},{8,0},{10,2},{12,4},{14,6},{16,24},{18,... | collective-permute-start | bytes 393224 | tf_op jit(solution)/shard_map/ppermute | solution.py:401
  34.6 10.2 %collective-permute-start.12 = (bf16[64,1280]{1,0:T(8,128)(2,1)S(1)}, bf16[64,1280]{1,0:T(8,128)(2,1)S(1)}, u32[]{:S(2)}, u32[]{:S(2)}) collective-permute-start(bf16[64,1280]{1,0:T(8,128)(2,1)S(1)} %add_convert_fusion.3), channel_id=1, source_target_pairs={{0,12},{1,13},{2,14},{3,15},{4,8},{5,9},{6,10},{7,11},{8,4},{9,5},... | collective-permute-start | bytes 491528 | tf_op jit(solution)/shard_map/ppermute | solution.py:417
  41.3 7.5 %collective-permute-start.9 = (bf16[32,1024]{1,0:T(8,128)(2,1)S(1)}, bf16[32,1024]{1,0:T(8,128)(2,1)S(1)}, u32[]{:S(2)}, u32[]{:S(2)}) collective-permute-start(bf16[32,1024]{1,0:T(8,128)(2,1)S(1)} %slice.41), channel_id=1, source_target_pairs={{0,16},{2,18},{4,20},{6,22},{8,24},{10,26},{12,28},{14,30},{16,0},... | collective-permute-start | bytes 196616 | tf_op jit(solution)/shard_map/ppermute | solution.py:401
  44.9 9.5 %collective-permute-start.14 = (bf16[32,1280]{1,0:T(8,128)(2,1)S(1)}, bf16[32,1280]{1,0:T(8,128)(2,1)S(1)}, u32[]{:S(2)}, u32[]{:S(2)}) collective-permute-start(bf16[32,1280]{1,0:T(8,128)(2,1)S(1)} %get-tuple-element.79), channel_id=1, source_target_pairs={{0,16},{1,17},{2,18},{3,19},{4,20},{5,21},{6,22},{7,23},{8,24},{9,... | collective-permute-start | bytes 245768 | tf_op jit(solution)/shard_map/ppermute | solution.py:417
  47.7 8.0 %collective-permute-start.15 = (bf16[32,1280]{1,0:T(8,128)(2,1)S(1)}, bf16[32,1280]{1,0:T(8,128)(2,1)S(1)}, u32[]{:S(2)}, u32[]{:S(2)}) collective-permute-start(bf16[32,1280]{1,0:T(8,128)(2,1)S(1)} %get-tuple-element.79), channel_id=1, source_target_pairs={{0,17},{1,16},{2,19},{3,18},{4,21},{5,20},{6,23},{7,22},{8,25},{9,... | collective-permute-start | bytes 245768 | tf_op jit(solution)/shard_map/ppermute | solution.py:417
  48.9 5.5 %collective-permute-start.13 = (bf16[32,2304]{1,0:T(8,128)(2,1)S(1)}, bf16[32,2304]{1,0:T(8,128)(2,1)S(1)}, u32[]{:S(2)}, u32[]{:S(2)}) collective-permute-start(bf16[32,2304]{1,0:T(8,128)(2,1)S(1)} %pad_maximum_fusion), channel_id=1, source_target_pairs={{0,1},{1,0},{2,3},{3,2},{4,5},{5,4},{6,7},{7,6},{8,9},{9,8},{10,11... | collective-permute-start | bytes 442376 | tf_op jit(solution)/shard_map/ppermute | solution.py:417

commit v5 on v4

--- a/solution.py
+++ b/solution.py
@@ -211,8 +211,8 @@
 def forward_kernel(
     devices, meta_ref, core_ref, other_ref, hid_in, wr_ref, s1_ref, b1_ref, dense_ref,
     s2_ref, b2_ref, wet_ref, s3_ref, b3_ref, x_ref, g_ref,
-    out_ref, back_ref, errc_ref, slopeb_ref, hid_ref, edge_ref, send_ref, keep_ref,
-    win_ref, hidb_ref,
+    out_ref, back_ref, errc_ref, slopeb_ref, hid_ref, edge_ref, hide_ref, slopee_ref, send_ref, keep_ref,
+    win_ref, wine_ref, hidb_ref,
 ):
     me = lax.axis_index("tile")
     held = meta_ref[HELD]
@@ -236,6 +236,13 @@
     hid_ref[EDGE] = (pre * sigmoid(pre)).astype(BF)
     hid_ref[ZERO] = jnp.zeros((MID, PIX), BF)
 
+    build_windows(hid_ref, wine_ref, meta_ref, (EDGE,), EDGE, False)
+    for b in range(2):
+        rows = slice(b * HALF, (b + 1) * HALF)
+        act, slope = silu_slope(nn_dot(dense_ref[b], wine_ref[b]) * scale2[rows] + shift2[rows])
+        hide_ref[rows, :] = act.astype(BF)
+        slopee_ref[rows, :] = slope * scale2[rows]
+
     for first, count in CHUNKS:
         build_windows(hid_ref, win_ref, meta_ref, range(first, first + count), 0, False)
         lanes = slice(first * PIX, (first + count) * PIX)
@@ -262,7 +269,11 @@
     own = SLOTS * PIX
     for ref, flip in ((send_ref, 1), (keep_ref, 0)):
         rows = jnp.concatenate([hidb_ref[at, :own] for at in row_blocks(devices, me, flip)], axis=0)
-        ref[...] = nt_dot(rows, errc_ref[:, :own]).astype(BF)
+        part = nt_dot(rows, errc_ref[:, :own]).astype(BF)
+        per = MID // devices
+        for j in range(devices // 2):
+            for c in range(CIN // PIX):
+                ref[j, c * per : (c + 1) * per, :] = part[j * per : (j + 1) * per, c * PIX : (c + 1) * PIX]
 
 
 def row_blocks(devices, me, flip):
@@ -279,8 +290,8 @@
 
 
 def pull_kernel(
-    meta_ref, core_ref, other_ref, hid_ref, dense_ref, s2_ref, b2_ref, wet_ref, s3_ref, b3_ref,
-    edge_ref, we_ref, errc_ref, slopeb_ref, errb_ref, win_ref, hidb_ref, slope_ref,
+    core_ref, other_ref, hide_ref, slopee_ref, wet_ref, s3_ref, b3_ref,
+    edge_ref, we_ref, errc_ref, slopeb_ref, errb_ref,
 ):
     odd = lax.axis_index("tile") % 2
     core_g = jnp.where(odd == 0, 0, TW - 1)
@@ -289,27 +300,18 @@
         tn_dot(core_ref[2 * TH :, :], edge_select(TH, g_lane(core_g)))
         + tn_dot(other_ref[2 * TH :, :], edge_select(TH, g_lane(other_g)))
     )
-    scale2 = column(s2_ref)
-    shift2 = column(b2_ref)
     scale3 = column(s3_ref)
     shift3 = column(b3_ref)
-    build_windows(hid_ref, win_ref, meta_ref, (EDGE,), EDGE, False)
-    for b in range(2):
-        conv = nn_dot(dense_ref[b], win_ref[b])
-        rows = slice(b * HALF, (b + 1) * HALF)
-        act, slope = silu_slope(conv * scale2[rows] + shift2[rows])
-        hidb_ref[rows, :] = act.astype(BF)
-        slope_ref[rows, :] = slope * scale2[rows]
     for first, count in CHUNKS:
         lanes = slice(first * PIX, (first + count) * PIX)
         pulled = nn_dot(we_ref[...], errc_ref[:, lanes])
         errb = (pulled * slopeb_ref[:, lanes]).astype(BF)
         for k in range(count):
             errb_ref[first + k] = errb[:, k * PIX : (k + 1) * PIX]
-    grown = nn_dot(wet_ref[...], hidb_ref[...])
+    grown = nn_dot(wet_ref[...], hide_ref[...])
     _, slope = silu_slope(grown * scale3 + shift3 + edge_ref[...].astype(F32))
     errc = (edge_g * slope * scale3).astype(BF)
-    errb_ref[EDGE] = (nn_dot(we_ref[...], errc) * slope_ref[...]).astype(BF)
+    errb_ref[EDGE] = (nn_dot(we_ref[...], errc) * slopee_ref[...]).astype(BF)
     errb_ref[ZERO] = jnp.zeros((MID, PIX), BF)
 
 
@@ -342,16 +344,31 @@
             kept_ref[:, k * HALF : (k + 1) * HALF] = jnp.where(same, full, 0.0).astype(BF)
         groups_ref[rows, :] = nn_dot(kept_ref[...], place_ref[...]).astype(BF)
     tiles = jnp.concatenate([x_ref[i] for i in range(SLOTS)], axis=1)
-    count = HALF // 4
+    per = MID // devices
+    inner = devices // 8
+    lane = lax.broadcasted_iota(jnp.int32, (HALF, PIX), 1)
+    row = lax.broadcasted_iota(jnp.int32, (HALF, PIX), 0)
+    own_lanes = lane // GW == row % 8
+    lane = lax.broadcasted_iota(jnp.int32, (PIX, PIX), 1)
+    row = lax.broadcasted_iota(jnp.int32, (PIX, PIX), 0)
+    repeat = (lane % GW == row).astype(F32).astype(BF)
+    pack = lax.broadcasted_iota(jnp.int32, (4 * devices, HALF), 0)
+    row = lax.broadcasted_iota(jnp.int32, (4 * devices, HALF), 1)
+    gather = jnp.logical_and(pack // 8 == row // per, pack % 8 == (row % per) // 8).astype(F32).astype(BF)
     for refs, flip in ((send_refs, 1), (keep_refs, 0)):
         blocks = row_blocks(devices, me, flip)
         rows = jnp.concatenate([flat_ref[at, :] for at in blocks], axis=0)
         group_rows = jnp.concatenate([groups_ref[at, :] for at in blocks], axis=0)
         part = nt_dot(rows, tiles).astype(BF)
-        for k in range(4):
-            at = slice(k * count, (k + 1) * count)
-            refs[k][:, :CIN] = part[at]
-            refs[k][:, CIN:] = group_rows[at]
+        tail = jnp.where(own_lanes, nn_dot(group_rows[:, PIX:], repeat), 0.0).astype(BF)
+        tail = nn_dot(gather, tail).astype(BF)
+        for j in range(devices // 2):
+            ref, i = refs[j // inner], j % inner
+            at = slice(j * per, (j + 1) * per)
+            for c in range(CIN // PIX):
+                ref[i, c * per : (c + 1) * per, :] = part[at, c * PIX : (c + 1) * PIX]
+            ref[i, 8 * per : 9 * per, :] = group_rows[at, :PIX]
+            ref[i, 9 * per :, :] = tail[8 * j : 8 * j + 8]
 
 
 def grad_kernel(wr_ref, erra_ref, back_ref, act_ref, grad_ref, out_ref):
@@ -366,13 +383,25 @@
 
 def finish_kernel(norm, ea_ref, eb_ref, *refs):
     parts, (reduce_ref, group_ref, expand_ref) = refs[:4], refs[4:]
-    expand_ref[...] = (ea_ref[...].astype(F32) + eb_ref[...].astype(F32)) * norm
+    expand = (ea_ref[...].astype(F32) + eb_ref[...].astype(F32)) * norm
     total = sum(part[...].astype(F32) for part in parts) * norm
-    reduce_ref[...] = total[:, :CIN]
-    group_ref[...] = total[:, CIN : CIN + TAPS * GW]
-
-
-LIMITS = {"edges": 56, "prep": 13, "forward": 26, "pull": 14, "backward": 18, "grads": 9, "finish": 2}
+    per = reduce_ref.shape[0]
+    for c in range(CIN // PIX):
+        reduce_ref[:, c * PIX : (c + 1) * PIX] = total[c * per : (c + 1) * per]
+        expand_ref[:, c * PIX : (c + 1) * PIX] = expand[c * per : (c + 1) * per]
+    group_ref[:, :PIX] = total[8 * per : 9 * per]
+    tail = jnp.concatenate(
+        [jnp.broadcast_to(total[9 * per + k : 9 * per + k + 1], (8, PIX)) for k in range(per // 8)], axis=0
+    )
+    lane = lax.broadcasted_iota(jnp.int32, (per, PIX), 1)
+    row = lax.broadcasted_iota(jnp.int32, (per, PIX), 0)
+    tail = jnp.where(lane // GW == row % 8, tail, 0.0)
+    for shift in (64, 32, 16):
+        tail = tail + pltpu.roll(tail, shift, 1)
+    group_ref[:, PIX:] = tail[:, : TAPS * GW - PIX]
+
+
+LIMITS = {"edges": 56, "prep": 13, "forward": 26, "pull": 11, "backward": 18, "grads": 9, "finish": 2}
 WORK = {"edges": 2, "prep": 3, "forward": 7, "pull": 2, "backward": 5, "grads": 2, "finish": 1}
 
 
@@ -471,25 +500,24 @@
     )(meta, x, w_reduce, w_expand, w_group.T, s1, b1)
 
     lanes = SLOTS * PIX
-    act, back, errc, slope_b, hid, edge, e_send, e_keep = call(
+    act, back, errc, slope_b, hid, edge, hid_e, slope_e, e_send, e_keep = call(
         functools.partial(forward_kernel, devices), "forward",
         [shape((SLOTS, CIN, PIX), BF), shape((SLOTS, CIN, PIX), F32), shape((CIN, lanes), BF),
          shape((MID, lanes), F32), shape((SLOTS + 2, MID, PIX), BF), shape((CIN, PIX), BF),
-         shape((HALF, CIN), BF), shape((HALF, CIN), BF)],
+         shape((MID, PIX), BF), shape((MID, PIX), F32), shape((devices // 2, 8 * per, PIX), BF), shape((devices // 2, 8 * per, PIX), BF)],
         (0,), (), 15,
-        [pltpu.VMEM((2, KDIM, lanes), BF), pltpu.VMEM((MID, lanes), BF)],
+        [pltpu.VMEM((2, KDIM, lanes), BF), pltpu.VMEM((2, KDIM, PIX), BF), pltpu.VMEM((MID, lanes), BF)],
     )(meta, from_core, from_other, hid, w_reduce, s1, b1, dense, s2, b2, wet, s3, b3, x, g)
 
     e_core = swap(e_send, "tile", 1)
     (errb,) = call(
-        pull_kernel, "pull", [shape((SLOTS + 2, MID, PIX), BF)], (0,), (), 14,
-        [pltpu.VMEM((2, KDIM, PIX), BF), pltpu.VMEM((MID, PIX), BF), pltpu.VMEM((MID, PIX), F32)],
-    )(meta, from_core, from_other, hid, dense, s2, b2, wet, s3, b3, edge, w_expand, errc, slope_b)
+        pull_kernel, "pull", [shape((SLOTS + 2, MID, PIX), BF)], (), (), 11,
+    )(from_core, from_other, hid_e, slope_e, wet, s3, b3, edge, w_expand, errc, slope_b)
     e_part = add_pair(e_keep, e_core)
     errb, e_part = lax.optimization_barrier((errb, e_part))
     e_part = halve(e_part, 2)
 
-    piece = [shape((HALF // 4, CIN + HALF), BF)] * 8
+    piece = [shape((devices // 8, 9 * per + 8, PIX), BF)] * 8
     erra, *pieces = call(
         functools.partial(backward_kernel, devices), "backward", [shape((SLOTS, MID, PIX), BF)] + piece,
         (0,), (), 7,
@@ -503,8 +531,12 @@
     r_core = [swap(value, "tile", 1) for value in pieces[:4]]
     *r_core, e_part = lax.optimization_barrier((*r_core, e_part))
     r_parts = [add_pair(a, b) for a, b in zip(pieces[4:], r_core)]
+    tall, half = r_parts[1].shape[1], e_part.shape[0] // 2
+    r_parts[1] = jnp.concatenate([r_parts[1], e_part[half:]], axis=1)
     r_parts = [r_parts[0]] + [cross(r_parts[k], devices, slides, 2 * (k // 2 + 2 * (k % 2)), 0) for k in (1, 2, 3)]
-    mask = 4
+    e_part = add_pair(e_part[:half], r_parts[1][:, tall:])
+    r_parts[1] = r_parts[1][:, :tall]
+    mask = 8
     while mask < devices:
         e_part = halve(e_part, mask)
         mask *= 2
@@ -513,17 +545,18 @@
     while 2 * mask < devices:
         r_part = halve(r_part, mask)
         mask *= 2
-    mine, theirs = r_part[:per], r_part[per:]
-    both = cross(jnp.concatenate([mine, e_part], axis=1), devices, slides, 0, 1)
-    e_other = both[:, CIN + HALF :]
+    mine, theirs = r_part[0], r_part[1]
+    near = mine.shape[0]
+    both = cross(jnp.concatenate([mine, e_part[0]], axis=0), devices, slides, 0, 1)
+    e_other = both[near:]
     finals = [
         mine,
-        both[:, : CIN + HALF],
+        both[:near],
         cross(theirs, devices, slides, devices // 2, 0),
         cross(theirs, devices, slides, devices // 2, 1),
     ]
     if slides > 2:
-        e_part, e_other = add_pair(e_part, e_other), jnp.zeros_like(e_part)
+        e_part, e_other = add_pair(e_part, e_other[None]), jnp.zeros_like(e_other)
         total = add_all(*finals)
         mask = 2
         while mask < slides:
@@ -535,7 +568,7 @@
     grad_reduce, grad_group, grad_expand = call(
         functools.partial(finish_kernel, norm), "finish",
         [shape((per, CIN), F32), shape((per, TAPS * GW), F32), shape((per, CIN), F32)], (), (), 6,
-    )(e_part, e_other, *finals)
+    )(e_part[0], e_other, *finals)
     return (out[None], grad_in[None], grad_reduce, grad_group, grad_expand)
 
 

time: 56.6 us -> 55.6 us (0.982)
  starting transfers between devices: 20.6 us -> 19.7 us
    ppermute x9 -> x8, waiting for transfers between devices: 5.53 us -> 1.01 us  [swap(): return lax.ppermute(value, axis, [(i, i ^ mask) for i in range(size)])]
    ppermute x6, waiting for transfers between devices: 4.95 us -> 9.18 us  [cross(): return lax.ppermute(value, ('tile', 'slide'), pairs)]
    pallas_call x1, Pallas kernels: 3.13 us -> 1.92 us  [shards(): call(pull_kernel, 'pull', [shape((SLOTS + 2, MID, PIX), BF)], (), (), 11)]
    pallas_call x1, Pallas kernels: 6.16 us -> 6.96 us  [shards(): call(functools.partial(forward_kernel, devices), 'forward', [shape((SLOTS...]
    ppermute x9 -> x8, starting transfers between devices: 10.6 us -> 10.2 us  [swap(): return lax.ppermute(value, axis, [(i, i ^ mask) for i in range(size)])]
  transfers between devices with their start and end apart: 16 -> 15, of which waited for: 9 -> 8; matrix products, arithmetic and copies ran while one was open for 1% -> 1% of each run, Pallas kernels for 24% -> 23%
where the time goes in v5:
time: 55.6 us; the launch traced here: 55.4 us
  Pallas kernels  23.3 us (42%)
  starting transfers between devices  19.7 us (35%)
  waiting for transfers between devices  10.2 us (18%)
  between operations  0.97 us (2%)
  local copies, waits for them, and re-layouts  0.76 us (1%)
  other arithmetic  0.56 us (1%)
    ppermute x8, starting transfers between devices, swap(): return lax.ppermute(value, axis, [(i, i ^ mask) for i in range(size)])  10.2 us
    ppermute x6, waiting for transfers between devices, cross(): return lax.ppermute(value, ('tile', 'slide'), pairs)  9.18 us
    ppermute x6, starting transfers between devices, cross(): return lax.ppermute(value, ('tile', 'slide'), pairs)  8.85 us
    pallas_call x1, Pallas kernels, shards(): call(functools.partial(forward_kernel, devices), 'forward', [shape((SLOTS...  6.96 us
    pallas_call x1, Pallas kernels, shards(): call(functools.partial(backward_kernel, devices), 'backward', [shape((SLO...  5.73 us
    pallas_call x1, Pallas kernels, shards(): call(prep_kernel, 'prep', [shape((SLOTS, MID, PIX), BF), shape((SLOTS, MI...  2.85 us
    pallas_call x1, Pallas kernels, shards(): call(edge_kernel, 'edges', [shape((PAY, CIN), BF), shape((PAY, CIN), BF),...  2.85 us
    pallas_call x1, Pallas kernels, shards(): call(grad_kernel, 'grads', [shape((SLOTS, CIN, PIX), BF), shape((SLOTS, C...  2.1 us
  transfers between devices with their start and end apart: 15, of which 8 were waited for; matrix products, arithmetic and copies ran while one was open for 1% of the time, Pallas kernels for 23%

profile of v5, /device:TPU:0, one launch (start us, length us, event | category | flops | bytes accessed | tf_op | source)
XLA Modules:
  0.0 55.4 jit_solution(6866945031590790714)
XLA Ops:
  0.6 0.0 copy-start.1
  0.6 0.0 copy-start.2
  0.7 0.0 copy-start.3
  0.7 0.0 copy-start.4
  0.7 0.0 copy-start.7
  0.7 0.0 copy-start.8
  0.7 2.8 %edges.1 = (bf16[48,1024]{1,0:T(8,128)(2,1)}, bf16[48,1024]{1,0:T(8,128)(2,1)}, s32[16]{0:T(128)}) custom-call(s32[1,16]{1,0:T(1,128)} %count_hbm.1, s32[1,31]{1,0:T(1,128)} %joined_hbm.1, bf16[4,1024,128]{2,1,0:T(8,128)(2,1)} %bitcast.19, bf16[4,1024,128]{2,1,0:T(8,128)(2,1)} %bitcast.17), custom_call_target="tpu_custom_call" | custom-call | flops 2200000000 | bytes 1048576 | tf_op jit(solution)/shard_map/edges/pallas_call | solution.py:483
  3.5 0.5 collective-permute-start
  4.1 0.7 %collective-permute-start.1 = (bf16[48,1024]{1,0:T(8,128)(2,1)}, bf16[48,1024]{1,0:T(8,128)(2,1)S(1)}, u32[]{:S(2)}, u32[]{:S(2)}) collective-permute-start(bf16[48,1024]{1,0:T(8,128)(2,1)} %get-tuple-element.46), channel_id=1, source_target_pairs={{2,4},{6,8},{10,12},{14,16},{18,20},{22,24},{26,28},{4,2},{8,6},{1... | collective-permute-start | bytes 294920 | tf_op jit(solution)/shard_map/ppermute | solution.py:492
  4.7 0.0 copy-done.1
  4.7 0.0 copy-done.2
  4.8 0.0 copy-done.3
  4.8 0.0 copy-done.4
  4.8 0.0 copy-done.7
  4.8 0.0 copy-done.8
  4.8 0.0 copy-start.12
  4.8 0.6 %copy-done.12 = s32[16]{0:T(128)S(1)} copy-done((s32[16]{0:T(128)S(1)}, s32[16]{0:T(128)}, u32[]{:S(2)}) %copy-start.12) | copy-done | bytes 88
  5.5 0.0 copy-start
  5.5 0.0 copy-start.5
  5.5 0.0 copy-start.10
  5.5 2.9 %prep.1 = (bf16[4,512,128]{2,1,0:T(8,128)(2,1)S(1)}, f32[4,512,128]{2,1,0:T(8,128)S(1)}, bf16[2,256,2304]{2,1,0:T(8,128)(2,1)S(1)}, bf16[2,256,2304]{2,1,0:T(8,128)(2,1)S(1)}, bf16[1024,512]{1,0:T(8,128)(2,1)S(1)}) custom-call(s32[16]{0:T(128)S(1)} %copy-done.12, bf16[4,1024,128]{2,1,0:T(8,128)(2,1)S(1)} %bitcast.20, bf16[512,1024]{1,0:T(8,128)(2,1)S(1)} %copy-done.3, ...), custom_call_target="tpu_custom_call" | custom-call | flops 3300000000 | bytes 1048576 | tf_op jit(solution)/shard_map/prep/pallas_call | solution.py:495
  8.3 0.0 collective-permute-done.core_ref
  8.4 0.0 collective-permute-done.1.other_ref
  8.4 0.0 copy-done
  8.4 0.0 copy-done.5
  8.4 0.0 copy-done.6
  8.4 0.0 copy-done.9
  8.4 0.0 copy-done.10
  8.4 7.0 %forward.1 = (bf16[4,1024,128]{2,1,0:T(8,128)(2,1)S(1)}, f32[4,1024,128]{2,1,0:T(8,128)S(1)}, bf16[1024,512]{1,0:T(8,128)(2,1)S(1)}, f32[512,512]{1,0:T(8,128)S(...) custom-call(s32[16]{0:T(128)S(1)} %copy-done.12, ...), custom_call_target="tpu_custom_call" | custom-call | flops 7699999744 | bytes 1048576 | tf_op jit(solution)/shard_map/forward/pallas_call | solution.py:503
  15.4 4.0 %collective-permute-start.2 = (bf16[8,256,128]{2,1,0:T(8,128)(2,1)S(1)}, bf16[8,256,128]{2,1,0:T(8,128)(2,1)S(1)}, u32[]{:S(2)}, u32[]{:S(2)}) collective-permute-start(bf16[8,256,128]{2,1,0:T(8,128)(2,1)S(1)} %get-tuple-element.56), channel_id=1, source_target_pairs={{0,2},{2,0},{4,6},{6,4},{8,10},{10,8},{12,14},{14,12},{16,18},{18,... | collective-permute-start | bytes 1572872 | tf_op jit(solution)/shard_map/ppermute | solution.py:430
  19.3 1.9 %pull.1.errb_ref = bf16[6,512,128]{2,1,0:T(8,128)(2,1)S(1)} custom-call(bf16[48,1024]{1,0:T(8,128)(2,1)S(1)} %collective-permute-done.core_ref, bf16[48,1024]{1,0:T(8,128)(2,1)S(1)} %collective-permute-done.1.other_ref, bf16[512,128]{1,0:T(8,128)(2,1)S(1)} %get-tuple-element.50.hide_ref, f32[512,128]{1,0:T(8,128)S(1)} %get-tuple-element.51.slopee_ref, ...), custom_call_target="tpu_custom_call" | custom-call | flops 2200000000 | bytes 1048576 | tf_op jit(solution)/shard_map/pull/pallas_call | solution.py:513
  21.3 0.0 collective-permute-done.2
  21.3 0.1 add_convert_fusion
  21.5 1.9 %collective-permute-start.7 = (bf16[4,256,128]{2,1,0:T(8,128)(2,1)S(1)}, bf16[4,256,128]{2,1,0:T(8,128)(2,1)S(1)}, u32[]{:S(2)}, u32[]{:S(2)}) collective-permute-start(bf16[4,256,128]{2,1,0:T(8,128)(2,1)S(1)} %slice.37), channel_id=1, source_target_pairs={{0,4},{2,6},{4,0},{6,2},{8,12},{10,14},{12,8},{14,10},{16,20},{18,... | collective-permute-start | bytes 786440 | tf_op jit(solution)/shard_map/ppermute | solution.py:430
  23.4 0.0 copy-done.11
  23.4 5.7 %backward.1 = (bf16[4,512,128]{2,1,0:T(8,128)(2,1)S(1)}, bf16[2,296,128]{2,1,0:T(8,128)(2,1)S(1)}, bf16[2,296,128]{2,1,0:T(8,128)(2,1)S(1)}, bf16[2,296,128]{2,1...) custom-call(s32[16]{0:T(128)S(1)} %copy-done.12, ...), custom_call_target="tpu_custom_call" | custom-call | flops 5500000256 | bytes 1048576 | tf_op jit(solution)/shard_map/backward/pallas_call | solution.py:521
  29.1 0.1 collective-permute-start.3
  29.2 0.5 collective-permute-start.4
  29.7 0.1 collective-permute-start.5
  29.8 0.4 collective-permute-start.6
  30.2 0.0 collective-permute-done.7
  30.2 0.1 add_convert_fusion.1
  30.3 0.3 collective-permute-done.3
  30.6 0.2 collective-permute-done.4
  30.8 0.3 collective-permute-done.5
  31.1 0.2 collective-permute-done.6
  31.4 1.7 %collective-permute-start.8 = (bf16[2,552,128]{2,1,0:T(8,128)(2,1)S(1)}, bf16[2,552,128]{2,1,0:T(8,128)(2,1)S(1)}, u32[]{:S(2)}, u32[]{:S(2)}) collective-permute-start(bf16[2,552,128]{2,1,0:T(8,128)(2,1)S(1)} %pad_maximum_fusion), channel_id=1, source_target_pairs={{0,8},{1,9},{2,10},{3,11},{4,12},{5,13},{6,14},{7,15},{8,0},{9,1},... | collective-permute-start | bytes 847880 | tf_op jit(solution)/shard_map/ppermute | solution.py:446
  33.0 0.1 add_convert_fusion.4
  33.1 0.7 %collective-permute-start.10 = (bf16[2,296,128]{2,1,0:T(8,128)(2,1)S(1)}, bf16[2,296,128]{2,1,0:T(8,128)(2,1)S(1)}, u32[]{:S(2)}, u32[]{:S(2)}) collective-permute-start(bf16[2,296,128]{2,1,0:T(8,128)(2,1)S(1)} %add_convert_fusion.4), channel_id=1, source_target_pairs={{0,4},{1,5},{2,6},{3,7},{4,0},{5,1},{6,2},{7,3},{8,12},{9,13},{10,... | collective-permute-start | bytes 454664 | tf_op jit(solution)/shard_map/ppermute | solution.py:446
  33.9 1.3 %collective-permute-start.11 = (bf16[2,296,128]{2,1,0:T(8,128)(2,1)S(1)}, bf16[2,296,128]{2,1,0:T(8,128)(2,1)S(1)}, u32[]{:S(2)}, u32[]{:S(2)}) collective-permute-start(bf16[2,296,128]{2,1,0:T(8,128)(2,1)S(1)} %add_convert_fusion.3), channel_id=1, source_target_pairs={{0,12},{1,13},{2,14},{3,15},{4,8},{5,9},{6,10},{7,11},{8,4},{9,5},... | collective-permute-start | bytes 454664 | tf_op jit(solution)/shard_map/ppermute | solution.py:446
  35.2 5.9 %collective-permute-done.8 = bf16[2,552,128]{2,1,0:T(8,128)(2,1)S(1)} collective-permute-done((bf16[2,552,128]{2,1,0:T(8,128)(2,1)S(1)}, bf16[2,552,128]{2,1,0:T(8,128)(2,1)S(1)}, u32[]{:S(2)}, u32[]{:S(2)}) %collective-permute-start.8) | collective-permute-done | bytes 282656 | tf_op jit(solution)/shard_map/ppermute | solution.py:446
  41.1 2.7 %collective-permute-start.9 = (bf16[1,256,128]{2,1,0:T(8,128)(2,1)S(1)}, bf16[1,256,128]{2,1,0:T(8,128)(2,1)S(1)}, u32[]{:S(2)}, u32[]{:S(2)}) collective-permute-start(bf16[1,256,128]{2,1,0:T(8,128)(2,1)S(1)} %slice.50), channel_id=1, source_target_pairs={{0,16},{2,18},{4,20},{6,22},{8,24},{10,26},{12,28},{14,30},{16,0},... | collective-permute-start | bytes 196616 | tf_op jit(solution)/shard_map/ppermute | solution.py:430
  43.7 0.0 collective-permute-done.10
  43.7 0.0 collective-permute-done.11
  43.8 0.1 add_convert_fusion.2
  43.9 4.2 %collective-permute-start.14 = (bf16[296,128]{1,0:T(8,128)(2,1)S(1)}, bf16[296,128]{1,0:T(8,128)(2,1)S(1)}, u32[]{:S(2)}, u32[]{:S(2)}) collective-permute-start(bf16[296,128]{1,0:T(8,128)(2,1)S(1)} %get-tuple-element.83), channel_id=1, source_target_pairs={{0,17},{1,16},{2,19},{3,18},{4,21},{5,20},{6,23},{7,22},{8,25},{9,... | collective-permute-start | bytes 227336 | tf_op jit(solution)/shard_map/ppermute | solution.py:446
  48.1 0.0 collective-permute-start.13
  48.1 0.0 collective-permute-done.9
  48.1 1.0 %collective-permute-start.12 = (bf16[552,128]{1,0:T(8,128)(2,1)S(1)}, bf16[552,128]{1,0:T(8,128)(2,1)S(1)}, u32[]{:S(2)}, u32[]{:S(2)}) collective-permute-start(bf16[552,128]{1,0:T(8,128)(2,1)S(1)} %pad_maximum_fusion.1), channel_id=1, source_target_pairs={{0,1},{1,0},{2,3},{3,2},{4,5},{5,4},{6,7},{7,6},{8,9},{9,8},{10,11... | collective-permute-start | bytes 423944 | tf_op jit(solution)/shard_map/ppermute | solution.py:446
  49.1 2.1 %grads.1 = (bf16[4,1024,128]{2,1,0:T(8,128)(2,1)}, bf16[4,1024,128]{2,1,0:T(8,128)(2,1)}) custom-call(bf16[512,1024]{1,0:T(8,128)(2,1)S(1)} %copy-done.3, bf16[4,512,128]{2,1,0:T(8,128)(2,1)S(1)} %get-tuple-element.61.erra_ref, f32[4,1024,128]{2,1,0:T(8,128)S(1)} %get-tuple-element.62.back_ref, bf16[4,1024,128]{2,1,0:T(8,128)(2,1)S(1)} %get-tuple-element.63.act_ref), custom_call_target="tpu_custom_call" | custom-call | flops 2200000000 | bytes 1048576 | tf_op jit(solution)/shard_map/grads/pallas_call | solution.py:527
  51.2 2.6 %collective-permute-done.12 = bf16[552,128]{1,0:T(8,128)(2,1)S(1)} collective-permute-done((bf16[552,128]{1,0:T(8,128)(2,1)S(1)}, bf16[552,128]{1,0:T(8,128)(2,1)S(1)}, u32[]{:S(2)}, u32[]{:S(2)}) %collective-permute-start.12) | collective-permute-done | bytes 141344 | tf_op jit(solution)/shard_map/ppermute | solution.py:446
  53.8 0.1 collective-permute-done.14.refs_3_
  53.9 0.7 %collective-permute-done.13.refs_2_ = bf16[296,128]{1,0:T(8,128)(2,1)S(1)} collective-permute-done((bf16[296,128]{1,0:T(8,128)(2,1)S(1)}, bf16[296,128]{1,0:T(8,128)(2,1)S(1)}, u32[]{:S(2)}, u32[]{:S(2)}) %collective-permute-start.13) | collective-permute-done | bytes 75808 | tf_op jit(solution)/shard_map/ppermute | solution.py:446
  54.5 0.9 %finish.1 = (f32[32,1024]{1,0:T(8,128)}, f32[32,144]{1,0:T(8,128)}, f32[32,1024]{1,0:T(8,128)}) custom-call(bf16[256,128]{1,0:T(8,128)(2,1)S(1)} %fusion.ea_ref, bf16[256,128]{1,0:T(8,128)(2,1)S(1)} %slice.53.eb_ref, bf16[296,128]{1,0:T(8,128)(2,1)S(1)} %get-tuple-element.84.refs_0_, bf16[296,128]{1,0:T(8,128)(2,1)S(1)} %slice.54.refs_1_, ...), custom_call_target="tpu_custom_call" | custom-call | flops 1100000000 | bytes 1048576 | tf_op jit(solution)/shard_map/finish/pallas_call | solution.py:568
  (15 shorter events, 0.2 us)
Async XLA Ops:
  0.6 4.1 %copy-start.1 = (bf16[512,1024]{1,0:T(8,128)(2,1)S(1)}, bf16[512,1024]{1,0:T(8,128)(2,1)}, u32[]{:S(2)}) copy-start(bf16[512,1024]{1,0:T(8,128)(2,1)} %we_ref.3) | copy-start | bytes 3145732
  0.6 4.1 %copy-start.2 = (bf16[1,4,1024,128]{3,2,1,0:T(8,128)(2,1)S(1)}, bf16[1,4,1024,128]{3,2,1,0:T(8,128)(2,1)}, u32[]{:S(2)}) copy-start(bf16[1,4,1024,128]{3,2,1,0:T(8,128)(2,1)} %param.14) | copy-start | bytes 3145732
  0.7 4.1 %copy-start.3 = (bf16[512,1024]{1,0:T(8,128)(2,1)S(1)}, bf16[512,1024]{1,0:T(8,128)(2,1)}, u32[]{:S(2)}) copy-start(bf16[512,1024]{1,0:T(8,128)(2,1)} %wr_ref.5) | copy-start | bytes 3145732
  0.7 4.1 %copy-start.4 = (bf16[512,144]{0,1:T(8,128)(2,1)S(1)}, bf16[512,144]{0,1:T(8,128)(2,1)}, u32[]{:S(2)}) copy-start(bf16[512,144]{0,1:T(8,128)(2,1)} %param.17) | copy-start | bytes 442372
  0.7 4.1 %copy-start.7 = (f32[512]{0:T(512)S(1)}, f32[512]{0:T(512)}, u32[]{:S(2)}) copy-start(f32[512]{0:T(512)} %param.19) | copy-start | bytes 6148
  0.7 4.1 %copy-start.8 = (f32[512]{0:T(512)S(1)}, f32[512]{0:T(512)}, u32[]{:S(2)}) copy-start(f32[512]{0:T(512)} %param.20) | copy-start | bytes 6148
  3.5 4.8 %collective-permute-start = (bf16[48,1024]{1,0:T(8,128)(2,1)}, bf16[48,1024]{1,0:T(8,128)(2,1)S(1)}, u32[]{:S(2)}, u32[]{:S(2)}) collective-permute-start(bf16[48,1024]{1,0:T(8,128)(2,1)} %get-tuple-element.45), channel_id=1, source_target_pairs={{0,2},{2,0},{4,6},{6,4},{8,10},{10,8},{12,14},{14,12},{16,18},{18,... | collective-permute-start | bytes 294920 | tf_op jit(solution)/shard_map/ppermute | solution.py:430
  4.1 4.3 %collective-permute-start.1 = (bf16[48,1024]{1,0:T(8,128)(2,1)}, bf16[48,1024]{1,0:T(8,128)(2,1)S(1)}, u32[]{:S(2)}, u32[]{:S(2)}) collective-permute-start(bf16[48,1024]{1,0:T(8,128)(2,1)} %get-tuple-element.46), channel_id=1, source_target_pairs={{2,4},{6,8},{10,12},{14,16},{18,20},{22,24},{26,28},{4,2},{8,6},{1... | collective-permute-start | bytes 294920 | tf_op jit(solution)/shard_map/ppermute | solution.py:492
  4.8 0.7 %copy-start.12 = (s32[16]{0:T(128)S(1)}, s32[16]{0:T(128)}, u32[]{:S(2)}) copy-start(s32[16]{0:T(128)} %get-tuple-element.44.meta_ref) | copy-start | bytes 196
  5.5 2.9 %copy-start = (bf16[1,4,1024,128]{3,2,1,0:T(8,128)(2,1)S(1)}, bf16[1,4,1024,128]{3,2,1,0:T(8,128)(2,1)}, u32[]{:S(2)}) copy-start(bf16[1,4,1024,128]{3,2,1,0:T(8,128)(2,1)} %param.15) | copy-start | bytes 3145732
  5.5 2.9 %copy-start.5 = (f32[1024]{0:T(1024)S(1)}, f32[1024]{0:T(1024)}, u32[]{:S(2)}) copy-start(f32[1024]{0:T(1024)} %param.23) | copy-start | bytes 12292
  5.5 2.9 %copy-start.6 = (f32[1024]{0:T(1024)S(1)}, f32[1024]{0:T(1024)}, u32[]{:S(2)}) copy-start(f32[1024]{0:T(1024)} %param.24) | copy-start | bytes 12292
  5.5 2.9 %copy-start.9 = (f32[512]{0:T(512)S(1)}, f32[512]{0:T(512)}, u32[]{:S(2)}) copy-start(f32[512]{0:T(512)} %param.21) | copy-start | bytes 6148
  5.5 2.9 %copy-start.10 = (f32[512]{0:T(512)S(1)}, f32[512]{0:T(512)}, u32[]{:S(2)}) copy-start(f32[512]{0:T(512)} %param.22) | copy-start | bytes 6148
  15.4 5.9 %collective-permute-start.2 = (bf16[8,256,128]{2,1,0:T(8,128)(2,1)S(1)}, bf16[8,256,128]{2,1,0:T(8,128)(2,1)S(1)}, u32[]{:S(2)}, u32[]{:S(2)}) collective-permute-start(bf16[8,256,128]{2,1,0:T(8,128)(2,1)S(1)} %get-tuple-element.56), channel_id=1, source_target_pairs={{0,2},{2,0},{4,6},{6,4},{8,10},{10,8},{12,14},{14,12},{16,18},{18,... | collective-permute-start | bytes 1572872 | tf_op jit(solution)/shard_map/ppermute | solution.py:430
  19.3 4.0 %copy-start.11 = (bf16[2304,256]{1,0:T(8,128)(2,1)S(1)}, bf16[2304,256]{1,0:T(8,128)(2,1)}, u32[]{:S(2)}) copy-start(bf16[2304,256]{1,0:T(8,128)(2,1)} %constant.2.clone.place_ref) | copy-start | bytes 3538948
  21.5 8.8 %collective-permute-start.7 = (bf16[4,256,128]{2,1,0:T(8,128)(2,1)S(1)}, bf16[4,256,128]{2,1,0:T(8,128)(2,1)S(1)}, u32[]{:S(2)}, u32[]{:S(2)}) collective-permute-start(bf16[4,256,128]{2,1,0:T(8,128)(2,1)S(1)} %slice.37), channel_id=1, source_target_pairs={{0,4},{2,6},{4,0},{6,2},{8,12},{10,14},{12,8},{14,10},{16,20},{18,... | collective-permute-start | bytes 786440 | tf_op jit(solution)/shard_map/ppermute | solution.py:430
  29.1 1.4 %collective-permute-start.3 = (bf16[2,296,128]{2,1,0:T(8,128)(2,1)S(1)}, bf16[2,296,128]{2,1,0:T(8,128)(2,1)S(1)}, u32[]{:S(2)}, u32[]{:S(2)}) collective-permute-start(bf16[2,296,128]{2,1,0:T(8,128)(2,1)S(1)} %get-tuple-element.66), channel_id=1, source_target_pairs={{0,2},{2,0},{4,6},{6,4},{8,10},{10,8},{12,14},{14,12},{16,18},{18,... | collective-permute-start | bytes 454664 | tf_op jit(solution)/shard_map/ppermute | solution.py:430
  29.2 1.6 %collective-permute-start.4 = (bf16[2,296,128]{2,1,0:T(8,128)(2,1)S(1)}, bf16[2,296,128]{2,1,0:T(8,128)(2,1)S(1)}, u32[]{:S(2)}, u32[]{:S(2)}) collective-permute-start(bf16[2,296,128]{2,1,0:T(8,128)(2,1)S(1)} %get-tuple-element.67), channel_id=1, source_target_pairs={{0,2},{2,0},{4,6},{6,4},{8,10},{10,8},{12,14},{14,12},{16,18},{18,... | collective-permute-start | bytes 454664 | tf_op jit(solution)/shard_map/ppermute | solution.py:430
  29.7 1.4 %collective-permute-start.5 = (bf16[2,296,128]{2,1,0:T(8,128)(2,1)S(1)}, bf16[2,296,128]{2,1,0:T(8,128)(2,1)S(1)}, u32[]{:S(2)}, u32[]{:S(2)}) collective-permute-start(bf16[2,296,128]{2,1,0:T(8,128)(2,1)S(1)} %get-tuple-element.68), channel_id=1, source_target_pairs={{0,2},{2,0},{4,6},{6,4},{8,10},{10,8},{12,14},{14,12},{16,18},{18,... | collective-permute-start | bytes 454664 | tf_op jit(solution)/shard_map/ppermute | solution.py:430
  29.8 1.5 %collective-permute-start.6 = (bf16[2,296,128]{2,1,0:T(8,128)(2,1)S(1)}, bf16[2,296,128]{2,1,0:T(8,128)(2,1)S(1)}, u32[]{:S(2)}, u32[]{:S(2)}) collective-permute-start(bf16[2,296,128]{2,1,0:T(8,128)(2,1)S(1)} %get-tuple-element.69), channel_id=1, source_target_pairs={{0,2},{2,0},{4,6},{6,4},{8,10},{10,8},{12,14},{14,12},{16,18},{18,... | collective-permute-start | bytes 454664 | tf_op jit(solution)/shard_map/ppermute | solution.py:430
  31.4 9.6 %collective-permute-start.8 = (bf16[2,552,128]{2,1,0:T(8,128)(2,1)S(1)}, bf16[2,552,128]{2,1,0:T(8,128)(2,1)S(1)}, u32[]{:S(2)}, u32[]{:S(2)}) collective-permute-start(bf16[2,552,128]{2,1,0:T(8,128)(2,1)S(1)} %pad_maximum_fusion), channel_id=1, source_target_pairs={{0,8},{1,9},{2,10},{3,11},{4,12},{5,13},{6,14},{7,15},{8,0},{9,1},... | collective-permute-start | bytes 847880 | tf_op jit(solution)/shard_map/ppermute | solution.py:446
  33.1 10.7 %collective-permute-start.10 = (bf16[2,296,128]{2,1,0:T(8,128)(2,1)S(1)}, bf16[2,296,128]{2,1,0:T(8,128)(2,1)S(1)}, u32[]{:S(2)}, u32[]{:S(2)}) collective-permute-start(bf16[2,296,128]{2,1,0:T(8,128)(2,1)S(1)} %add_convert_fusion.4), channel_id=1, source_target_pairs={{0,4},{1,5},{2,6},{3,7},{4,0},{5,1},{6,2},{7,3},{8,12},{9,13},{10,... | collective-permute-start | bytes 454664 | tf_op jit(solution)/shard_map/ppermute | solution.py:446
  33.9 9.9 %collective-permute-start.11 = (bf16[2,296,128]{2,1,0:T(8,128)(2,1)S(1)}, bf16[2,296,128]{2,1,0:T(8,128)(2,1)S(1)}, u32[]{:S(2)}, u32[]{:S(2)}) collective-permute-start(bf16[2,296,128]{2,1,0:T(8,128)(2,1)S(1)} %add_convert_fusion.3), channel_id=1, source_target_pairs={{0,12},{1,13},{2,14},{3,15},{4,8},{5,9},{6,10},{7,11},{8,4},{9,5},... | collective-permute-start | bytes 454664 | tf_op jit(solution)/shard_map/ppermute | solution.py:446
  41.1 7.0 %collective-permute-start.9 = (bf16[1,256,128]{2,1,0:T(8,128)(2,1)S(1)}, bf16[1,256,128]{2,1,0:T(8,128)(2,1)S(1)}, u32[]{:S(2)}, u32[]{:S(2)}) collective-permute-start(bf16[1,256,128]{2,1,0:T(8,128)(2,1)S(1)} %slice.50), channel_id=1, source_target_pairs={{0,16},{2,18},{4,20},{6,22},{8,24},{10,26},{12,28},{14,30},{16,0},... | collective-permute-start | bytes 196616 | tf_op jit(solution)/shard_map/ppermute | solution.py:430
  43.9 10.0 %collective-permute-start.14 = (bf16[296,128]{1,0:T(8,128)(2,1)S(1)}, bf16[296,128]{1,0:T(8,128)(2,1)S(1)}, u32[]{:S(2)}, u32[]{:S(2)}) collective-permute-start(bf16[296,128]{1,0:T(8,128)(2,1)S(1)} %get-tuple-element.83), channel_id=1, source_target_pairs={{0,17},{1,16},{2,19},{3,18},{4,21},{5,20},{6,23},{7,22},{8,25},{9,... | collective-permute-start | bytes 227336 | tf_op jit(solution)/shard_map/ppermute | solution.py:446
  48.1 6.5 %collective-permute-start.13 = (bf16[296,128]{1,0:T(8,128)(2,1)S(1)}, bf16[296,128]{1,0:T(8,128)(2,1)S(1)}, u32[]{:S(2)}, u32[]{:S(2)}) collective-permute-start(bf16[296,128]{1,0:T(8,128)(2,1)S(1)} %get-tuple-element.83), channel_id=1, source_target_pairs={{0,16},{1,17},{2,18},{3,19},{4,20},{5,21},{6,22},{7,23},{8,24},{9,... | collective-permute-start | bytes 227336 | tf_op jit(solution)/shard_map/ppermute | solution.py:446
  48.1 5.6 %collective-permute-start.12 = (bf16[552,128]{1,0:T(8,128)(2,1)S(1)}, bf16[552,128]{1,0:T(8,128)(2,1)S(1)}, u32[]{:S(2)}, u32[]{:S(2)}) collective-permute-start(bf16[552,128]{1,0:T(8,128)(2,1)S(1)} %pad_maximum_fusion.1), channel_id=1, source_target_pairs={{0,1},{1,0},{2,3},{3,2},{4,5},{5,4},{6,7},{7,6},{8,9},{9,8},{10,11... | collective-permute-start | bytes 423944 | tf_op jit(solution)/shard_map/ppermute | solution.py:446

commit v6 on v5

--- a/solution.py
+++ b/solution.py
@@ -132,12 +132,17 @@
 
 
 def prep_kernel(
-    meta_ref, x_ref, wr_ref, we_ref, wg_ref, s1_ref, b1_ref,
-    hid_ref, slope_ref, dense_ref, denset_ref, wet_ref,
+    x_ref, wr_ref, we_ref, wg_ref, s1_ref, b1_ref, s2_ref, b2_ref, s3_ref, b3_ref,
+    hid_ref, slope_ref, dense_ref, denset_ref, wet_ref, mid_ref, end_ref, part_ref, win_ref,
 ):
     scale = column(s1_ref)
     shift = column(b1_ref)
-    held = meta_ref[HELD]
+    mid_ref[0] = scale
+    mid_ref[1] = shift
+    mid_ref[2] = column(s2_ref)
+    mid_ref[3] = column(b2_ref)
+    end_ref[0] = column(s3_ref)
+    end_ref[1] = column(b3_ref)
     for half in range(SLOTS // 2):
         tiles = jnp.concatenate([x_ref[2 * half], x_ref[2 * half + 1]], axis=1)
         reduced = nn_dot(wr_ref[...], tiles)
@@ -147,11 +152,12 @@
             sig = sigmoid(pre)
             act = pre * sig
             hid_ref[i] = act.astype(BF)
-            live = jnp.where(i < held, 1.0, 0.0).astype(F32)
-            slope_ref[i] = (sig + act * (1.0 - sig)) * (scale * live)
+            slope_ref[i] = (sig + act * (1.0 - sig)) * scale
     tap_row = lax.broadcasted_iota(jnp.int32, (TAPS * GW, KDIM), 0)
     lane = lax.broadcasted_iota(jnp.int32, (TAPS * GW, KDIM), 1)
-    pick = (tap_row == (lane // HALF) * GW + lane % GW).astype(F32).astype(BF)
+    block = lane // HALF
+    tap = 3 * (block % 3) + jnp.where(block < 3, 1, jnp.where(block < 6, 0, 2))
+    pick = (tap_row == tap * GW + lane % GW).astype(F32).astype(BF)
     spread = tn_dot(wg_ref[...], pick)
     row = lax.broadcasted_iota(jnp.int32, (MID, KDIM), 0)
     col = lax.broadcasted_iota(jnp.int32, (MID, KDIM), 1)
@@ -168,6 +174,14 @@
         for b in range(2):
             denset_ref[b, :, k * HALF : (k + 1) * HALF] = spread_t[:, b * HALF : (b + 1) * HALF]
     wet_ref[...] = jnp.transpose(we_ref[...])
+    lane = lax.broadcasted_iota(jnp.int32, (HALF, PIX), 1)
+    for i in range(SLOTS):
+        for b in range(2):
+            shifts = row_shifts(hid_ref[i, b * HALF : (b + 1) * HALF, :], lane >= TW, lane < PIX - TW)
+            for u, shifted in enumerate(shifts):
+                win_ref[b, u * HALF : (u + 1) * HALF, i * PIX : (i + 1) * PIX] = shifted
+    for b in range(2):
+        part_ref[b * HALF : (b + 1) * HALF, :] = nn_dot(dense_ref[b, :, :MIDDLE], win_ref[b])
 
 
 def silu_slope(v):
@@ -176,14 +190,37 @@
     return act, sig + act * (1.0 - sig)
 
 
-def build_windows(field_ref, win_ref, meta_ref, tiles, first, transposed):
+MIDDLE = 3 * HALF
+
+
+def forward_place(u, v):
+    return (1, 0, 2)[v] * 3 + u
+
+
+def side_place(u, v):
+    return None if v == 1 else forward_place(u, v) - 3
+
+
+def transposed_place(u, v):
+    return TAPS - 1 - (3 * u + v)
+
+
+def row_shifts(base, has_above, has_below):
+    zero = jnp.zeros((), BF)
+    return (
+        jnp.where(has_above, pltpu.roll(base, TW, 1), zero),
+        base,
+        jnp.where(has_below, pltpu.roll(base, PIX - TW, 1), zero),
+    )
+
+
+def build_windows(field_ref, win_ref, meta_ref, tiles, first, place):
     lane = lax.broadcasted_iota(jnp.int32, (HALF, PIX), 1)
     col = lane % TW
     first_col = col == 0
     last_col = col == TW - 1
     has_above = lane >= TW
     has_below = lane < PIX - TW
-    zero = jnp.zeros((), BF)
     for i in tiles:
         left_at = meta_ref[L_IDX + i]
         right_at = meta_ref[R_IDX + i]
@@ -196,33 +233,23 @@
             west = jnp.where(first_col, pltpu.roll(left, PIX - TW + 1, 1), pltpu.roll(own, 1, 1))
             east = jnp.where(last_col, pltpu.roll(right, TW - 1, 1), pltpu.roll(own, PIX - 1, 1))
             for v, base in enumerate((west, own, east)):
-                above = jnp.where(has_above, pltpu.roll(base, TW, 1), zero)
-                below = jnp.where(has_below, pltpu.roll(base, PIX - TW, 1), zero)
-                for u, shifted in enumerate((above, base, below)):
-                    tap = 3 * u + v
-                    if transposed:
-                        tap = TAPS - 1 - tap
-                    win_ref[b, pl.ds(tap * HALF, HALF), lanes] = shifted
+                if place(0, v) is None:
+                    continue
+                for u, shifted in enumerate(row_shifts(base, has_above, has_below)):
+                    win_ref[b, pl.ds(place(u, v) * HALF, HALF), lanes] = shifted
 
 
 CHUNKS = ((0, 2), (2, 2))
 
 
 def forward_kernel(
-    devices, meta_ref, core_ref, other_ref, hid_in, wr_ref, s1_ref, b1_ref, dense_ref,
-    s2_ref, b2_ref, wet_ref, s3_ref, b3_ref, x_ref, g_ref,
+    devices, meta_ref, core_ref, other_ref, hid_in, wr_ref, dense_ref, wet_ref, mid_ref, end_ref, part_ref, x_ref, g_ref,
     out_ref, back_ref, errc_ref, slopeb_ref, hid_ref, edge_ref, hide_ref, slopee_ref, send_ref, keep_ref,
     win_ref, wine_ref, hidb_ref,
 ):
     me = lax.axis_index("tile")
     held = meta_ref[HELD]
     odd = me % 2
-    scale1 = column(s1_ref)
-    shift1 = column(b1_ref)
-    scale2 = column(s2_ref)
-    shift2 = column(b2_ref)
-    scale3 = column(s3_ref)
-    shift3 = column(b3_ref)
     core_first = jnp.where(odd == 0, 0, TW - 2)
     other_first = jnp.where(odd == 0, TW - 2, 0)
     edge_x = (
@@ -232,39 +259,39 @@
     edge_ref[...] = edge_x
     for i in range(SLOTS):
         hid_ref[i] = hid_in[i]
-    pre = nn_dot(wr_ref[...], edge_x) * scale1 + shift1
+    pre = nn_dot(wr_ref[...], edge_x) * mid_ref[0] + mid_ref[1]
     hid_ref[EDGE] = (pre * sigmoid(pre)).astype(BF)
     hid_ref[ZERO] = jnp.zeros((MID, PIX), BF)
 
-    build_windows(hid_ref, wine_ref, meta_ref, (EDGE,), EDGE, False)
+    build_windows(hid_ref, wine_ref, meta_ref, (EDGE,), EDGE, forward_place)
     for b in range(2):
         rows = slice(b * HALF, (b + 1) * HALF)
-        act, slope = silu_slope(nn_dot(dense_ref[b], wine_ref[b]) * scale2[rows] + shift2[rows])
+        act, slope = silu_slope(nn_dot(dense_ref[b], wine_ref[b]) * mid_ref[2, rows, :] + mid_ref[3, rows, :])
         hide_ref[rows, :] = act.astype(BF)
-        slopee_ref[rows, :] = slope * scale2[rows]
+        slopee_ref[rows, :] = slope * mid_ref[2, rows, :]
 
     for first, count in CHUNKS:
-        build_windows(hid_ref, win_ref, meta_ref, range(first, first + count), 0, False)
+        build_windows(hid_ref, win_ref, meta_ref, range(first, first + count), 0, side_place)
         lanes = slice(first * PIX, (first + count) * PIX)
         for b in range(2):
-            conv = nn_dot(dense_ref[b], win_ref[b, :, lanes])
             rows = slice(b * HALF, (b + 1) * HALF)
+            conv = nn_dot(dense_ref[b, :, MIDDLE:], win_ref[b, :, lanes]) + part_ref[rows, lanes]
             for k in range(count):
                 at = slice((first + k) * PIX, (first + k + 1) * PIX)
-                act, slope = silu_slope(conv[:, k * PIX : (k + 1) * PIX] * scale2[rows] + shift2[rows])
+                act, slope = silu_slope(conv[:, k * PIX : (k + 1) * PIX] * mid_ref[2, rows, :] + mid_ref[3, rows, :])
                 hidb_ref[rows, at] = act.astype(BF)
-                slopeb_ref[rows, at] = slope * scale2[rows]
+                slopeb_ref[rows, at] = slope * mid_ref[2, rows, :]
         grown = nn_dot(wet_ref[...], hidb_ref[:, lanes])
         for k in range(count):
             i = first + k
             act, slope = silu_slope(
-                grown[:, k * PIX : (k + 1) * PIX] * scale3 + shift3 + x_ref[i].astype(F32)
+                grown[:, k * PIX : (k + 1) * PIX] * end_ref[0] + end_ref[1] + x_ref[i].astype(F32)
             )
             live = jnp.where(i < held, 1.0, 0.0).astype(F32)
             back = g_ref[i].astype(F32) * slope * live
             out_ref[i] = (act * live).astype(BF)
             back_ref[i] = back
-            errc_ref[:, i * PIX : (i + 1) * PIX] = (back * scale3).astype(BF)
+            errc_ref[:, i * PIX : (i + 1) * PIX] = (back * end_ref[0]).astype(BF)
 
     own = SLOTS * PIX
     for ref, flip in ((send_ref, 1), (keep_ref, 0)):
@@ -290,7 +317,7 @@
 
 
 def pull_kernel(
-    core_ref, other_ref, hide_ref, slopee_ref, wet_ref, s3_ref, b3_ref,
+    core_ref, other_ref, hide_ref, slopee_ref, wet_ref, end_ref,
     edge_ref, we_ref, errc_ref, slopeb_ref, errb_ref,
 ):
     odd = lax.axis_index("tile") % 2
@@ -300,8 +327,6 @@
         tn_dot(core_ref[2 * TH :, :], edge_select(TH, g_lane(core_g)))
         + tn_dot(other_ref[2 * TH :, :], edge_select(TH, g_lane(other_g)))
     )
-    scale3 = column(s3_ref)
-    shift3 = column(b3_ref)
     for first, count in CHUNKS:
         lanes = slice(first * PIX, (first + count) * PIX)
         pulled = nn_dot(we_ref[...], errc_ref[:, lanes])
@@ -309,8 +334,8 @@
         for k in range(count):
             errb_ref[first + k] = errb[:, k * PIX : (k + 1) * PIX]
     grown = nn_dot(wet_ref[...], hide_ref[...])
-    _, slope = silu_slope(grown * scale3 + shift3 + edge_ref[...].astype(F32))
-    errc = (edge_g * slope * scale3).astype(BF)
+    _, slope = silu_slope(grown * end_ref[0] + end_ref[1] + edge_ref[...].astype(F32))
+    errc = (edge_g * slope * end_ref[0]).astype(BF)
     errb_ref[EDGE] = (nn_dot(we_ref[...], errc) * slopee_ref[...]).astype(BF)
     errb_ref[ZERO] = jnp.zeros((MID, PIX), BF)
 
@@ -322,15 +347,17 @@
     send_refs, keep_refs = rest[:4], rest[4:8]
     win_ref, flat_ref, groups_ref, kept_ref = rest[8:]
     me = lax.axis_index("tile")
+    held = meta_ref[HELD]
     for first, count in CHUNKS:
-        build_windows(errb_ref, win_ref, meta_ref, range(first, first + count), 0, True)
+        build_windows(errb_ref, win_ref, meta_ref, range(first, first + count), 0, transposed_place)
         lanes = slice(first * PIX, (first + count) * PIX)
         for b in range(2):
             conv = nn_dot(denset_ref[b], win_ref[b, :, lanes])
             rows = slice(b * HALF, (b + 1) * HALF)
             for k in range(count):
                 i = first + k
-                err = (conv[:, k * PIX : (k + 1) * PIX] * slope_ref[i, rows, :]).astype(BF)
+                live = jnp.where(i < held, 1.0, 0.0).astype(F32)
+                err = (conv[:, k * PIX : (k + 1) * PIX] * slope_ref[i, rows, :] * live).astype(BF)
                 flat_ref[rows, i * PIX : (i + 1) * PIX] = err
                 erra_ref[i, rows, :] = err
     row = lax.broadcasted_iota(jnp.int32, (HALF, HALF), 0)
@@ -401,7 +428,7 @@
     group_ref[:, PIX:] = tail[:, : TAPS * GW - PIX]
 
 
-LIMITS = {"edges": 56, "prep": 13, "forward": 26, "pull": 11, "backward": 18, "grads": 9, "finish": 2}
+LIMITS = {"edges": 56, "prep": 20, "forward": 28, "pull": 12, "backward": 18, "grads": 9, "finish": 2}
 WORK = {"edges": 2, "prep": 3, "forward": 7, "pull": 2, "backward": 5, "grads": 2, "finish": 1}
 
 
@@ -492,12 +519,13 @@
     from_other = lax.ppermute(to_other, "tile", hops + [(b, a) for a, b in hops])
     from_core = swap(to_core, "tile", 1)
 
-    hid, slope_a, dense, denset, wet = call(
+    hid, slope_a, dense, denset, wet, mid, end, part = call(
         prep_kernel, "prep",
         [shape((SLOTS, MID, PIX), BF), shape((SLOTS, MID, PIX), F32), shape((2, HALF, KDIM), BF),
-         shape((2, HALF, KDIM), BF), shape((CIN, MID), BF)],
-        (0,), (), 7,
-    )(meta, x, w_reduce, w_expand, w_group.T, s1, b1)
+         shape((2, HALF, KDIM), BF), shape((CIN, MID), BF), shape((4, MID, PIX), F32), shape((2, CIN, PIX), F32),
+         shape((MID, SLOTS * PIX), F32)],
+        (), (), 10, [pltpu.VMEM((2, MIDDLE, SLOTS * PIX), BF)],
+    )(x, w_reduce, w_expand, w_group.T, s1, b1, s2, b2, s3, b3)
 
     lanes = SLOTS * PIX
     act, back, errc, slope_b, hid, edge, hid_e, slope_e, e_send, e_keep = call(
@@ -505,14 +533,14 @@
         [shape((SLOTS, CIN, PIX), BF), shape((SLOTS, CIN, PIX), F32), shape((CIN, lanes), BF),
          shape((MID, lanes), F32), shape((SLOTS + 2, MID, PIX), BF), shape((CIN, PIX), BF),
          shape((MID, PIX), BF), shape((MID, PIX), F32), shape((devices // 2, 8 * per, PIX), BF), shape((devices // 2, 8 * per, PIX), BF)],
-        (0,), (), 15,
-        [pltpu.VMEM((2, KDIM, lanes), BF), pltpu.VMEM((2, KDIM, PIX), BF), pltpu.VMEM((MID, lanes), BF)],
-    )(meta, from_core, from_other, hid, w_reduce, s1, b1, dense, s2, b2, wet, s3, b3, x, g)
+        (0,), (), 12,
+        [pltpu.VMEM((2, KDIM - MIDDLE, lanes), BF), pltpu.VMEM((2, KDIM, PIX), BF), pltpu.VMEM((MID, lanes), BF)],
+    )(meta, from_core, from_other, hid, w_reduce, dense, wet, mid, end, part, x, g)
 
     e_core = swap(e_send, "tile", 1)
     (errb,) = call(
-        pull_kernel, "pull", [shape((SLOTS + 2, MID, PIX), BF)], (), (), 11,
-    )(from_core, from_other, hid_e, slope_e, wet, s3, b3, edge, w_expand, errc, slope_b)
+        pull_kernel, "pull", [shape((SLOTS + 2, MID, PIX), BF)], (), (), 10,
+    )(from_core, from_other, hid_e, slope_e, wet, end, edge, w_expand, errc, slope_b)
     e_part = add_pair(e_keep, e_core)
     errb, e_part = lax.optimization_barrier((errb, e_part))
     e_part = halve(e_part, 2)

time: 55.6 us -> 54.6 us (0.982)
  Pallas kernels: 23.3 us -> 22.4 us
  local copies, waits for them, and re-layouts: 0.76 us -> 0.12 us
    pallas_call x1, Pallas kernels: 6.96 us -> 6.02 us  [shards(): call(functools.partial(forward_kernel, devices), 'forward', [shape((SLOTS...]
    unnamed x26, local copies, waits for them, and re-layouts: 0.7 us -> 0.06 us
where the time goes in v6:
time: 54.6 us; the launch traced here: 54.4 us
  Pallas kernels  22.4 us (41%)
  starting transfers between devices  20.2 us (37%)
  waiting for transfers between devices  10.2 us (19%)
  between operations  1 us (2%)
  other arithmetic  0.57 us (1%)
    ppermute x8, starting transfers between devices, swap(): return lax.ppermute(value, axis, [(i, i ^ mask) for i in range(size)])  10.7 us
    ppermute x6, waiting for transfers between devices, cross(): return lax.ppermute(value, ('tile', 'slide'), pairs)  9.18 us
    ppermute x6, starting transfers between devices, cross(): return lax.ppermute(value, ('tile', 'slide'), pairs)  8.86 us
    pallas_call x1, Pallas kernels, shards(): call(functools.partial(forward_kernel, devices), 'forward', [shape((SLOTS...  6.02 us
    pallas_call x1, Pallas kernels, shards(): call(functools.partial(backward_kernel, devices), 'backward', [shape((SLO...  5.68 us
    pallas_call x1, Pallas kernels, shards(): call(prep_kernel, 'prep', [shape((SLOTS, MID, PIX), BF), shape((SLOTS, MI...  2.91 us
    pallas_call x1, Pallas kernels, shards(): call(edge_kernel, 'edges', [shape((PAY, CIN), BF), shape((PAY, CIN), BF),...  2.85 us
    pallas_call x1, Pallas kernels, shards(): call(grad_kernel, 'grads', [shape((SLOTS, CIN, PIX), BF), shape((SLOTS, C...  2.1 us
  transfers between devices with their start and end apart: 15, of which 8 were waited for; matrix products, arithmetic and copies ran while one was open for 1% of the time, Pallas kernels for 23%

profile of v6, /device:TPU:0, one launch (start us, length us, event | category | flops | bytes accessed | tf_op | source)
XLA Modules:
  0.0 54.4 jit_solution(3122935768159297411)
XLA Ops:
  0.6 0.0 copy-start.1
  0.6 0.0 copy-start.2
  0.7 0.0 copy-start.3
  0.7 0.0 copy-start.4
  0.7 0.0 copy-start.5
  0.7 0.0 copy-start.6
  0.7 0.0 copy-start.7
  0.7 0.0 copy-start.8
  0.7 0.0 copy-start.9
  0.7 0.0 copy-start.10
  0.7 2.8 %edges.1 = (bf16[48,1024]{1,0:T(8,128)(2,1)}, bf16[48,1024]{1,0:T(8,128)(2,1)}, s32[16]{0:T(128)}) custom-call(s32[1,16]{1,0:T(1,128)} %count_hbm.1, s32[1,31]{1,0:T(1,128)} %joined_hbm.1, bf16[4,1024,128]{2,1,0:T(8,128)(2,1)} %bitcast.19, bf16[4,1024,128]{2,1,0:T(8,128)(2,1)} %bitcast.17), custom_call_target="tpu_custom_call" | custom-call | flops 2200000000 | bytes 1048576 | tf_op jit(solution)/shard_map/edges/pallas_call | solution.py:510
  3.6 0.5 collective-permute-start
  4.1 0.7 %collective-permute-start.1 = (bf16[48,1024]{1,0:T(8,128)(2,1)}, bf16[48,1024]{1,0:T(8,128)(2,1)S(1)}, u32[]{:S(2)}, u32[]{:S(2)}) collective-permute-start(bf16[48,1024]{1,0:T(8,128)(2,1)} %get-tuple-element.49), channel_id=1, source_target_pairs={{2,4},{6,8},{10,12},{14,16},{18,20},{22,24},{26,28},{4,2},{8,6},{1... | collective-permute-start | bytes 294920 | tf_op jit(solution)/shard_map/ppermute | solution.py:519
  4.8 0.0 copy-done.1
  4.8 0.0 copy-done.2
  4.8 0.0 copy-done.3
  4.8 0.0 copy-done.4
  4.8 0.0 copy-done.5
  4.8 0.0 copy-done.6
  4.8 0.0 copy-done.7
  4.9 0.0 copy-done.8
  4.9 0.0 copy-done.9
  4.9 0.0 copy-done.10
  4.9 0.0 copy-start
  4.9 0.0 copy-start.12
  4.9 2.9 %prep.1 = (bf16[4,512,128]{2,1,0:T(8,128)(2,1)S(1)}, f32[4,512,128]{2,1,0:T(8,128)S(1)}, bf16[2,256,2304]{2,1,0:T(8,128)(2,1)S(1)}, bf16[2,256,2304]{2,1,0:T(8,1...) custom-call(bf16[4,1024,128]{2,1,0:T(8,128)(2,1)S(1)} %bitcast.20, ...), custom_call_target="tpu_custom_call" | custom-call | flops 3300000000 | bytes 1048576 | tf_op jit(solution)/shard_map/prep/pallas_call | solution.py:522
  7.8 0.0 collective-permute-done.core_ref
  7.8 0.0 collective-permute-done.1.other_ref
  7.9 6.0 %forward.1 = (bf16[4,1024,128]{2,1,0:T(8,128)(2,1)S(1)}, f32[4,1024,128]{2,1,0:T(8,128)S(1)}, bf16[1024,512]{1,0:T(8,128)(2,1)S(1)}, f32[512,512]{1,0:T(8,128)S(...) custom-call(s32[16]{0:T(128)S(1)} %copy-done.12, ...), custom_call_target="tpu_custom_call" | custom-call | flops 7699999744 | bytes 1048576 | tf_op jit(solution)/shard_map/forward/pallas_call | solution.py:531
  13.9 4.0 %collective-permute-start.2 = (bf16[8,256,128]{2,1,0:T(8,128)(2,1)S(1)}, bf16[8,256,128]{2,1,0:T(8,128)(2,1)S(1)}, u32[]{:S(2)}, u32[]{:S(2)}) collective-permute-start(bf16[8,256,128]{2,1,0:T(8,128)(2,1)S(1)} %get-tuple-element.62), channel_id=1, source_target_pairs={{0,2},{2,0},{4,6},{6,4},{8,10},{10,8},{12,14},{14,12},{16,18},{18,... | collective-permute-start | bytes 1572872 | tf_op jit(solution)/shard_map/ppermute | solution.py:457
  17.8 1.9 %pull.1.errb_ref = bf16[6,512,128]{2,1,0:T(8,128)(2,1)S(1)} custom-call(bf16[48,1024]{1,0:T(8,128)(2,1)S(1)} %collective-permute-done.core_ref, bf16[48,1024]{1,0:T(8,128)(2,1)S(1)} %collective-permute-done.1.other_ref, bf16[512,128]{1,0:T(8,128)(2,1)S(1)} %get-tuple-element.56.hide_ref, f32[512,128]{1,0:T(8,128)S(1)} %get-tuple-element.57.slopee_ref, ...), custom_call_target="tpu_custom_call" | custom-call | flops 2200000000 | bytes 1048576 | tf_op jit(solution)/shard_map/pull/pallas_call | solution.py:541
  19.8 0.0 collective-permute-done.2
  19.8 0.1 add_convert_fusion
  20.0 2.5 %collective-permute-start.7 = (bf16[4,256,128]{2,1,0:T(8,128)(2,1)S(1)}, bf16[4,256,128]{2,1,0:T(8,128)(2,1)S(1)}, u32[]{:S(2)}, u32[]{:S(2)}) collective-permute-start(bf16[4,256,128]{2,1,0:T(8,128)(2,1)S(1)} %slice.37), channel_id=1, source_target_pairs={{0,4},{2,6},{4,0},{6,2},{8,12},{10,14},{12,8},{14,10},{16,20},{18,... | collective-permute-start | bytes 786440 | tf_op jit(solution)/shard_map/ppermute | solution.py:457
  22.4 5.7 %backward.1 = (bf16[4,512,128]{2,1,0:T(8,128)(2,1)S(1)}, bf16[2,296,128]{2,1,0:T(8,128)(2,1)S(1)}, bf16[2,296,128]{2,1,0:T(8,128)(2,1)S(1)}, bf16[2,296,128]{2,1...) custom-call(s32[16]{0:T(128)S(1)} %copy-done.12, ...), custom_call_target="tpu_custom_call" | custom-call | flops 5500000256 | bytes 1048576 | tf_op jit(solution)/shard_map/backward/pallas_call | solution.py:549
  28.1 0.1 collective-permute-start.3
  28.2 0.5 collective-permute-start.4
  28.7 0.1 collective-permute-start.5
  28.8 0.4 collective-permute-start.6
  29.2 0.0 collective-permute-done.7
  29.2 0.1 add_convert_fusion.1
  29.3 0.3 collective-permute-done.3
  29.6 0.2 collective-permute-done.4
  29.8 0.3 collective-permute-done.5
  30.1 0.2 collective-permute-done.6
  30.3 0.1 add_convert_fusion.6
  30.4 1.6 %collective-permute-start.8 = (bf16[2,552,128]{2,1,0:T(8,128)(2,1)S(1)}, bf16[2,552,128]{2,1,0:T(8,128)(2,1)S(1)}, u32[]{:S(2)}, u32[]{:S(2)}) collective-permute-start(bf16[2,552,128]{2,1,0:T(8,128)(2,1)S(1)} %pad_maximum_fusion), channel_id=1, source_target_pairs={{0,8},{1,9},{2,10},{3,11},{4,12},{5,13},{6,14},{7,15},{8,0},{9,1},... | collective-permute-start | bytes 847880 | tf_op jit(solution)/shard_map/ppermute | solution.py:473
  32.1 0.7 %collective-permute-start.10 = (bf16[2,296,128]{2,1,0:T(8,128)(2,1)S(1)}, bf16[2,296,128]{2,1,0:T(8,128)(2,1)S(1)}, u32[]{:S(2)}, u32[]{:S(2)}) collective-permute-start(bf16[2,296,128]{2,1,0:T(8,128)(2,1)S(1)} %add_convert_fusion.4), channel_id=1, source_target_pairs={{0,4},{1,5},{2,6},{3,7},{4,0},{5,1},{6,2},{7,3},{8,12},{9,13},{10,... | collective-permute-start | bytes 454664 | tf_op jit(solution)/shard_map/ppermute | solution.py:473
  32.8 0.1 add_convert_fusion.3
  32.9 1.3 %collective-permute-start.11 = (bf16[2,296,128]{2,1,0:T(8,128)(2,1)S(1)}, bf16[2,296,128]{2,1,0:T(8,128)(2,1)S(1)}, u32[]{:S(2)}, u32[]{:S(2)}) collective-permute-start(bf16[2,296,128]{2,1,0:T(8,128)(2,1)S(1)} %add_convert_fusion.3), channel_id=1, source_target_pairs={{0,12},{1,13},{2,14},{3,15},{4,8},{5,9},{6,10},{7,11},{8,4},{9,5},... | collective-permute-start | bytes 454664 | tf_op jit(solution)/shard_map/ppermute | solution.py:473
  34.2 5.8 %collective-permute-done.8 = bf16[2,552,128]{2,1,0:T(8,128)(2,1)S(1)} collective-permute-done((bf16[2,552,128]{2,1,0:T(8,128)(2,1)S(1)}, bf16[2,552,128]{2,1,0:T(8,128)(2,1)S(1)}, u32[]{:S(2)}, u32[]{:S(2)}) %collective-permute-start.8) | collective-permute-done | bytes 282656 | tf_op jit(solution)/shard_map/ppermute | solution.py:473
  40.1 2.7 %collective-permute-start.9 = (bf16[1,256,128]{2,1,0:T(8,128)(2,1)S(1)}, bf16[1,256,128]{2,1,0:T(8,128)(2,1)S(1)}, u32[]{:S(2)}, u32[]{:S(2)}) collective-permute-start(bf16[1,256,128]{2,1,0:T(8,128)(2,1)S(1)} %slice.50), channel_id=1, source_target_pairs={{0,16},{2,18},{4,20},{6,22},{8,24},{10,26},{12,28},{14,30},{16,0},... | collective-permute-start | bytes 196616 | tf_op jit(solution)/shard_map/ppermute | solution.py:457
  42.8 0.0 collective-permute-done.10
  42.8 0.0 collective-permute-done.11
  42.8 0.1 add_convert_fusion.2
  42.9 4.2 %collective-permute-start.14 = (bf16[296,128]{1,0:T(8,128)(2,1)S(1)}, bf16[296,128]{1,0:T(8,128)(2,1)S(1)}, u32[]{:S(2)}, u32[]{:S(2)}) collective-permute-start(bf16[296,128]{1,0:T(8,128)(2,1)S(1)} %get-tuple-element.89), channel_id=1, source_target_pairs={{0,17},{1,16},{2,19},{3,18},{4,21},{5,20},{6,23},{7,22},{8,25},{9,... | collective-permute-start | bytes 227336 | tf_op jit(solution)/shard_map/ppermute | solution.py:473
  47.1 0.0 collective-permute-start.13
  47.1 0.0 collective-permute-done.9
  47.1 1.0 %collective-permute-start.12 = (bf16[552,128]{1,0:T(8,128)(2,1)S(1)}, bf16[552,128]{1,0:T(8,128)(2,1)S(1)}, u32[]{:S(2)}, u32[]{:S(2)}) collective-permute-start(bf16[552,128]{1,0:T(8,128)(2,1)S(1)} %pad_maximum_fusion.1), channel_id=1, source_target_pairs={{0,1},{1,0},{2,3},{3,2},{4,5},{5,4},{6,7},{7,6},{8,9},{9,8},{10,11... | collective-permute-start | bytes 423944 | tf_op jit(solution)/shard_map/ppermute | solution.py:473
  48.1 2.1 %grads.1 = (bf16[4,1024,128]{2,1,0:T(8,128)(2,1)}, bf16[4,1024,128]{2,1,0:T(8,128)(2,1)}) custom-call(bf16[512,1024]{1,0:T(8,128)(2,1)S(1)} %copy-done.3, bf16[4,512,128]{2,1,0:T(8,128)(2,1)S(1)} %get-tuple-element.67.erra_ref, f32[4,1024,128]{2,1,0:T(8,128)S(1)} %get-tuple-element.68.back_ref, bf16[4,1024,128]{2,1,0:T(8,128)(2,1)S(1)} %get-tuple-element.69.act_ref), custom_call_target="tpu_custom_call" | custom-call | flops 2200000000 | bytes 1048576 | tf_op jit(solution)/shard_map/grads/pallas_call | solution.py:555
  50.2 2.6 %collective-permute-done.12 = bf16[552,128]{1,0:T(8,128)(2,1)S(1)} collective-permute-done((bf16[552,128]{1,0:T(8,128)(2,1)S(1)}, bf16[552,128]{1,0:T(8,128)(2,1)S(1)}, u32[]{:S(2)}, u32[]{:S(2)}) %collective-permute-start.12) | collective-permute-done | bytes 141344 | tf_op jit(solution)/shard_map/ppermute | solution.py:473
  52.8 0.1 collective-permute-done.14.refs_3_
  52.9 0.7 %collective-permute-done.13.refs_2_ = bf16[296,128]{1,0:T(8,128)(2,1)S(1)} collective-permute-done((bf16[296,128]{1,0:T(8,128)(2,1)S(1)}, bf16[296,128]{1,0:T(8,128)(2,1)S(1)}, u32[]{:S(2)}, u32[]{:S(2)}) %collective-permute-start.13) | collective-permute-done | bytes 75808 | tf_op jit(solution)/shard_map/ppermute | solution.py:473
  53.6 0.9 %finish.1 = (f32[32,1024]{1,0:T(8,128)}, f32[32,144]{1,0:T(8,128)}, f32[32,1024]{1,0:T(8,128)}) custom-call(bf16[256,128]{1,0:T(8,128)(2,1)S(1)} %fusion.ea_ref, bf16[256,128]{1,0:T(8,128)(2,1)S(1)} %slice.53.eb_ref, bf16[296,128]{1,0:T(8,128)(2,1)S(1)} %get-tuple-element.90.refs_0_, bf16[296,128]{1,0:T(8,128)(2,1)S(1)} %slice.54.refs_1_, ...), custom_call_target="tpu_custom_call" | custom-call | flops 1100000000 | bytes 1048576 | tf_op jit(solution)/shard_map/finish/pallas_call | solution.py:596
  (15 shorter events, 0.2 us)
Async XLA Ops:
  0.6 4.1 %copy-start.1 = (bf16[512,1024]{1,0:T(8,128)(2,1)S(1)}, bf16[512,1024]{1,0:T(8,128)(2,1)}, u32[]{:S(2)}) copy-start(bf16[512,1024]{1,0:T(8,128)(2,1)} %we_ref.3) | copy-start | bytes 3145732
  0.6 4.1 %copy-start.2 = (bf16[1,4,1024,128]{3,2,1,0:T(8,128)(2,1)S(1)}, bf16[1,4,1024,128]{3,2,1,0:T(8,128)(2,1)}, u32[]{:S(2)}) copy-start(bf16[1,4,1024,128]{3,2,1,0:T(8,128)(2,1)} %param.14) | copy-start | bytes 3145732
  0.7 4.1 %copy-start.3 = (bf16[512,1024]{1,0:T(8,128)(2,1)S(1)}, bf16[512,1024]{1,0:T(8,128)(2,1)}, u32[]{:S(2)}) copy-start(bf16[512,1024]{1,0:T(8,128)(2,1)} %wr_ref.5) | copy-start | bytes 3145732
  0.7 4.1 %copy-start.4 = (bf16[512,144]{0,1:T(8,128)(2,1)S(1)}, bf16[512,144]{0,1:T(8,128)(2,1)}, u32[]{:S(2)}) copy-start(bf16[512,144]{0,1:T(8,128)(2,1)} %param.17) | copy-start | bytes 442372
  0.7 4.1 %copy-start.5 = (f32[1024]{0:T(1024)S(1)}, f32[1024]{0:T(1024)}, u32[]{:S(2)}) copy-start(f32[1024]{0:T(1024)} %param.23) | copy-start | bytes 12292
  0.7 4.1 %copy-start.6 = (f32[1024]{0:T(1024)S(1)}, f32[1024]{0:T(1024)}, u32[]{:S(2)}) copy-start(f32[1024]{0:T(1024)} %param.24) | copy-start | bytes 12292
  0.7 4.1 %copy-start.7 = (f32[512]{0:T(512)S(1)}, f32[512]{0:T(512)}, u32[]{:S(2)}) copy-start(f32[512]{0:T(512)} %param.19) | copy-start | bytes 6148
  0.7 4.1 %copy-start.8 = (f32[512]{0:T(512)S(1)}, f32[512]{0:T(512)}, u32[]{:S(2)}) copy-start(f32[512]{0:T(512)} %param.20) | copy-start | bytes 6148
  0.7 4.1 %copy-start.9 = (f32[512]{0:T(512)S(1)}, f32[512]{0:T(512)}, u32[]{:S(2)}) copy-start(f32[512]{0:T(512)} %param.21) | copy-start | bytes 6148
  0.7 4.1 %copy-start.10 = (f32[512]{0:T(512)S(1)}, f32[512]{0:T(512)}, u32[]{:S(2)}) copy-start(f32[512]{0:T(512)} %param.22) | copy-start | bytes 6148
  3.6 4.2 %collective-permute-start = (bf16[48,1024]{1,0:T(8,128)(2,1)}, bf16[48,1024]{1,0:T(8,128)(2,1)S(1)}, u32[]{:S(2)}, u32[]{:S(2)}) collective-permute-start(bf16[48,1024]{1,0:T(8,128)(2,1)} %get-tuple-element.48), channel_id=1, source_target_pairs={{0,2},{2,0},{4,6},{6,4},{8,10},{10,8},{12,14},{14,12},{16,18},{18,... | collective-permute-start | bytes 294920 | tf_op jit(solution)/shard_map/ppermute | solution.py:457
  4.1 3.7 %collective-permute-start.1 = (bf16[48,1024]{1,0:T(8,128)(2,1)}, bf16[48,1024]{1,0:T(8,128)(2,1)S(1)}, u32[]{:S(2)}, u32[]{:S(2)}) collective-permute-start(bf16[48,1024]{1,0:T(8,128)(2,1)} %get-tuple-element.49), channel_id=1, source_target_pairs={{2,4},{6,8},{10,12},{14,16},{18,20},{22,24},{26,28},{4,2},{8,6},{1... | collective-permute-start | bytes 294920 | tf_op jit(solution)/shard_map/ppermute | solution.py:519
  4.9 3.0 %copy-start = (bf16[1,4,1024,128]{3,2,1,0:T(8,128)(2,1)S(1)}, bf16[1,4,1024,128]{3,2,1,0:T(8,128)(2,1)}, u32[]{:S(2)}) copy-start(bf16[1,4,1024,128]{3,2,1,0:T(8,128)(2,1)} %param.15) | copy-start | bytes 3145732
  4.9 3.0 %copy-start.12 = (s32[16]{0:T(128)S(1)}, s32[16]{0:T(128)}, u32[]{:S(2)}) copy-start(s32[16]{0:T(128)} %get-tuple-element.47.meta_ref) | copy-start | bytes 196
  13.9 5.9 %collective-permute-start.2 = (bf16[8,256,128]{2,1,0:T(8,128)(2,1)S(1)}, bf16[8,256,128]{2,1,0:T(8,128)(2,1)S(1)}, u32[]{:S(2)}, u32[]{:S(2)}) collective-permute-start(bf16[8,256,128]{2,1,0:T(8,128)(2,1)S(1)} %get-tuple-element.62), channel_id=1, source_target_pairs={{0,2},{2,0},{4,6},{6,4},{8,10},{10,8},{12,14},{14,12},{16,18},{18,... | collective-permute-start | bytes 1572872 | tf_op jit(solution)/shard_map/ppermute | solution.py:457
  17.8 4.6 %copy-start.11 = (bf16[2304,256]{1,0:T(8,128)(2,1)S(1)}, bf16[2304,256]{1,0:T(8,128)(2,1)}, u32[]{:S(2)}) copy-start(bf16[2304,256]{1,0:T(8,128)(2,1)} %constant.2.clone.place_ref) | copy-start | bytes 3538948
  20.0 9.2 %collective-permute-start.7 = (bf16[4,256,128]{2,1,0:T(8,128)(2,1)S(1)}, bf16[4,256,128]{2,1,0:T(8,128)(2,1)S(1)}, u32[]{:S(2)}, u32[]{:S(2)}) collective-permute-start(bf16[4,256,128]{2,1,0:T(8,128)(2,1)S(1)} %slice.37), channel_id=1, source_target_pairs={{0,4},{2,6},{4,0},{6,2},{8,12},{10,14},{12,8},{14,10},{16,20},{18,... | collective-permute-start | bytes 786440 | tf_op jit(solution)/shard_map/ppermute | solution.py:457
  28.1 1.4 %collective-permute-start.3 = (bf16[2,296,128]{2,1,0:T(8,128)(2,1)S(1)}, bf16[2,296,128]{2,1,0:T(8,128)(2,1)S(1)}, u32[]{:S(2)}, u32[]{:S(2)}) collective-permute-start(bf16[2,296,128]{2,1,0:T(8,128)(2,1)S(1)} %get-tuple-element.72), channel_id=1, source_target_pairs={{0,2},{2,0},{4,6},{6,4},{8,10},{10,8},{12,14},{14,12},{16,18},{18,... | collective-permute-start | bytes 454664 | tf_op jit(solution)/shard_map/ppermute | solution.py:457
  28.2 1.6 %collective-permute-start.4 = (bf16[2,296,128]{2,1,0:T(8,128)(2,1)S(1)}, bf16[2,296,128]{2,1,0:T(8,128)(2,1)S(1)}, u32[]{:S(2)}, u32[]{:S(2)}) collective-permute-start(bf16[2,296,128]{2,1,0:T(8,128)(2,1)S(1)} %get-tuple-element.73), channel_id=1, source_target_pairs={{0,2},{2,0},{4,6},{6,4},{8,10},{10,8},{12,14},{14,12},{16,18},{18,... | collective-permute-start | bytes 454664 | tf_op jit(solution)/shard_map/ppermute | solution.py:457
  28.7 1.4 %collective-permute-start.5 = (bf16[2,296,128]{2,1,0:T(8,128)(2,1)S(1)}, bf16[2,296,128]{2,1,0:T(8,128)(2,1)S(1)}, u32[]{:S(2)}, u32[]{:S(2)}) collective-permute-start(bf16[2,296,128]{2,1,0:T(8,128)(2,1)S(1)} %get-tuple-element.74), channel_id=1, source_target_pairs={{0,2},{2,0},{4,6},{6,4},{8,10},{10,8},{12,14},{14,12},{16,18},{18,... | collective-permute-start | bytes 454664 | tf_op jit(solution)/shard_map/ppermute | solution.py:457
  28.8 1.5 %collective-permute-start.6 = (bf16[2,296,128]{2,1,0:T(8,128)(2,1)S(1)}, bf16[2,296,128]{2,1,0:T(8,128)(2,1)S(1)}, u32[]{:S(2)}, u32[]{:S(2)}) collective-permute-start(bf16[2,296,128]{2,1,0:T(8,128)(2,1)S(1)} %get-tuple-element.75), channel_id=1, source_target_pairs={{0,2},{2,0},{4,6},{6,4},{8,10},{10,8},{12,14},{14,12},{16,18},{18,... | collective-permute-start | bytes 454664 | tf_op jit(solution)/shard_map/ppermute | solution.py:457
  30.4 9.6 %collective-permute-start.8 = (bf16[2,552,128]{2,1,0:T(8,128)(2,1)S(1)}, bf16[2,552,128]{2,1,0:T(8,128)(2,1)S(1)}, u32[]{:S(2)}, u32[]{:S(2)}) collective-permute-start(bf16[2,552,128]{2,1,0:T(8,128)(2,1)S(1)} %pad_maximum_fusion), channel_id=1, source_target_pairs={{0,8},{1,9},{2,10},{3,11},{4,12},{5,13},{6,14},{7,15},{8,0},{9,1},... | collective-permute-start | bytes 847880 | tf_op jit(solution)/shard_map/ppermute | solution.py:473
  32.1 10.7 %collective-permute-start.10 = (bf16[2,296,128]{2,1,0:T(8,128)(2,1)S(1)}, bf16[2,296,128]{2,1,0:T(8,128)(2,1)S(1)}, u32[]{:S(2)}, u32[]{:S(2)}) collective-permute-start(bf16[2,296,128]{2,1,0:T(8,128)(2,1)S(1)} %add_convert_fusion.4), channel_id=1, source_target_pairs={{0,4},{1,5},{2,6},{3,7},{4,0},{5,1},{6,2},{7,3},{8,12},{9,13},{10,... | collective-permute-start | bytes 454664 | tf_op jit(solution)/shard_map/ppermute | solution.py:473
  32.9 9.9 %collective-permute-start.11 = (bf16[2,296,128]{2,1,0:T(8,128)(2,1)S(1)}, bf16[2,296,128]{2,1,0:T(8,128)(2,1)S(1)}, u32[]{:S(2)}, u32[]{:S(2)}) collective-permute-start(bf16[2,296,128]{2,1,0:T(8,128)(2,1)S(1)} %add_convert_fusion.3), channel_id=1, source_target_pairs={{0,12},{1,13},{2,14},{3,15},{4,8},{5,9},{6,10},{7,11},{8,4},{9,5},... | collective-permute-start | bytes 454664 | tf_op jit(solution)/shard_map/ppermute | solution.py:473
  40.1 7.0 %collective-permute-start.9 = (bf16[1,256,128]{2,1,0:T(8,128)(2,1)S(1)}, bf16[1,256,128]{2,1,0:T(8,128)(2,1)S(1)}, u32[]{:S(2)}, u32[]{:S(2)}) collective-permute-start(bf16[1,256,128]{2,1,0:T(8,128)(2,1)S(1)} %slice.50), channel_id=1, source_target_pairs={{0,16},{2,18},{4,20},{6,22},{8,24},{10,26},{12,28},{14,30},{16,0},... | collective-permute-start | bytes 196616 | tf_op jit(solution)/shard_map/ppermute | solution.py:457
  42.9 10.0 %collective-permute-start.14 = (bf16[296,128]{1,0:T(8,128)(2,1)S(1)}, bf16[296,128]{1,0:T(8,128)(2,1)S(1)}, u32[]{:S(2)}, u32[]{:S(2)}) collective-permute-start(bf16[296,128]{1,0:T(8,128)(2,1)S(1)} %get-tuple-element.89), channel_id=1, source_target_pairs={{0,17},{1,16},{2,19},{3,18},{4,21},{5,20},{6,23},{7,22},{8,25},{9,... | collective-permute-start | bytes 227336 | tf_op jit(solution)/shard_map/ppermute | solution.py:473
  47.1 6.5 %collective-permute-start.13 = (bf16[296,128]{1,0:T(8,128)(2,1)S(1)}, bf16[296,128]{1,0:T(8,128)(2,1)S(1)}, u32[]{:S(2)}, u32[]{:S(2)}) collective-permute-start(bf16[296,128]{1,0:T(8,128)(2,1)S(1)} %get-tuple-element.89), channel_id=1, source_target_pairs={{0,16},{1,17},{2,18},{3,19},{4,20},{5,21},{6,22},{7,23},{8,24},{9,... | collective-permute-start | bytes 227336 | tf_op jit(solution)/shard_map/ppermute | solution.py:473
  47.1 5.6 %collective-permute-start.12 = (bf16[552,128]{1,0:T(8,128)(2,1)S(1)}, bf16[552,128]{1,0:T(8,128)(2,1)S(1)}, u32[]{:S(2)}, u32[]{:S(2)}) collective-permute-start(bf16[552,128]{1,0:T(8,128)(2,1)S(1)} %pad_maximum_fusion.1), channel_id=1, source_target_pairs={{0,1},{1,0},{2,3},{3,2},{4,5},{5,4},{6,7},{7,6},{8,9},{9,8},{10,11... | collective-permute-start | bytes 423944 | tf_op jit(solution)/shard_map/ppermute | solution.py:473

commit v7 on v6

--- a/solution.py
+++ b/solution.py
@@ -76,8 +76,15 @@
         pltpu.make_async_copy(count_hbm, count_ref, sems.at[2]),
         pltpu.make_async_copy(joined_hbm, joined_ref, sems.at[3]),
     ]
-    loads = [pltpu.make_async_copy(x_any, xbuf, sems.at[0]), pltpu.make_async_copy(g_any, gbuf, sems.at[1])]
-    for copy in tables + loads:
+    firsts = [
+        pltpu.make_async_copy(x_any.at[0], xbuf.at[0], sems.at[0]),
+        pltpu.make_async_copy(g_any.at[0], gbuf.at[0], sems.at[1]),
+    ]
+    loads = [
+        pltpu.make_async_copy(x_any.at[1:], xbuf.at[1:], sems.at[4]),
+        pltpu.make_async_copy(g_any.at[1:], gbuf.at[1:], sems.at[5]),
+    ]
+    for copy in tables + firsts + loads:
         copy.start()
     for copy in tables:
         copy.wait()
@@ -103,7 +110,7 @@
     meta_ref[L_IDX + EDGE] = joined_to(start + last, last)
     meta_ref[R_IDX + EDGE] = joined_to(start - 1, 0)
 
-    for copy in loads:
+    for copy in firsts:
         copy.wait()
     even = me % 2 == 0
 
@@ -114,6 +121,8 @@
         )
 
     left_x, left_g = payload(0, 0, 0)
+    for copy in loads:
+        copy.wait()
     right_x, right_g = payload(last, TW - 2, TW - 1)
 
     @pl.when(even)
@@ -428,7 +437,7 @@
     group_ref[:, PIX:] = tail[:, : TAPS * GW - PIX]
 
 
-LIMITS = {"edges": 56, "prep": 20, "forward": 28, "pull": 12, "backward": 18, "grads": 9, "finish": 2}
+LIMITS = {"edges": 56, "prep": 18, "forward": 25, "pull": 12, "backward": 18, "grads": 9, "finish": 2}
 WORK = {"edges": 2, "prep": 3, "forward": 7, "pull": 2, "backward": 5, "grads": 2, "finish": 1}
 
 
@@ -512,7 +521,7 @@
         [shape((PAY, CIN), BF), shape((PAY, CIN), BF), shape((META,), jnp.int32)],
         (), (0, 1, 2, 3), 4,
         [pltpu.SMEM(tile_count.shape, jnp.int32), pltpu.SMEM(joined.shape, jnp.int32),
-         pltpu.VMEM((SLOTS, CIN, PIX), BF), pltpu.VMEM((SLOTS, CIN, PIX), BF), pltpu.SemaphoreType.DMA((4,))],
+         pltpu.VMEM((SLOTS, CIN, PIX), BF), pltpu.VMEM((SLOTS, CIN, PIX), BF), pltpu.SemaphoreType.DMA((6,))],
         (2,),
     )(tile_count, joined, x, g)
     hops = [(i, i + 1) for i in range(1, devices - 1, 2)]

time: 54.6 us -> 54.4 us (level)
  no operation moved by 1% of the time
where the time goes in v7:
time: 54.4 us; the launch traced here: 54.3 us
  Pallas kernels  22.2 us (41%)
  starting transfers between devices  20.2 us (37%)
  waiting for transfers between devices  10.2 us (19%)
  between operations  1 us (2%)
  other arithmetic  0.57 us (1%)
    ppermute x8, starting transfers between devices, swap(): return lax.ppermute(value, axis, [(i, i ^ mask) for i in range(size)])  10.7 us
    ppermute x6, waiting for transfers between devices, cross(): return lax.ppermute(value, ('tile', 'slide'), pairs)  9.17 us
    ppermute x6, starting transfers between devices, cross(): return lax.ppermute(value, ('tile', 'slide'), pairs)  8.87 us
    pallas_call x1, Pallas kernels, shards(): call(functools.partial(forward_kernel, devices), 'forward', [shape((SLOTS...  6.02 us
    pallas_call x1, Pallas kernels, shards(): call(functools.partial(backward_kernel, devices), 'backward', [shape((SLO...  5.69 us
    pallas_call x1, Pallas kernels, shards(): call(prep_kernel, 'prep', [shape((SLOTS, MID, PIX), BF), shape((SLOTS, MI...  2.91 us
    pallas_call x1, Pallas kernels, shards(): call(edge_kernel, 'edges', [shape((PAY, CIN), BF), shape((PAY, CIN), BF),...  2.7 us
    pallas_call x1, Pallas kernels, shards(): call(grad_kernel, 'grads', [shape((SLOTS, CIN, PIX), BF), shape((SLOTS, C...  2.09 us
  transfers between devices with their start and end apart: 15, of which 8 were waited for; matrix products, arithmetic and copies ran while one was open for 1% of the time, Pallas kernels for 23%

profile of v7, /device:TPU:0, one launch (start us, length us, event | category | flops | bytes accessed | tf_op | source)
XLA Modules:
  0.0 54.3 jit_solution(8709140935121182894)
XLA Ops:
  0.6 0.0 copy-start.1
  0.6 0.0 copy-start.2
  0.7 0.0 copy-start.3
  0.7 0.0 copy-start.4
  0.7 0.0 copy-start.5
  0.7 0.0 copy-start.6
  0.7 0.0 copy-start.7
  0.7 0.0 copy-start.8
  0.7 0.0 copy-start.9
  0.7 0.0 copy-start.10
  0.7 2.7 %edges.1 = (bf16[48,1024]{1,0:T(8,128)(2,1)}, bf16[48,1024]{1,0:T(8,128)(2,1)}, s32[16]{0:T(128)}) custom-call(s32[1,16]{1,0:T(1,128)} %count_hbm.1, s32[1,31]{1,0:T(1,128)} %joined_hbm.1, bf16[4,1024,128]{2,1,0:T(8,128)(2,1)} %bitcast.19, bf16[4,1024,128]{2,1,0:T(8,128)(2,1)} %bitcast.17), custom_call_target="tpu_custom_call" | custom-call | flops 2200000000 | bytes 1048576 | tf_op jit(solution)/shard_map/edges/pallas_call | solution.py:519
  3.4 0.5 collective-permute-start
  4.0 0.7 %collective-permute-start.1 = (bf16[48,1024]{1,0:T(8,128)(2,1)}, bf16[48,1024]{1,0:T(8,128)(2,1)S(1)}, u32[]{:S(2)}, u32[]{:S(2)}) collective-permute-start(bf16[48,1024]{1,0:T(8,128)(2,1)} %get-tuple-element.49), channel_id=1, source_target_pairs={{2,4},{6,8},{10,12},{14,16},{18,20},{22,24},{26,28},{4,2},{8,6},{1... | collective-permute-start | bytes 294920 | tf_op jit(solution)/shard_map/ppermute | solution.py:528
  4.6 0.0 copy-done.1
  4.6 0.0 copy-done.2
  4.7 0.0 copy-done.3
  4.7 0.0 copy-done.4
  4.7 0.0 copy-done.5
  4.7 0.0 copy-done.6
  4.7 0.0 copy-done.7
  4.7 0.0 copy-done.8
  4.7 0.0 copy-done.9
  4.7 0.0 copy-done.10
  4.7 0.0 copy-start
  4.7 0.0 copy-start.12
  4.8 2.9 %prep.1 = (bf16[4,512,128]{2,1,0:T(8,128)(2,1)S(1)}, f32[4,512,128]{2,1,0:T(8,128)S(1)}, bf16[2,256,2304]{2,1,0:T(8,128)(2,1)S(1)}, bf16[2,256,2304]{2,1,0:T(8,1...) custom-call(bf16[4,1024,128]{2,1,0:T(8,128)(2,1)S(1)} %bitcast.20, ...), custom_call_target="tpu_custom_call" | custom-call | flops 3300000000 | bytes 1048576 | tf_op jit(solution)/shard_map/prep/pallas_call | solution.py:531
  7.7 0.0 collective-permute-done.core_ref
  7.7 0.0 collective-permute-done.1.other_ref
  7.7 6.0 %forward.1 = (bf16[4,1024,128]{2,1,0:T(8,128)(2,1)S(1)}, f32[4,1024,128]{2,1,0:T(8,128)S(1)}, bf16[1024,512]{1,0:T(8,128)(2,1)S(1)}, f32[512,512]{1,0:T(8,128)S(...) custom-call(s32[16]{0:T(128)S(1)} %copy-done.12, ...), custom_call_target="tpu_custom_call" | custom-call | flops 7699999744 | bytes 1048576 | tf_op jit(solution)/shard_map/forward/pallas_call | solution.py:540
  13.7 4.0 %collective-permute-start.2 = (bf16[8,256,128]{2,1,0:T(8,128)(2,1)S(1)}, bf16[8,256,128]{2,1,0:T(8,128)(2,1)S(1)}, u32[]{:S(2)}, u32[]{:S(2)}) collective-permute-start(bf16[8,256,128]{2,1,0:T(8,128)(2,1)S(1)} %get-tuple-element.62), channel_id=1, source_target_pairs={{0,2},{2,0},{4,6},{6,4},{8,10},{10,8},{12,14},{14,12},{16,18},{18,... | collective-permute-start | bytes 1572872 | tf_op jit(solution)/shard_map/ppermute | solution.py:466
  17.7 1.9 %pull.1.errb_ref = bf16[6,512,128]{2,1,0:T(8,128)(2,1)S(1)} custom-call(bf16[48,1024]{1,0:T(8,128)(2,1)S(1)} %collective-permute-done.core_ref, bf16[48,1024]{1,0:T(8,128)(2,1)S(1)} %collective-permute-done.1.other_ref, bf16[512,128]{1,0:T(8,128)(2,1)S(1)} %get-tuple-element.56.hide_ref, f32[512,128]{1,0:T(8,128)S(1)} %get-tuple-element.57.slopee_ref, ...), custom_call_target="tpu_custom_call" | custom-call | flops 2200000000 | bytes 1048576 | tf_op jit(solution)/shard_map/pull/pallas_call | solution.py:550
  19.6 0.0 collective-permute-done.2
  19.6 0.1 add_convert_fusion
  19.8 2.5 %collective-permute-start.7 = (bf16[4,256,128]{2,1,0:T(8,128)(2,1)S(1)}, bf16[4,256,128]{2,1,0:T(8,128)(2,1)S(1)}, u32[]{:S(2)}, u32[]{:S(2)}) collective-permute-start(bf16[4,256,128]{2,1,0:T(8,128)(2,1)S(1)} %slice.37), channel_id=1, source_target_pairs={{0,4},{2,6},{4,0},{6,2},{8,12},{10,14},{12,8},{14,10},{16,20},{18,... | collective-permute-start | bytes 786440 | tf_op jit(solution)/shard_map/ppermute | solution.py:466
  22.3 5.7 %backward.1 = (bf16[4,512,128]{2,1,0:T(8,128)(2,1)S(1)}, bf16[2,296,128]{2,1,0:T(8,128)(2,1)S(1)}, bf16[2,296,128]{2,1,0:T(8,128)(2,1)S(1)}, bf16[2,296,128]{2,1...) custom-call(s32[16]{0:T(128)S(1)} %copy-done.12, ...), custom_call_target="tpu_custom_call" | custom-call | flops 5500000256 | bytes 1048576 | tf_op jit(solution)/shard_map/backward/pallas_call | solution.py:558
  28.0 0.1 collective-permute-start.3
  28.1 0.5 collective-permute-start.4
  28.6 0.1 collective-permute-start.5
  28.6 0.4 collective-permute-start.6
  29.1 0.0 collective-permute-done.7
  29.1 0.1 add_convert_fusion.1
  29.1 0.3 collective-permute-done.3
  29.4 0.2 collective-permute-done.4
  29.6 0.3 collective-permute-done.5
  29.9 0.2 collective-permute-done.6
  30.2 0.1 add_convert_fusion.6
  30.2 1.6 %collective-permute-start.8 = (bf16[2,552,128]{2,1,0:T(8,128)(2,1)S(1)}, bf16[2,552,128]{2,1,0:T(8,128)(2,1)S(1)}, u32[]{:S(2)}, u32[]{:S(2)}) collective-permute-start(bf16[2,552,128]{2,1,0:T(8,128)(2,1)S(1)} %pad_maximum_fusion), channel_id=1, source_target_pairs={{0,8},{1,9},{2,10},{3,11},{4,12},{5,13},{6,14},{7,15},{8,0},{9,1},... | collective-permute-start | bytes 847880 | tf_op jit(solution)/shard_map/ppermute | solution.py:482
  31.9 0.7 %collective-permute-start.10 = (bf16[2,296,128]{2,1,0:T(8,128)(2,1)S(1)}, bf16[2,296,128]{2,1,0:T(8,128)(2,1)S(1)}, u32[]{:S(2)}, u32[]{:S(2)}) collective-permute-start(bf16[2,296,128]{2,1,0:T(8,128)(2,1)S(1)} %add_convert_fusion.4), channel_id=1, source_target_pairs={{0,4},{1,5},{2,6},{3,7},{4,0},{5,1},{6,2},{7,3},{8,12},{9,13},{10,... | collective-permute-start | bytes 454664 | tf_op jit(solution)/shard_map/ppermute | solution.py:482
  32.6 0.1 add_convert_fusion.3
  32.7 1.3 %collective-permute-start.11 = (bf16[2,296,128]{2,1,0:T(8,128)(2,1)S(1)}, bf16[2,296,128]{2,1,0:T(8,128)(2,1)S(1)}, u32[]{:S(2)}, u32[]{:S(2)}) collective-permute-start(bf16[2,296,128]{2,1,0:T(8,128)(2,1)S(1)} %add_convert_fusion.3), channel_id=1, source_target_pairs={{0,12},{1,13},{2,14},{3,15},{4,8},{5,9},{6,10},{7,11},{8,4},{9,5},... | collective-permute-start | bytes 454664 | tf_op jit(solution)/shard_map/ppermute | solution.py:482
  34.0 5.9 %collective-permute-done.8 = bf16[2,552,128]{2,1,0:T(8,128)(2,1)S(1)} collective-permute-done((bf16[2,552,128]{2,1,0:T(8,128)(2,1)S(1)}, bf16[2,552,128]{2,1,0:T(8,128)(2,1)S(1)}, u32[]{:S(2)}, u32[]{:S(2)}) %collective-permute-start.8) | collective-permute-done | bytes 282656 | tf_op jit(solution)/shard_map/ppermute | solution.py:482
  39.9 2.6 %collective-permute-start.9 = (bf16[1,256,128]{2,1,0:T(8,128)(2,1)S(1)}, bf16[1,256,128]{2,1,0:T(8,128)(2,1)S(1)}, u32[]{:S(2)}, u32[]{:S(2)}) collective-permute-start(bf16[1,256,128]{2,1,0:T(8,128)(2,1)S(1)} %slice.50), channel_id=1, source_target_pairs={{0,16},{2,18},{4,20},{6,22},{8,24},{10,26},{12,28},{14,30},{16,0},... | collective-permute-start | bytes 196616 | tf_op jit(solution)/shard_map/ppermute | solution.py:466
  42.6 0.0 collective-permute-done.10
  42.6 0.0 collective-permute-done.11
  42.6 0.1 add_convert_fusion.2
  42.7 4.2 %collective-permute-start.14 = (bf16[296,128]{1,0:T(8,128)(2,1)S(1)}, bf16[296,128]{1,0:T(8,128)(2,1)S(1)}, u32[]{:S(2)}, u32[]{:S(2)}) collective-permute-start(bf16[296,128]{1,0:T(8,128)(2,1)S(1)} %get-tuple-element.89), channel_id=1, source_target_pairs={{0,17},{1,16},{2,19},{3,18},{4,21},{5,20},{6,23},{7,22},{8,25},{9,... | collective-permute-start | bytes 227336 | tf_op jit(solution)/shard_map/ppermute | solution.py:482
  46.9 0.0 collective-permute-start.13
  46.9 0.0 collective-permute-done.9
  47.0 1.0 %collective-permute-start.12 = (bf16[552,128]{1,0:T(8,128)(2,1)S(1)}, bf16[552,128]{1,0:T(8,128)(2,1)S(1)}, u32[]{:S(2)}, u32[]{:S(2)}) collective-permute-start(bf16[552,128]{1,0:T(8,128)(2,1)S(1)} %pad_maximum_fusion.1), channel_id=1, source_target_pairs={{0,1},{1,0},{2,3},{3,2},{4,5},{5,4},{6,7},{7,6},{8,9},{9,8},{10,11... | collective-permute-start | bytes 423944 | tf_op jit(solution)/shard_map/ppermute | solution.py:482
  48.0 2.1 %grads.1 = (bf16[4,1024,128]{2,1,0:T(8,128)(2,1)}, bf16[4,1024,128]{2,1,0:T(8,128)(2,1)}) custom-call(bf16[512,1024]{1,0:T(8,128)(2,1)S(1)} %copy-done.3, bf16[4,512,128]{2,1,0:T(8,128)(2,1)S(1)} %get-tuple-element.67.erra_ref, f32[4,1024,128]{2,1,0:T(8,128)S(1)} %get-tuple-element.68.back_ref, bf16[4,1024,128]{2,1,0:T(8,128)(2,1)S(1)} %get-tuple-element.69.act_ref), custom_call_target="tpu_custom_call" | custom-call | flops 2200000000 | bytes 1048576 | tf_op jit(solution)/shard_map/grads/pallas_call | solution.py:564
  50.1 2.5 %collective-permute-done.12 = bf16[552,128]{1,0:T(8,128)(2,1)S(1)} collective-permute-done((bf16[552,128]{1,0:T(8,128)(2,1)S(1)}, bf16[552,128]{1,0:T(8,128)(2,1)S(1)}, u32[]{:S(2)}, u32[]{:S(2)}) %collective-permute-start.12) | collective-permute-done | bytes 141344 | tf_op jit(solution)/shard_map/ppermute | solution.py:482
  52.6 0.1 collective-permute-done.14.refs_3_
  52.7 0.7 %collective-permute-done.13.refs_2_ = bf16[296,128]{1,0:T(8,128)(2,1)S(1)} collective-permute-done((bf16[296,128]{1,0:T(8,128)(2,1)S(1)}, bf16[296,128]{1,0:T(8,128)(2,1)S(1)}, u32[]{:S(2)}, u32[]{:S(2)}) %collective-permute-start.13) | collective-permute-done | bytes 75808 | tf_op jit(solution)/shard_map/ppermute | solution.py:482
  53.4 0.9 %finish.1 = (f32[32,1024]{1,0:T(8,128)}, f32[32,144]{1,0:T(8,128)}, f32[32,1024]{1,0:T(8,128)}) custom-call(bf16[256,128]{1,0:T(8,128)(2,1)S(1)} %fusion.ea_ref, bf16[256,128]{1,0:T(8,128)(2,1)S(1)} %slice.53.eb_ref, bf16[296,128]{1,0:T(8,128)(2,1)S(1)} %get-tuple-element.90.refs_0_, bf16[296,128]{1,0:T(8,128)(2,1)S(1)} %slice.54.refs_1_, ...), custom_call_target="tpu_custom_call" | custom-call | flops 1100000000 | bytes 1048576 | tf_op jit(solution)/shard_map/finish/pallas_call | solution.py:605
  (15 shorter events, 0.2 us)
Async XLA Ops:
  0.6 4.0 %copy-start.1 = (bf16[512,1024]{1,0:T(8,128)(2,1)S(1)}, bf16[512,1024]{1,0:T(8,128)(2,1)}, u32[]{:S(2)}) copy-start(bf16[512,1024]{1,0:T(8,128)(2,1)} %we_ref.3) | copy-start | bytes 3145732
  0.6 4.0 %copy-start.2 = (bf16[1,4,1024,128]{3,2,1,0:T(8,128)(2,1)S(1)}, bf16[1,4,1024,128]{3,2,1,0:T(8,128)(2,1)}, u32[]{:S(2)}) copy-start(bf16[1,4,1024,128]{3,2,1,0:T(8,128)(2,1)} %param.14) | copy-start | bytes 3145732
  0.7 4.0 %copy-start.3 = (bf16[512,1024]{1,0:T(8,128)(2,1)S(1)}, bf16[512,1024]{1,0:T(8,128)(2,1)}, u32[]{:S(2)}) copy-start(bf16[512,1024]{1,0:T(8,128)(2,1)} %wr_ref.5) | copy-start | bytes 3145732
  0.7 4.0 %copy-start.4 = (bf16[512,144]{0,1:T(8,128)(2,1)S(1)}, bf16[512,144]{0,1:T(8,128)(2,1)}, u32[]{:S(2)}) copy-start(bf16[512,144]{0,1:T(8,128)(2,1)} %param.17) | copy-start | bytes 442372
  0.7 4.0 %copy-start.5 = (f32[1024]{0:T(1024)S(1)}, f32[1024]{0:T(1024)}, u32[]{:S(2)}) copy-start(f32[1024]{0:T(1024)} %param.23) | copy-start | bytes 12292
  0.7 4.0 %copy-start.6 = (f32[1024]{0:T(1024)S(1)}, f32[1024]{0:T(1024)}, u32[]{:S(2)}) copy-start(f32[1024]{0:T(1024)} %param.24) | copy-start | bytes 12292
  0.7 4.0 %copy-start.7 = (f32[512]{0:T(512)S(1)}, f32[512]{0:T(512)}, u32[]{:S(2)}) copy-start(f32[512]{0:T(512)} %param.19) | copy-start | bytes 6148
  0.7 4.0 %copy-start.8 = (f32[512]{0:T(512)S(1)}, f32[512]{0:T(512)}, u32[]{:S(2)}) copy-start(f32[512]{0:T(512)} %param.20) | copy-start | bytes 6148
  0.7 4.0 %copy-start.9 = (f32[512]{0:T(512)S(1)}, f32[512]{0:T(512)}, u32[]{:S(2)}) copy-start(f32[512]{0:T(512)} %param.21) | copy-start | bytes 6148
  0.7 4.0 %copy-start.10 = (f32[512]{0:T(512)S(1)}, f32[512]{0:T(512)}, u32[]{:S(2)}) copy-start(f32[512]{0:T(512)} %param.22) | copy-start | bytes 6148
  3.4 4.2 %collective-permute-start = (bf16[48,1024]{1,0:T(8,128)(2,1)}, bf16[48,1024]{1,0:T(8,128)(2,1)S(1)}, u32[]{:S(2)}, u32[]{:S(2)}) collective-permute-start(bf16[48,1024]{1,0:T(8,128)(2,1)} %get-tuple-element.48), channel_id=1, source_target_pairs={{0,2},{2,0},{4,6},{6,4},{8,10},{10,8},{12,14},{14,12},{16,18},{18,... | collective-permute-start | bytes 294920 | tf_op jit(solution)/shard_map/ppermute | solution.py:466
  4.0 3.7 %collective-permute-start.1 = (bf16[48,1024]{1,0:T(8,128)(2,1)}, bf16[48,1024]{1,0:T(8,128)(2,1)S(1)}, u32[]{:S(2)}, u32[]{:S(2)}) collective-permute-start(bf16[48,1024]{1,0:T(8,128)(2,1)} %get-tuple-element.49), channel_id=1, source_target_pairs={{2,4},{6,8},{10,12},{14,16},{18,20},{22,24},{26,28},{4,2},{8,6},{1... | collective-permute-start | bytes 294920 | tf_op jit(solution)/shard_map/ppermute | solution.py:528
  4.7 3.0 %copy-start = (bf16[1,4,1024,128]{3,2,1,0:T(8,128)(2,1)S(1)}, bf16[1,4,1024,128]{3,2,1,0:T(8,128)(2,1)}, u32[]{:S(2)}) copy-start(bf16[1,4,1024,128]{3,2,1,0:T(8,128)(2,1)} %param.15) | copy-start | bytes 3145732
  4.7 3.0 %copy-start.12 = (s32[16]{0:T(128)S(1)}, s32[16]{0:T(128)}, u32[]{:S(2)}) copy-start(s32[16]{0:T(128)} %get-tuple-element.47.meta_ref) | copy-start | bytes 196
  13.7 5.9 %collective-permute-start.2 = (bf16[8,256,128]{2,1,0:T(8,128)(2,1)S(1)}, bf16[8,256,128]{2,1,0:T(8,128)(2,1)S(1)}, u32[]{:S(2)}, u32[]{:S(2)}) collective-permute-start(bf16[8,256,128]{2,1,0:T(8,128)(2,1)S(1)} %get-tuple-element.62), channel_id=1, source_target_pairs={{0,2},{2,0},{4,6},{6,4},{8,10},{10,8},{12,14},{14,12},{16,18},{18,... | collective-permute-start | bytes 1572872 | tf_op jit(solution)/shard_map/ppermute | solution.py:466
  17.7 4.6 %copy-start.11 = (bf16[2304,256]{1,0:T(8,128)(2,1)S(1)}, bf16[2304,256]{1,0:T(8,128)(2,1)}, u32[]{:S(2)}) copy-start(bf16[2304,256]{1,0:T(8,128)(2,1)} %constant.2.clone.place_ref) | copy-start | bytes 3538948
  19.8 9.3 %collective-permute-start.7 = (bf16[4,256,128]{2,1,0:T(8,128)(2,1)S(1)}, bf16[4,256,128]{2,1,0:T(8,128)(2,1)S(1)}, u32[]{:S(2)}, u32[]{:S(2)}) collective-permute-start(bf16[4,256,128]{2,1,0:T(8,128)(2,1)S(1)} %slice.37), channel_id=1, source_target_pairs={{0,4},{2,6},{4,0},{6,2},{8,12},{10,14},{12,8},{14,10},{16,20},{18,... | collective-permute-start | bytes 786440 | tf_op jit(solution)/shard_map/ppermute | solution.py:466
  28.0 1.4 %collective-permute-start.3 = (bf16[2,296,128]{2,1,0:T(8,128)(2,1)S(1)}, bf16[2,296,128]{2,1,0:T(8,128)(2,1)S(1)}, u32[]{:S(2)}, u32[]{:S(2)}) collective-permute-start(bf16[2,296,128]{2,1,0:T(8,128)(2,1)S(1)} %get-tuple-element.72), channel_id=1, source_target_pairs={{0,2},{2,0},{4,6},{6,4},{8,10},{10,8},{12,14},{14,12},{16,18},{18,... | collective-permute-start | bytes 454664 | tf_op jit(solution)/shard_map/ppermute | solution.py:466
  28.1 1.6 %collective-permute-start.4 = (bf16[2,296,128]{2,1,0:T(8,128)(2,1)S(1)}, bf16[2,296,128]{2,1,0:T(8,128)(2,1)S(1)}, u32[]{:S(2)}, u32[]{:S(2)}) collective-permute-start(bf16[2,296,128]{2,1,0:T(8,128)(2,1)S(1)} %get-tuple-element.73), channel_id=1, source_target_pairs={{0,2},{2,0},{4,6},{6,4},{8,10},{10,8},{12,14},{14,12},{16,18},{18,... | collective-permute-start | bytes 454664 | tf_op jit(solution)/shard_map/ppermute | solution.py:466
  28.6 1.4 %collective-permute-start.5 = (bf16[2,296,128]{2,1,0:T(8,128)(2,1)S(1)}, bf16[2,296,128]{2,1,0:T(8,128)(2,1)S(1)}, u32[]{:S(2)}, u32[]{:S(2)}) collective-permute-start(bf16[2,296,128]{2,1,0:T(8,128)(2,1)S(1)} %get-tuple-element.74), channel_id=1, source_target_pairs={{0,2},{2,0},{4,6},{6,4},{8,10},{10,8},{12,14},{14,12},{16,18},{18,... | collective-permute-start | bytes 454664 | tf_op jit(solution)/shard_map/ppermute | solution.py:466
  28.6 1.5 %collective-permute-start.6 = (bf16[2,296,128]{2,1,0:T(8,128)(2,1)S(1)}, bf16[2,296,128]{2,1,0:T(8,128)(2,1)S(1)}, u32[]{:S(2)}, u32[]{:S(2)}) collective-permute-start(bf16[2,296,128]{2,1,0:T(8,128)(2,1)S(1)} %get-tuple-element.75), channel_id=1, source_target_pairs={{0,2},{2,0},{4,6},{6,4},{8,10},{10,8},{12,14},{14,12},{16,18},{18,... | collective-permute-start | bytes 454664 | tf_op jit(solution)/shard_map/ppermute | solution.py:466
  30.2 9.6 %collective-permute-start.8 = (bf16[2,552,128]{2,1,0:T(8,128)(2,1)S(1)}, bf16[2,552,128]{2,1,0:T(8,128)(2,1)S(1)}, u32[]{:S(2)}, u32[]{:S(2)}) collective-permute-start(bf16[2,552,128]{2,1,0:T(8,128)(2,1)S(1)} %pad_maximum_fusion), channel_id=1, source_target_pairs={{0,8},{1,9},{2,10},{3,11},{4,12},{5,13},{6,14},{7,15},{8,0},{9,1},... | collective-permute-start | bytes 847880 | tf_op jit(solution)/shard_map/ppermute | solution.py:482
  31.9 10.7 %collective-permute-start.10 = (bf16[2,296,128]{2,1,0:T(8,128)(2,1)S(1)}, bf16[2,296,128]{2,1,0:T(8,128)(2,1)S(1)}, u32[]{:S(2)}, u32[]{:S(2)}) collective-permute-start(bf16[2,296,128]{2,1,0:T(8,128)(2,1)S(1)} %add_convert_fusion.4), channel_id=1, source_target_pairs={{0,4},{1,5},{2,6},{3,7},{4,0},{5,1},{6,2},{7,3},{8,12},{9,13},{10,... | collective-permute-start | bytes 454664 | tf_op jit(solution)/shard_map/ppermute | solution.py:482
  32.7 9.9 %collective-permute-start.11 = (bf16[2,296,128]{2,1,0:T(8,128)(2,1)S(1)}, bf16[2,296,128]{2,1,0:T(8,128)(2,1)S(1)}, u32[]{:S(2)}, u32[]{:S(2)}) collective-permute-start(bf16[2,296,128]{2,1,0:T(8,128)(2,1)S(1)} %add_convert_fusion.3), channel_id=1, source_target_pairs={{0,12},{1,13},{2,14},{3,15},{4,8},{5,9},{6,10},{7,11},{8,4},{9,5},... | collective-permute-start | bytes 454664 | tf_op jit(solution)/shard_map/ppermute | solution.py:482
  39.9 7.0 %collective-permute-start.9 = (bf16[1,256,128]{2,1,0:T(8,128)(2,1)S(1)}, bf16[1,256,128]{2,1,0:T(8,128)(2,1)S(1)}, u32[]{:S(2)}, u32[]{:S(2)}) collective-permute-start(bf16[1,256,128]{2,1,0:T(8,128)(2,1)S(1)} %slice.50), channel_id=1, source_target_pairs={{0,16},{2,18},{4,20},{6,22},{8,24},{10,26},{12,28},{14,30},{16,0},... | collective-permute-start | bytes 196616 | tf_op jit(solution)/shard_map/ppermute | solution.py:466
  42.7 10.0 %collective-permute-start.14 = (bf16[296,128]{1,0:T(8,128)(2,1)S(1)}, bf16[296,128]{1,0:T(8,128)(2,1)S(1)}, u32[]{:S(2)}, u32[]{:S(2)}) collective-permute-start(bf16[296,128]{1,0:T(8,128)(2,1)S(1)} %get-tuple-element.89), channel_id=1, source_target_pairs={{0,17},{1,16},{2,19},{3,18},{4,21},{5,20},{6,23},{7,22},{8,25},{9,... | collective-permute-start | bytes 227336 | tf_op jit(solution)/shard_map/ppermute | solution.py:482
  46.9 6.5 %collective-permute-start.13 = (bf16[296,128]{1,0:T(8,128)(2,1)S(1)}, bf16[296,128]{1,0:T(8,128)(2,1)S(1)}, u32[]{:S(2)}, u32[]{:S(2)}) collective-permute-start(bf16[296,128]{1,0:T(8,128)(2,1)S(1)} %get-tuple-element.89), channel_id=1, source_target_pairs={{0,16},{1,17},{2,18},{3,19},{4,20},{5,21},{6,22},{7,23},{8,24},{9,... | collective-permute-start | bytes 227336 | tf_op jit(solution)/shard_map/ppermute | solution.py:482
  47.0 5.6 %collective-permute-start.12 = (bf16[552,128]{1,0:T(8,128)(2,1)S(1)}, bf16[552,128]{1,0:T(8,128)(2,1)S(1)}, u32[]{:S(2)}, u32[]{:S(2)}) collective-permute-start(bf16[552,128]{1,0:T(8,128)(2,1)S(1)} %pad_maximum_fusion.1), channel_id=1, source_target_pairs={{0,1},{1,0},{2,3},{3,2},{4,5},{5,4},{6,7},{7,6},{8,9},{9,8},{10,11... | collective-permute-start | bytes 423944 | tf_op jit(solution)/shard_map/ppermute | solution.py:482
